TPU v7x, 512 devices: a whole 4x4x16 slice. The times are simulated.
512 devices in a mesh: img: 32 (over x, z_hi, core), py: 4 (over y), px: 4 (over z_lo).
Axes of the slice: x: 4, y: 4, z: 16 (z_hi: 4, z_lo: 4; z = z_hi * 4 + z_lo), core: 2. Of those that a mesh axis runs over, the one named last changes fastest.
Arguments:
- queries: bfloat16 [32, 64, 64, 1536], P('img', 'py', 'px')
- keys: bfloat16 [32, 64, 64, 1536], P('img', 'py', 'px')
- values: bfloat16 [32, 64, 64, 1536], P('img', 'py', 'px'), may hold values from -6 to 6
- pattern: int32 [32, 8, 8, 9], P('img', 'py', 'px'), may hold values from 0 to 1, as said below
- targets: int32 [32, 8, 8, 12, 3], P('img', 'py', 'px'), may hold values from 0 to 8, as said below
- router_q: float32 [12, 128, 64], replicated, may hold values from -1.5 to 1.5
- router_k: float32 [12, 128, 64], replicated, may hold values from -1.5 to 1.5
Outputs:
- attended: bfloat16 [32, 64, 64, 1536], P('img', 'py', 'px')
- grad_q: float32 [12, 128, 64], replicated
- grad_k: float32 [12, 128, 64], replicated
Inputs may be any that keep to these rules, and one draw needn't show every extreme that they name: `pattern`: the centre offset and the offsets one block away along one axis that lie in the image are 1; offsets outside the image are 0. `targets`: 3 different offsets per query block and head, each with pattern 1.
All inputs are finite; a program needn't handle non-finite values.
Results may differ from a plain program's by a relative error of at most 0.0049.
Values may be sent and summed in bfloat16 or wider, within the bound.
No kernel may reach another device: no remote copies, remote signals or barrier semaphores. Data moves between devices by JAX's collectives and lax.ppermute only.
A program may use at most 64 MiB of HBM per device.

v0:
```python
import math

import jax
import jax.numpy as jnp
from jax import lax
from jax.sharding import PartitionSpec as P

HEADS = 12
DH = 128
RW = 64
BS = 8
RADIUS = 1
TOPK = 3
NOFF = 9


def extended_2(cells, sides, width):
    for axis, dim in sides:
        count = lax.axis_size(axis)
        ends = count - 1
        head = lax.slice_in_dim(cells, 0, width, axis=dim)
        tail = lax.slice_in_dim(cells, cells.shape[dim] - width, cells.shape[dim], axis=dim)
        cells = jnp.concatenate(
            [
                lax.ppermute(tail, axis, [(i, (i + 1) % count) for i in range(ends)]),
                cells,
                lax.ppermute(head, axis, [((i + 1) % count, i) for i in range(ends)]),
            ],
            axis=dim,
        )
    return cells


def attend(query_tile, key_ext, value_ext, live):
    tile_y, tile_x, feat = query_tile.shape
    blocks_y = tile_y // BS
    blocks_x = tile_x // BS
    width = 2 * RADIUS + 1
    side = width * BS
    scale = 1.0 / math.sqrt(DH)
    anchor = jnp.zeros((), jnp.int32)

    def regroup(window):
        return (
            window.reshape(width, BS, width, BS, feat)
            .transpose(0, 2, 1, 3, 4)
            .reshape(NOFF * BS * BS, HEADS, DH)
        )

    def one_block(index):
        row = index // blocks_x
        col = index % blocks_x
        start_y = row * BS
        start_x = col * BS
        query = lax.dynamic_slice(query_tile, (start_y, start_x, anchor), (BS, BS, feat)).reshape(
            BS * BS, HEADS, DH
        )
        window_k = regroup(
            lax.dynamic_slice(key_ext, (start_y, start_x, anchor), (side, side, feat))
        )
        window_v = regroup(
            lax.dynamic_slice(value_ext, (start_y, start_x, anchor), (side, side, feat))
        )
        mask_row = lax.dynamic_slice(live, (row, col, anchor), (1, 1, NOFF)).reshape(NOFF)
        key_mask = jnp.repeat(mask_row, BS * BS) > 0
        scores = (
            jnp.einsum("qhd,khd->hqk", query, window_k, preferred_element_type=jnp.float32) * scale
        )
        scores = jnp.where(key_mask[None, None, :], scores, -1e30)
        top = jnp.max(scores, axis=-1, keepdims=True)
        weights = jnp.exp(scores - top)
        probs = (weights / jnp.sum(weights, axis=-1, keepdims=True)).astype(jnp.bfloat16)
        out = jnp.einsum("hqk,khd->qhd", probs, window_v, preferred_element_type=jnp.float32)
        return out.astype(jnp.bfloat16).reshape(BS, BS, feat)

    outs = lax.map(one_block, jnp.arange(blocks_y * blocks_x, dtype=jnp.int32))
    return (
        outs.reshape(blocks_y, blocks_x, BS, BS, feat)
        .transpose(0, 2, 1, 3, 4)
        .reshape(tile_y, tile_x, feat)
    )


def pooling(tile):
    tile_y, tile_x, feat = tile.shape
    shaped = tile.reshape(tile_y // BS, BS, tile_x // BS, BS, HEADS, DH)
    return jnp.sum(shaped, axis=(1, 3), dtype=jnp.float32) / (BS * BS)


def router_loss(weights_q, weights_k, pooled_q, pooled_k, live, chosen):
    route_q = jnp.einsum("yxhd,hdr->yxhr", pooled_q, weights_q, precision=lax.Precision.HIGHEST)
    route_k = jnp.einsum("yxhd,hdr->yxhr", pooled_k, weights_k, precision=lax.Precision.HIGHEST)
    blocks_y, blocks_x = (pooled_q.shape[0], pooled_q.shape[1])
    width = 2 * RADIUS + 1
    shifted = jnp.stack(
        [
            route_k[up : up + blocks_y, left : left + blocks_x]
            for up in range(width)
            for left in range(width)
        ],
        axis=2,
    )
    logits = jnp.einsum(
        "yxhr,yxohr->yxho", route_q, shifted, precision=lax.Precision.HIGHEST
    ) / math.sqrt(RW)
    logits = jnp.where(live[:, :, None, :] > 0, logits, -1e30)
    top = jnp.max(logits, axis=-1, keepdims=True)
    logz = top + jnp.log(jnp.sum(jnp.exp(logits - top), axis=-1, keepdims=True))
    logp = logits - logz
    picks = (chosen[..., None] == jnp.arange(NOFF, dtype=jnp.int32)).astype(jnp.float32)
    return -jnp.sum(picks * logp[:, :, :, None, :])


def per_device(queries, keys, values, pattern, targets, router_q, router_k):
    rim = RADIUS * BS
    stacked = jnp.stack([keys, values])
    extended = extended_2(stacked, (("py", 2), ("px", 3)), rim)
    key_ext = extended[0, 0]
    value_ext = extended[1, 0]
    attended = attend(queries[0], key_ext, value_ext, pattern[0])[None]
    pooled_q = pooling(queries[0])
    pooled_k = pooling(key_ext)
    blocks_y = pooled_q.shape[0]
    blocks_x = pooled_q.shape[1]
    normal = float(TOPK * HEADS * blocks_y * lax.axis_size("py") * blocks_x * lax.axis_size("px"))

    def local_loss(weights_q, weights_k):
        return (
            router_loss(weights_q, weights_k, pooled_q, pooled_k, pattern[0], targets[0]) / normal
        )

    grad_q, grad_k = jax.grad(local_loss, argnums=(0, 1))(router_q, router_k)
    grad_q, grad_k = lax.psum((grad_q, grad_k), ("img", "py", "px"))
    return (attended, grad_q, grad_k)


def solution(mesh):
    return jax.shard_map(
        per_device,
        mesh=mesh,
        in_specs=(
            P("img", "py", "px", None),
            P("img", "py", "px", None),
            P("img", "py", "px", None),
            P("img", "py", "px", None),
            P("img", "py", "px", None, None),
            P(),
            P(),
        ),
        out_specs=(P("img", "py", "px", None), P(), P()),
        check_vma=False,
    )
```

profile of v0, /device:TPU:2, one launch (start us, length us, event | category | flops | bytes accessed | tf_op | source)
XLA Modules:
  0.0 595.2 jit_solution(9057163803612186937)
XLA Ops:
  7.2 1.6 fusion.31
  8.9 3.5 collective-permute-start
  13.7 15.4 %collective-permute-done = bf16[2,1,8,16,1536]{4,3,2,1,0:T(8,128)(2,1)S(1)} collective-permute-done((bf16[2,1,8,16,1536]{4,3,2,1,0:T(8,128)(2,1)S(1)}, bf16[2,1,8,16,1536]{4,3,2,1,0:T(8,128)(2,1)S(1)}, u32[]{:S(2)}, u32[]{:S(2)}) %collective-permute-start) | collective-permute-done | bytes 786464 | tf_op jit(solution)/shard_map/ppermute | solution.py:25
  29.1 4.2 collective-permute-done.1
  34.6 1.9 fusion.85
  36.5 5.0 collective-permute-start.2
  44.5 1.7 fusion.37
  46.2 26.9 %collective-permute-done.2 = bf16[2,1,32,8,1536]{4,3,2,1,0:T(8,128)(2,1)} collective-permute-done((bf16[2,1,32,8,1536]{4,3,2,1,0:T(8,128)(2,1)}, bf16[2,1,32,8,1536]{4,3,2,1,0:T(8,128)(2,1)}, u32[]{:S(2)}, u32[]{:S(2)}) %collective-permute-start.2) | collective-permute-done | bytes 1572896 | tf_op jit(solution)/shard_map/ppermute | solution.py:25
  73.2 5.3 collective-permute-done.3
  78.5 3.2 pad_maximum_fusion
  81.6 2.4 fusion.84
  93.8 1.6 copy.53
  98.7 1.5 fusion.32
  100.1 2.3 convolution_bitcast_fusion
  102.5 2.6 convolution_bitcast_fusion.1
  105.1 122.5 %while.12 = (s32[]{:T(128)}, bf16[4,8,8,1536]{3,2,1,0:T(8,128)(2,1)}, s32[4]{0:T(128)S(1)}, bf16[32,32,1536]{2,1,0:T(8,128)(2,1)}, s32[2,2,9]{2,1,0:T(2,128)S(1)...) while((s32[]{:T(128)}, ...), condition=%wide.region_3.4_spmd, body=%wide.region_0.3_spmd.sunk | while | flops 343820224 | bytes 57812960 | solution.py:76
  108.5 3.0 constant_dynamic-slice_fusion.6
  111.5 1.5 copy.118
  113.0 3.0 reshape.102
  117.1 2.2 fusion.101
  119.5 2.0 fusion.100
  121.6 1.6 copy.117
  123.2 2.7 reshape.101
  125.9 4.7 fusion.102
  130.6 1.8 copy.119
  132.3 1.8 broadcast_in_dim.131
  134.1 1.6 constant_dynamic-update-slice_fusion.2
  139.1 3.1 constant_dynamic-slice_fusion.6
  142.1 1.5 copy.118
  143.6 3.0 reshape.102
  147.7 2.2 fusion.101
  150.2 2.0 fusion.100
  152.2 1.6 copy.117
  153.8 2.7 reshape.101
  156.5 4.7 fusion.102
  161.2 1.8 copy.119
  163.0 1.8 broadcast_in_dim.131
  164.7 1.6 constant_dynamic-update-slice_fusion.2
  169.7 3.0 constant_dynamic-slice_fusion.6
  172.7 1.5 copy.118
  174.2 3.0 reshape.102
  178.4 2.2 fusion.101
  180.8 2.0 fusion.100
  182.8 1.6 copy.117
  184.4 2.7 reshape.101
  187.1 4.7 fusion.102
  191.8 1.8 copy.119
  193.6 1.8 broadcast_in_dim.131
  195.3 1.6 constant_dynamic-update-slice_fusion.2
  200.3 3.1 constant_dynamic-slice_fusion.6
  203.4 1.5 copy.118
  204.9 3.0 reshape.102
  209.0 2.2 fusion.101
  211.4 2.0 fusion.100
  213.4 1.6 copy.117
  215.1 2.7 reshape.101
  217.8 4.7 fusion.102
  222.5 1.8 copy.119
  224.2 1.8 broadcast_in_dim.131
  226.0 1.6 constant_dynamic-update-slice_fusion.2
  227.6 2.1 copy.48
  229.7 355.1 %all-reduce.12.cloned.1.call-done = (f32[12,128,64]{1,2,0:T(8,128)}, f32[12,128,64]{1,2,0:T(8,128)}) async-done(((f32[12,128,64]{1,2,0:T(8,128)}, f32[12,128,64]{1,2,0:T(8,128)}), (f32[12,128,64]{1,2,0:T(8,128)}, f32[12,128,64]{1,2,0:T(8,128)})) %all-reduce.12.cloned.1.call-update) | async-done | bytes 786448 | tf_op jit(solution)/shard_map/psum | solution.py:133
  584.8 1.8 copy.137
  586.6 1.8 copy.138
  (95 shorter events, 26.4 us)
Async XLA Ops:
  7.2 78.1 %copy-start = (f32[12,128,64]{1,2,0:T(8,128)S(1)}, f32[12,128,64]{1,2,0:T(8,128)}, u32[]{:S(2)}) copy-start(f32[12,128,64]{1,2,0:T(8,128)} %param.15) | copy-start | bytes 1179652
  7.2 27.0 %copy-start.3 = (bf16[1,16,16,1536]{3,2,1,0:T(8,128)(2,1)S(1)}, bf16[1,16,16,1536]{3,2,1,0:T(8,128)(2,1)}, u32[]{:S(2)}) copy-start(bf16[1,16,16,1536]{3,2,1,0:T(8,128)(2,1)} %param.10) | copy-start | bytes 2359300
  7.2 27.0 %copy-start.4 = (bf16[1,16,16,1536]{3,2,1,0:T(8,128)(2,1)S(1)}, bf16[1,16,16,1536]{3,2,1,0:T(8,128)(2,1)}, u32[]{:S(2)}) copy-start(bf16[1,16,16,1536]{3,2,1,0:T(8,128)(2,1)} %param.11) | copy-start | bytes 2359300
  7.2 577.6 %all-reduce.12.cloned.1.call-start = ((), (), s32[]{:S(2)}) async-start(), calls=%async_computation | async-start | bytes 1572864 | tf_op jit(solution)/shard_map/psum | solution.py:133
  8.9 20.3 %collective-permute-start = (bf16[2,1,8,16,1536]{4,3,2,1,0:T(8,128)(2,1)S(1)}, bf16[2,1,8,16,1536]{4,3,2,1,0:T(8,128)(2,1)S(1)}, u32[]{:S(2)}, u32[]{:S(2)}) collective-permute-start(bf16[2,1,8,16,1536]{4,3,2,1,0:T(8,128)(2,1)S(1)} %get-tuple-element.123), channel_id=1, source_target_pairs={{0,4},{4,8},{8,12},{1,5},{5,9},{9,13},{2,6},{6,10},{10,14},{3,7},{... | collective-permute-start | bytes 2359304 | tf_op jit(solution)/shard_map/ppermute | solution.py:25
  12.4 20.9 %collective-permute-start.1 = (bf16[2,1,8,16,1536]{4,3,2,1,0:T(8,128)(2,1)S(1)}, bf16[2,1,8,16,1536]{4,3,2,1,0:T(8,128)(2,1)S(1)}, u32[]{:S(2)}, u32[]{:S(2)}) collective-permute-start(bf16[2,1,8,16,1536]{4,3,2,1,0:T(8,128)(2,1)S(1)} %get-tuple-element.124), channel_id=1, source_target_pairs={{4,0},{8,4},{12,8},{5,1},{9,5},{13,9},{6,2},{10,6},{14,10},{7,3},{... | collective-permute-start | bytes 2359304 | tf_op jit(solution)/shard_map/ppermute | solution.py:27
  33.3 0.9 copy-start.6
  34.6 8.2 %copy-start.11 = (s32[1,2,2,9]{3,2,1,0:T(2,128)S(1)}, s32[1,2,2,9]{3,2,1,0:T(2,128)}, u32[]{:S(2)}) copy-start(s32[1,2,2,9]{3,2,1,0:T(2,128)} %param.12) | copy-start | bytes 436
  34.6 9.7 %copy-start.5 = (bf16[1,16,16,1536]{3,2,1,0:T(8,128)(2,1)S(1)}, bf16[1,16,16,1536]{3,2,1,0:T(8,128)(2,1)}, u32[]{:S(2)}) copy-start(bf16[1,16,16,1536]{3,2,1,0:T(8,128)(2,1)} %param.9) | copy-start | bytes 2359300
  36.5 36.6 %collective-permute-start.2 = (bf16[2,1,32,8,1536]{4,3,2,1,0:T(8,128)(2,1)}, bf16[2,1,32,8,1536]{4,3,2,1,0:T(8,128)(2,1)}, u32[]{:S(2)}, u32[]{:S(2)}) collective-permute-start(bf16[2,1,32,8,1536]{4,3,2,1,0:T(8,128)(2,1)} %get-tuple-element.121), channel_id=1, source_target_pairs={{0,1},{1,2},{2,3},{4,5},{5,6},{6,7},{8,9},{9,10},{10,11},{12,13},{... | collective-permute-start | bytes 4718600 | tf_op jit(solution)/shard_map/ppermute | solution.py:25
  41.5 36.9 %collective-permute-start.3 = (bf16[2,1,32,8,1536]{4,3,2,1,0:T(8,128)(2,1)}, bf16[2,1,32,8,1536]{4,3,2,1,0:T(8,128)(2,1)}, u32[]{:S(2)}, u32[]{:S(2)}) collective-permute-start(bf16[2,1,32,8,1536]{4,3,2,1,0:T(8,128)(2,1)} %get-tuple-element.122), channel_id=1, source_target_pairs={{1,0},{2,1},{3,2},{5,4},{6,5},{7,6},{9,8},{10,9},{11,10},{13,12},{... | collective-permute-start | bytes 4718600 | tf_op jit(solution)/shard_map/ppermute | solution.py:27
  44.5 34.0 %copy-start.10 = (f32[2,2,12,128]{3,2,1,0:T(8,128)}, f32[2,2,12,128]{3,2,1,0:T(8,128)S(1)}, u32[]{:S(2)}) copy-start(f32[2,2,12,128]{3,2,1,0:T(8,128)S(1)} %broadcast_multiply_fusion.1) | copy-start | bytes 73732
  46.2 40.1 %copy-start.9 = (f32[12,2,2,64]{3,2,1,0:T(2,128)}, f32[12,2,2,64]{3,2,1,0:T(2,128)S(1)}, u32[]{:S(2)}) copy-start(f32[12,2,2,64]{3,2,1,0:T(2,128)S(1)} %fusion.37) | copy-start | bytes 36868
  84.6 0.7 copy-start.8
  86.3 0.7 copy-start.7
  105.1 6.4 %copy-start.1 = (bf16[32,32,1536]{2,1,0:T(8,128)(2,1)}, bf16[32,32,1536]{2,1,0:T(8,128)(2,1)S(1)}, u32[]{:S(2)}) copy-start(bf16[32,32,1536]{2,1,0:T(8,128)(2,1)S(1)} %get-tuple-element.215) | copy-start | bytes 9437188 | tf_op jit(solution)/shard_map/while
  125.9 9.8 %copy-start.2 = (bf16[32,32,1536]{2,1,0:T(8,128)(2,1)S(1)}, bf16[32,32,1536]{2,1,0:T(8,128)(2,1)}, u32[]{:S(2)}) copy-start(bf16[32,32,1536]{2,1,0:T(8,128)(2,1)} %copy-done.1) | copy-start | bytes 9437188 | tf_op jit(solution)/shard_map/while
  135.7 6.4 %copy-start.1 = (bf16[32,32,1536]{2,1,0:T(8,128)(2,1)}, bf16[32,32,1536]{2,1,0:T(8,128)(2,1)S(1)}, u32[]{:S(2)}) copy-start(bf16[32,32,1536]{2,1,0:T(8,128)(2,1)S(1)} %get-tuple-element.215) | copy-start | bytes 9437188 | tf_op jit(solution)/shard_map/while
  156.5 9.9 %copy-start.2 = (bf16[32,32,1536]{2,1,0:T(8,128)(2,1)S(1)}, bf16[32,32,1536]{2,1,0:T(8,128)(2,1)}, u32[]{:S(2)}) copy-start(bf16[32,32,1536]{2,1,0:T(8,128)(2,1)} %copy-done.1) | copy-start | bytes 9437188 | tf_op jit(solution)/shard_map/while
  166.4 6.4 %copy-start.1 = (bf16[32,32,1536]{2,1,0:T(8,128)(2,1)}, bf16[32,32,1536]{2,1,0:T(8,128)(2,1)S(1)}, u32[]{:S(2)}) copy-start(bf16[32,32,1536]{2,1,0:T(8,128)(2,1)S(1)} %get-tuple-element.215) | copy-start | bytes 9437188 | tf_op jit(solution)/shard_map/while
  187.1 9.9 %copy-start.2 = (bf16[32,32,1536]{2,1,0:T(8,128)(2,1)S(1)}, bf16[32,32,1536]{2,1,0:T(8,128)(2,1)}, u32[]{:S(2)}) copy-start(bf16[32,32,1536]{2,1,0:T(8,128)(2,1)} %copy-done.1) | copy-start | bytes 9437188 | tf_op jit(solution)/shard_map/while
  197.0 6.4 %copy-start.1 = (bf16[32,32,1536]{2,1,0:T(8,128)(2,1)}, bf16[32,32,1536]{2,1,0:T(8,128)(2,1)S(1)}, u32[]{:S(2)}) copy-start(bf16[32,32,1536]{2,1,0:T(8,128)(2,1)S(1)} %get-tuple-element.215) | copy-start | bytes 9437188 | tf_op jit(solution)/shard_map/while
  217.8 9.8 %copy-start.2 = (bf16[32,32,1536]{2,1,0:T(8,128)(2,1)S(1)}, bf16[32,32,1536]{2,1,0:T(8,128)(2,1)}, u32[]{:S(2)}) copy-start(bf16[32,32,1536]{2,1,0:T(8,128)(2,1)} %copy-done.1) | copy-start | bytes 9437188 | tf_op jit(solution)/shard_map/while
Sparse Core Ops, SparseCore 0:
  105.2 479.5 all-reduce.11
where the time goes:
time: 597 us; the launch traced here: 595 us
  waiting for transfers between devices  407 us (68%)
  local copies, waits for them, and re-layouts  93.3 us (16%)
  matrix products  46.1 us (8%)
  between operations  14.3 us (2%)
  other arithmetic  12.5 us (2%)
  starting transfers between devices  11.1 us (2%)
  loops' own time  10.9 us (2%)
    psum x1, waiting for transfers between devices, per_device(): grad_q, grad_k = lax.psum((grad_q, grad_k), ('img', 'py', 'px'))  355 us
    ppermute x2, waiting for transfers between devices, extended_2(): lax.ppermute(tail, axis, [(i, (i + 1) % count) for i in range(ends)])  42.4 us
    reshape x8, local copies, waits for them, and re-layouts, regroup(): return window.reshape(width, BS, width, BS, feat).transpose(0, 2, 1, 3, 4...  22.8 us
    dot_general x4, matrix products, one_block(): jnp.einsum('hqk,khd->qhd', probs, window_v, preferred_element_type=jnp.fl...  18.8 us
    transpose x8, local copies, waits for them, and re-layouts, regroup(): return window.reshape(width, BS, width, BS, feat).transpose(0, 2, 1, 3, 4...  12.4 us
    dynamic_slice x4, local copies, waits for them, and re-layouts, one_block(): lax.dynamic_slice(key_ext, (start_y, start_x, anchor), (side, side, feat))  12.2 us
  transfers between devices with their start and end apart: 5, of which 5 were waited for; matrix products, arithmetic and copies ran while one was open for 20% of the time, Pallas kernels for 0%

commit v1 on v0

v1 whole, which is shorter than its diff:
```python
import functools
import math

import jax
import jax.numpy as jnp
import numpy as np
from jax import lax
from jax.experimental import pallas as pl
from jax.experimental.pallas import tpu as pltpu
from jax.sharding import PartitionSpec as P

HEADS = 12
DH = 128
RW = 64
BS = 8
TOPK = 3
NOFF = 9
TILE = 16
TOK = TILE * TILE
FEAT = HEADS * DH
EDGE = BS * TILE
NKEY = TOK + 6 * EDGE
SLOTS = 16
HSTEP = 2
LIVE_CAP = 3.4e38
DEAD_CAP = -1e30
TILES = ("py", "px")


def key_block_ids():
    ids = np.zeros((8, NKEY), np.int32)
    own = np.arange(TOK)
    row = [(1 + own // TILE // BS) * 4 + 1 + own % TILE // BS]
    edge = np.arange(EDGE)
    row.append(1 + edge % TILE // BS)
    row.append(12 + 1 + edge % TILE // BS)
    row.append((1 + edge // BS // BS) * 4)
    row.append((1 + edge // BS // BS) * 4 + 3)
    row.append(edge // (BS * BS) * 12)
    row.append(edge // (BS * BS) * 12 + 3)
    ids[:] = np.concatenate(row)[None]
    return ids


def pool_kernel(q_ref, k_ref, aux_ref, out_ref):
    row = lax.broadcasted_iota(jnp.int32, (8, TOK), 0)
    tok = lax.broadcasted_iota(jnp.int32, (8, TOK), 1)
    block = tok // TILE // BS * 2 + tok % TILE // BS
    pick_q = (row == block).astype(jnp.float32).astype(jnp.bfloat16)
    pick_k = (row == block + 4).astype(jnp.float32).astype(jnp.bfloat16)
    sums = jnp.dot(pick_q, q_ref[...], preferred_element_type=jnp.float32)
    sums += jnp.dot(pick_k, k_ref[...], preferred_element_type=jnp.float32)
    means = sums / (BS * BS)
    for h in range(HEADS):
        out_ref[h, 0:8, :] = means[:, h * DH : (h + 1) * DH]
        out_ref[h, 8:16, :] = aux_ref[h]
    for h in range(HEADS, SLOTS):
        out_ref[h] = jnp.zeros((16, DH), jnp.float32)


def pool(query, key, aux):
    return pl.pallas_call(
        pool_kernel,
        out_shape=jax.ShapeDtypeStruct((SLOTS, 16, DH), jnp.float32),
        name="pool",
    )(query, key, aux)


def router_kernel(normal, head_ref, recv_ref, wq_ref, wk_ref, out_ref, pq_ref, pk_ref, ax_ref):
    for i in range(SLOTS):
        pq_ref[4 * i : 4 * i + 4, :] = recv_ref[i, 0:4, :]
        pk_ref[4 * i : 4 * i + 4, :] = recv_ref[i, 4:8, :]
        ax_ref[4 * i : 4 * i + 4, :] = recv_ref[i, 8:12, :]
    n = 4 * SLOTS
    dot = functools.partial(
        lax.dot_general, precision=lax.Precision.HIGHEST, preferred_element_type=jnp.float32
    )
    ab, abt, atb = (((1,), (0,)), ((), ())), (((1,), (1,)), ((), ())), (((0,), (0,)), ((), ()))
    pooled_q, pooled_k, aux = pq_ref[...], pk_ref[...], ax_ref[...]
    route_q = dot(pooled_q, wq_ref[0], ab)
    route_k = dot(pooled_k, wk_ref[0], ab)
    logits = dot(route_q, route_k, abt) / math.sqrt(RW)

    def place(i):
        tile, sub = i // 4, i % 4
        return tile // 4 * 2 + sub // 2, tile % 4 * 2 + sub % 2

    qy, qx = place(lax.broadcasted_iota(jnp.int32, (n, n), 0))
    ky, kx = place(lax.broadcasted_iota(jnp.int32, (n, n), 1))
    up, left = ky - qy + 1, kx - qx + 1
    near = (up >= 0) & (up <= 2) & (left >= 0) & (left <= 2)
    off = jnp.where(near, 3 * up + left, -1).astype(jnp.float32)
    live = jnp.zeros((n, n), jnp.float32)
    for o in range(NOFF):
        live = jnp.where(off == float(o), aux[:, o : o + 1], live)
    picks = jnp.zeros((n, n), jnp.float32)
    for k in range(TOPK):
        picks += (off == aux[:, NOFF + k : NOFF + k + 1]).astype(jnp.float32)
    logits = jnp.where(live > 0.5, logits, -1e30)
    top = jnp.max(logits, axis=1, keepdims=True)
    weights = jnp.exp(logits - top)
    soft = weights / jnp.sum(weights, axis=1, keepdims=True)
    count = jnp.sum(picks, axis=1, keepdims=True)
    slope = jnp.where(live > 0.5, count * soft - picks, 0.0) * (1.0 / (normal * math.sqrt(RW)))
    grad_q = dot(pooled_q, dot(slope, route_k, ab), atb)
    grad_k = dot(pooled_k, dot(slope, route_q, atb), atb)
    out_ref[...] = jnp.concatenate([grad_q, grad_k], axis=1)


def router_grads(head, recv, weights_q, weights_k, normal):
    spec = pl.BlockSpec((1, DH, RW), lambda i, h: (h[0], 0, 0))
    return pl.pallas_call(
        functools.partial(router_kernel, normal),
        out_shape=jax.ShapeDtypeStruct((DH, 2 * RW), jnp.float32),
        grid_spec=pltpu.PrefetchScalarGridSpec(
            num_scalar_prefetch=1,
            grid=(1,),
            in_specs=[
                pl.BlockSpec((SLOTS, 16, DH), lambda i, h: (0, 0, 0)),
                spec,
                spec,
            ],
            out_specs=pl.BlockSpec((DH, 2 * RW), lambda i, h: (0, 0)),
            scratch_shapes=[pltpu.VMEM((4 * SLOTS, DH), jnp.float32)] * 3,
        ),
        name="router",
    )(head, recv, weights_q, weights_k)


def attend_kernel(pat_ref, ids_ref, q_ref, k_ref, v_ref, *rest):
    sides, out_ref, cap_ref = rest[:6], rest[6], rest[7]

    @pl.when(pl.program_id(0) == 0)
    def _():
        ids = ids_ref[...]
        tok = lax.broadcasted_iota(jnp.int32, (TOK, NKEY), 0)
        block = tok // TILE // BS * 2 + tok % TILE // BS
        cap = jnp.full((TOK, NKEY), DEAD_CAP, jnp.float32)
        for b in range(4):
            line = jnp.full((8, NKEY), DEAD_CAP, jnp.float32)
            for o in range(NOFF):
                at = (b // 2 + o // 3) * 4 + b % 2 + o % 3
                value = jnp.where(pat_ref[b, o] > 0, LIVE_CAP, DEAD_CAP)
                line = jnp.where(ids == at, value, line)
            cap = jnp.where(block == b, line[0:1, :], cap)
        cap_ref[...] = cap

    for h in range(HSTEP):
        lanes = slice(h * DH, (h + 1) * DH)
        query = q_ref[:, lanes]
        keys = jnp.concatenate([k_ref[:, lanes]] + [s[0, :, lanes] for s in sides], axis=0)
        values = jnp.concatenate([v_ref[:, lanes]] + [s[1, :, lanes] for s in sides], axis=0)
        scores = lax.dot_general(
            query, keys, (((1,), (1,)), ((), ())), preferred_element_type=jnp.float32
        )
        scores = jnp.minimum(scores, cap_ref[...])
        top = jnp.max(scores, axis=1, keepdims=True)
        weights = jnp.exp2((scores - top) * (math.log2(math.e) / math.sqrt(DH)))
        total = jnp.sum(weights, axis=1, keepdims=True)
        probs = (weights * (1.0 / total)).astype(jnp.bfloat16)
        out = jnp.dot(probs, values, preferred_element_type=jnp.float32)
        out_ref[:, lanes] = out.astype(jnp.bfloat16)


def attend(pattern, query, key, value, sides):
    wide = HSTEP * DH
    own = pl.BlockSpec((TOK, wide), lambda h: (0, h))
    side = pl.BlockSpec((2, EDGE, wide), lambda h: (0, 0, h))
    return pl.pallas_call(
        attend_kernel,
        out_shape=jax.ShapeDtypeStruct((TOK, FEAT), jnp.bfloat16),
        grid=(HEADS // HSTEP,),
        in_specs=[
            pl.BlockSpec(memory_space=pltpu.SMEM),
            pl.BlockSpec((8, NKEY), lambda h: (0, 0)),
            own,
            own,
            own,
        ]
        + [side] * 6,
        out_specs=own,
        scratch_shapes=[pltpu.VMEM((TOK, NKEY), jnp.float32)],
        cost_estimate=pl.CostEstimate(
            flops=4 * HEADS * TOK * NKEY * DH,
            bytes_accessed=2 * FEAT * (2 * TOK + 2 * NKEY),
            transcendentals=HEADS * TOK * NKEY,
        ),
        name="attend",
    )(pattern, jnp.asarray(key_block_ids()), query, key, value, *sides)


def shift(x, axis, step):
    count = lax.axis_size(axis)
    if step > 0:
        pairs = [(i, i + 1) for i in range(count - 1)]
    else:
        pairs = [(i + 1, i) for i in range(count - 1)]
    return lax.ppermute(x, axis, pairs)


def halos(key, value):
    both = (key, value)

    def flat(cut):
        return jnp.stack([cut(x).reshape(EDGE, FEAT) for x in both])

    above = shift(flat(lambda x: x[TILE - BS :]), "py", 1)
    below = shift(flat(lambda x: x[:BS]), "py", -1)
    left = shift(flat(lambda x: x[:, TILE - BS :]), "px", 1)
    right = shift(flat(lambda x: x[:, :BS]), "px", -1)

    def corners(lo):
        cuts = [
            x.reshape(2, BS, TILE, FEAT)[:, :, lo : lo + BS].reshape(2, BS * BS, FEAT)
            for x in (above, below)
        ]
        return jnp.concatenate(cuts, axis=1)

    corner_l = shift(corners(TILE - BS), "px", 1)
    corner_r = shift(corners(0), "px", -1)
    return above, below, left, right, corner_l, corner_r


def everyone(x, axis, count):
    return lax.all_to_all(jnp.broadcast_to(x[None], (count,) + x.shape), axis, 0, 0)


def per_device(queries, keys, values, pattern, targets, router_q, router_k):
    images = lax.axis_size("img")
    tiles_y, tiles_x = lax.axis_size("py"), lax.axis_size("px")
    tiles = tiles_y * tiles_x
    normal = float(TOPK * HEADS * 4 * tiles)
    query, key, value = (x[0].reshape(TOK, FEAT) for x in (queries, keys, values))
    pat = pattern.reshape(4, NOFF)
    aim = targets.reshape(4, HEADS, TOPK).transpose(1, 0, 2)
    aux = jnp.concatenate([jnp.broadcast_to(pat, (HEADS, 4, NOFF)), aim], axis=2)
    aux = jnp.pad(aux.astype(jnp.float32), ((0, 0), (0, 4), (0, DH - NOFF - TOPK)))

    sent = pool(query, key, aux)
    recv = lax.all_to_all(sent, TILES, 0, 0)
    sides = halos(keys[0], values[0])
    me = lax.axis_index("py") * tiles_x + lax.axis_index("px")
    head = jnp.minimum(me, HEADS - 1).astype(jnp.int32).reshape(1)
    grads = router_grads(head, recv, router_q, router_k, normal)
    parts = lax.all_to_all(grads.reshape(images, DH // images, 2 * RW), "img", 0, 0)
    part = jnp.sum(parts, axis=0).astype(jnp.bfloat16)
    mine = everyone(part, "img", images).reshape(DH, 2 * RW)
    every = everyone(mine, TILES, tiles)[:HEADS].astype(jnp.float32)
    attended = attend(pat, query, key, value, sides)
    return (attended.reshape(1, TILE, TILE, FEAT), every[:, :, :RW], every[:, :, RW:])


def solution(mesh):
    return jax.shard_map(
        per_device,
        mesh=mesh,
        in_specs=(
            P("img", "py", "px", None),
            P("img", "py", "px", None),
            P("img", "py", "px", None),
            P("img", "py", "px", None),
            P("img", "py", "px", None, None),
            P(),
            P(),
        ),
        out_specs=(P("img", "py", "px", None), P(), P()),
        check_vma=False,
    )
```

time: 597 us -> 134 us (0.22)
  the two profiles are of different devices: /device:TPU:2 before, /device:TPU:32 now
where the time goes in v1:
time: 134 us
  starting transfers between devices  53.1 us (40%)
  waiting for transfers between devices  46.9 us (35%)
  Pallas kernels  16 us (12%)
  local copies, waits for them, and re-layouts  12.7 us (9%)
  other arithmetic  4.13 us (3%)
    ppermute x6, waiting for transfers between devices, shift(): return lax.ppermute(x, axis, pairs)  22.6 us
    ppermute x6, starting transfers between devices, shift(): return lax.ppermute(x, axis, pairs)  17.4 us
    all_to_all x1, starting transfers between devices, per_device(): lax.all_to_all(grads.reshape(images, DH // images, 2 * RW), 'img', 0, 0)  17 us
    pallas_call x1, Pallas kernels, attend(): pl.pallas_call(attend_kernel, out_shape=jax.ShapeDtypeStruct((TOK, FEAT),...  10.9 us
    all_to_all x1, waiting for transfers between devices, per_device(): lax.all_to_all(grads.reshape(images, DH // images, 2 * RW), 'img', 0, 0)  10.6 us
    all_to_all x2, starting transfers between devices, everyone(): lax.all_to_all(jnp.broadcast_to(x[None], (count,) + x.shape), axis, 0, 0)  10.4 us
    all_to_all x2, waiting for transfers between devices, everyone(): lax.all_to_all(jnp.broadcast_to(x[None], (count,) + x.shape), axis, 0, 0)  9.91 us
    all_to_all x1, starting transfers between devices, per_device(): recv = lax.all_to_all(sent, TILES, 0, 0)  8.31 us
  transfers between devices with their start and end apart: 10, of which 5 were waited for; matrix products, arithmetic and copies ran while one was open for 7% of the time, Pallas kernels for 12%

profile of v1, /device:TPU:32, one launch (start us, length us, event | category | flops | bytes accessed | tf_op | source)
XLA Modules:
  0.0 133.7 jit_solution(13829295821608710662)
XLA Ops:
  0.6 0.0 copy-start.1
  0.6 1.2 fusion.1
  1.9 0.1 copy-done.1
  2.0 0.1 fusion.2
  2.1 0.0 copy-start.9
  2.1 0.0 copy-start.8
  2.1 0.9 pad_maximum_fusion
  3.0 3.5 %collective-permute-start = (bf16[2,128,1536]{2,1,0:T(8,128)(2,1)}, bf16[2,128,1536]{2,1,0:T(8,128)(2,1)S(1)}, u32[]{:S(2)}, u32[]{:S(2)}) collective-permute-start(bf16[2,128,1536]{2,1,0:T(8,128)(2,1)} %pad_maximum_fusion), channel_id=1, source_target_pairs={{0,4},{4,8},{8,12},{1,5},{5,9},{9,13},{2,6},{6,10},{10,14},{3,7},{... | collective-permute-start | bytes 2359304 | tf_op jit(solution)/shard_map/ppermute | solution.py:198
  6.6 0.0 copy-done.9
  6.6 0.1 copy.14
  6.7 0.0 copy-done.8
  6.7 0.1 add_convert_fusion
  6.8 0.6 pad.4.aux_ref
  7.4 2.3 %pool.1 = f32[16,16,128]{2,1,0:T(8,128)} custom-call(bf16[256,1536]{1,0:T(8,128)(2,1)} %bitcast.40, bf16[256,1536]{1,0:T(8,128)(2,1)} %bitcast.35, f32[12,8,128]{2,1,0:T(8,128)} %pad.4.aux_ref), custom_call_target="tpu_custom_call" | custom-call | tf_op jit(solution)/shard_map/pool/pallas_call | solution.py:62
  9.8 8.3 %all-to-all-start = ((f32[16,16,128]{2,1,0:T(8,128)}), f32[16,16,128]{2,1,0:T(8,128)}, u32[]{:S(2)}, u32[]{:S(2)}) async-start(f32[16,16,128]{2,1,0:T(8,128)} %pool.1), calls=%async_computation | async-start | bytes 262144 | tf_op jit(solution)/shard_map/all_to_all | solution.py:240
  18.1 0.0 copy-start.7
  18.1 1.0 pad_maximum_fusion.1
  19.0 1.3 collective-permute-start.1
  20.3 0.0 copy-done.7
  20.4 1.2 copy.15.wq_ref
  21.5 0.0 copy-start
  21.5 2.2 %copy.16.wk_ref = f32[12,128,64]{2,1,0:T(8,128)} copy(f32[12,128,64]{1,2,0:T(8,128)} %param.14) | data formatting | bytes 786432 | tf_op args[6]
  23.8 0.0 copy-done
  23.8 0.8 slice_bitcast_fusion.5
  24.6 3.8 %all-to-all-done.recv_ref = f32[16,16,128]{2,1,0:T(8,128)} async-done(((f32[16,16,128]{2,1,0:T(8,128)}), f32[16,16,128]{2,1,0:T(8,128)}, u32[]{:S(2)}, u32[]{:S(2)}) %all-to-all-start) | async-done | bytes 131104 | tf_op jit(solution)/shard_map/all_to_all | solution.py:240
  28.4 2.8 %router.1 = f32[128,128]{1,0:T(8,128)} custom-call(s32[1]{0:T(128)} %bitcast.21.head_ref, f32[16,16,128]{2,1,0:T(8,128)} %all-to-all-done.recv_ref, f32[12,128,64]{2,1,0:T(8,128)} %copy.15.wq_ref, f32[12,128,64]{2,1,0:T(8,128)} %copy.16.wk_ref), custom_call_target="tpu_custom_call" | custom-call | tf_op jit(solution)/shard_map/router/pallas_call | solution.py:112
  31.2 17.0 %all-to-all-start.1 = ((f32[32,4,128]{2,1,0:T(4,128)}), f32[32,4,128]{2,1,0:T(4,128)S(1)}, u32[]{:S(2)}, u32[]{:S(2)}) async-start(f32[32,4,128]{2,1,0:T(4,128)} %bitcast.49), calls=%async_computation.1 | async-start | bytes 131072 | tf_op jit(solution)/shard_map/all_to_all | solution.py:245
  48.2 0.0 copy-start.4
  48.2 0.1 slice_bitcast_fusion.4
  48.3 0.9 copy-done.4
  49.2 1.0 pad_maximum_fusion.2
  50.2 2.9 %collective-permute-start.2 = (bf16[2,128,1536]{2,1,0:T(8,128)(2,1)}, bf16[2,128,1536]{2,1,0:T(8,128)(2,1)}, u32[]{:S(2)}, u32[]{:S(2)}) collective-permute-start(bf16[2,128,1536]{2,1,0:T(8,128)(2,1)} %pad_maximum_fusion.2), channel_id=1, source_target_pairs={{0,1},{1,2},{2,3},{4,5},{5,6},{6,7},{8,9},{9,10},{10,11},{12,13},{... | collective-permute-start | bytes 2359304 | tf_op jit(solution)/shard_map/ppermute | solution.py:198
  53.1 10.6 %all-to-all-done.1 = f32[32,4,128]{2,1,0:T(4,128)S(1)} async-done(((f32[32,4,128]{2,1,0:T(4,128)}), f32[32,4,128]{2,1,0:T(4,128)S(1)}, u32[]{:S(2)}, u32[]{:S(2)}) %all-to-all-start.1) | async-done | bytes 65568 | tf_op jit(solution)/shard_map/all_to_all | solution.py:245
  63.7 0.6 broadcast_in_dim.17
  64.3 4.0 %all-to-all-start.2 = ((bf16[32,4,128]{2,1,0:T(4,128)(2,1)}), bf16[32,4,128]{2,1,0:T(4,128)(2,1)S(1)}, u32[]{:S(2)}, u32[]{:S(2)}) async-start(bf16[32,4,128]{2,1,0:T(4,128)(2,1)} %broadcast_in_dim.17), calls=%async_computation.2 | async-start | bytes 65536 | tf_op jit(solution)/shard_map/all_to_all | solution.py:225
  68.4 1.0 pad_maximum_fusion.3
  69.3 3.8 %collective-permute-start.3 = (bf16[2,128,1536]{2,1,0:T(8,128)(2,1)}, bf16[2,128,1536]{2,1,0:T(8,128)(2,1)}, u32[]{:S(2)}, u32[]{:S(2)}) collective-permute-start(bf16[2,128,1536]{2,1,0:T(8,128)(2,1)} %pad_maximum_fusion.3), channel_id=1, source_target_pairs={{1,0},{2,1},{3,2},{5,4},{6,5},{7,6},{9,8},{10,9},{11,10},{13,12},{... | collective-permute-start | bytes 2359304 | tf_op jit(solution)/shard_map/ppermute | solution.py:198
  73.2 9.9 %all-to-all-done.2 = bf16[32,4,128]{2,1,0:T(4,128)(2,1)S(1)} async-done(((bf16[32,4,128]{2,1,0:T(4,128)(2,1)}), bf16[32,4,128]{2,1,0:T(4,128)(2,1)S(1)}, u32[]{:S(2)}, u32[]{:S(2)}) %all-to-all-start.2) | async-done | bytes 32800 | tf_op jit(solution)/shard_map/all_to_all | solution.py:225
  83.1 0.1 copy.17
  83.2 0.9 broadcast_in_dim.19
  84.1 6.3 %all-to-all-start.3 = ((bf16[16,128,128]{1,2,0:T(8,128)(2,1)}), bf16[16,128,128]{1,2,0:T(8,128)(2,1)S(1)}, u32[]{:S(2)}, u32[]{:S(2)}) async-start(bf16[16,128,128]{1,2,0:T(8,128)(2,1)} %broadcast_in_dim.19), calls=%async_computation.3 | async-start | bytes 1048576 | tf_op jit(solution)/shard_map/all_to_all | solution.py:225
  90.4 0.0 collective-permute-done.rest_0_
  90.4 0.0 copy-start.2
  90.4 0.1 slice_bitcast_fusion.1
  90.5 0.8 copy-done.2
  91.3 0.0 collective-permute-done.1.rest_1_
  91.3 0.0 copy-start.3
  91.3 0.1 slice_bitcast_fusion
  91.4 0.8 copy-done.3
  92.2 0.1 pad_maximum_fusion.4
  92.3 3.4 %collective-permute-start.4 = (bf16[2,128,1536]{2,1,0:T(8,128)(2,1)S(1)}, bf16[2,128,1536]{2,1,0:T(8,128)(2,1)S(1)}, u32[]{:S(2)}, u32[]{:S(2)}) collective-permute-start(bf16[2,128,1536]{2,1,0:T(8,128)(2,1)S(1)} %pad_maximum_fusion.4), channel_id=1, source_target_pairs={{0,1},{1,2},{2,3},{4,5},{5,6},{6,7},{8,9},{9,10},{10,11},{12,13},{... | collective-permute-start | bytes 2359304 | tf_op jit(solution)/shard_map/ppermute | solution.py:198
  95.7 0.1 pad_maximum_fusion.5
  95.7 2.5 %collective-permute-start.5 = (bf16[2,128,1536]{2,1,0:T(8,128)(2,1)S(1)}, bf16[2,128,1536]{2,1,0:T(8,128)(2,1)S(1)}, u32[]{:S(2)}, u32[]{:S(2)}) collective-permute-start(bf16[2,128,1536]{2,1,0:T(8,128)(2,1)S(1)} %pad_maximum_fusion.5), channel_id=1, source_target_pairs={{1,0},{2,1},{3,2},{5,4},{6,5},{7,6},{9,8},{10,9},{11,10},{13,12},{... | collective-permute-start | bytes 2359304 | tf_op jit(solution)/shard_map/ppermute | solution.py:198
  98.2 0.0 collective-permute-done.2.rest_2_
  98.3 0.0 collective-permute-done.3.rest_3_
  98.3 20.6 %collective-permute-done.4.rest_4_ = bf16[2,128,1536]{2,1,0:T(8,128)(2,1)S(1)} collective-permute-done((bf16[2,128,1536]{2,1,0:T(8,128)(2,1)S(1)}, bf16[2,128,1536]{2,1,0:T(8,128)(2,1)S(1)}, u32[]{:S(2)}, u32[]{:S(2)}) %collective-permute-start.4) | collective-permute-done | bytes 786464 | tf_op jit(solution)/shard_map/ppermute | solution.py:198
  118.8 0.0 copy-start.5
  118.8 2.0 %collective-permute-done.5.rest_5_ = bf16[2,128,1536]{2,1,0:T(8,128)(2,1)S(1)} collective-permute-done((bf16[2,128,1536]{2,1,0:T(8,128)(2,1)S(1)}, bf16[2,128,1536]{2,1,0:T(8,128)(2,1)S(1)}, u32[]{:S(2)}, u32[]{:S(2)}) %collective-permute-start.5) | collective-permute-done | bytes 786464 | tf_op jit(solution)/shard_map/ppermute | solution.py:198
  120.9 0.0 copy-done.5
  120.9 0.9 copy-done.6
  121.8 10.9 %attend.1 = bf16[256,1536]{1,0:T(8,128)(2,1)} custom-call(s32[4,9]{1,0:T(4,128)} %bitcast.52, s32[8,1024]{1,0:T(8,128)} %constant.17.clone.ids_ref, bf16[256,1536]{1,0:T(8,128)(2,1)} %bitcast.41, bf16[256,1536]{1,0:T(8,128)(2,1)} %bitcast.36, bf16[256,1536]{1,0:T(8,128)(2,1)} %bitcast.38, bf16[2,128,1536]{2,1,0:T(8,128)(2,1)} %copy-done.2, ...), custom_call_target="tpu_custom_call" | custom-call | flops 1610612736 | bytes 7864320 | tf_op jit(solution)/shard_map/attend/pallas_call | solution.py:169
  132.7 0.0 all-to-all-done.3
  132.7 0.1 slice_convert_fusion
  132.8 1.0 fusion
  (3 shorter events, 0.1 us)
Async XLA Ops:
  0.6 1.4 %copy-start.1 = (bf16[1,16,16,1536]{3,2,1,0:T(8,128)(2,1)S(1)}, bf16[1,16,16,1536]{3,2,1,0:T(8,128)(2,1)}, u32[]{:S(2)}) copy-start(bf16[1,16,16,1536]{3,2,1,0:T(8,128)(2,1)} %param.10) | copy-start | bytes 2359300
  2.1 4.5 %copy-start.9 = (s32[1,2,2,12,3]{3,2,4,1,0:T(2,128)S(1)}, s32[1,2,2,12,3]{3,2,4,1,0:T(2,128)}, u32[]{:S(2)}) copy-start(s32[1,2,2,12,3]{3,2,4,1,0:T(2,128)} %param.12) | copy-start | bytes 1732
  2.1 4.6 %copy-start.8 = (s32[1,2,2,9]{3,2,1,0:T(2,128)S(1)}, s32[1,2,2,9]{3,2,1,0:T(2,128)}, u32[]{:S(2)}) copy-start(s32[1,2,2,9]{3,2,1,0:T(2,128)} %param.11) | copy-start | bytes 436
  3.0 87.4 %collective-permute-start = (bf16[2,128,1536]{2,1,0:T(8,128)(2,1)}, bf16[2,128,1536]{2,1,0:T(8,128)(2,1)S(1)}, u32[]{:S(2)}, u32[]{:S(2)}) collective-permute-start(bf16[2,128,1536]{2,1,0:T(8,128)(2,1)} %pad_maximum_fusion), channel_id=1, source_target_pairs={{0,4},{4,8},{8,12},{1,5},{5,9},{9,13},{2,6},{6,10},{10,14},{3,7},{... | collective-permute-start | bytes 2359304 | tf_op jit(solution)/shard_map/ppermute | solution.py:198
  9.8 18.6 %all-to-all-start = ((f32[16,16,128]{2,1,0:T(8,128)}), f32[16,16,128]{2,1,0:T(8,128)}, u32[]{:S(2)}, u32[]{:S(2)}) async-start(f32[16,16,128]{2,1,0:T(8,128)} %pool.1), calls=%async_computation | async-start | bytes 262144 | tf_op jit(solution)/shard_map/all_to_all | solution.py:240
  18.1 2.3 %copy-start.7 = (f32[12,128,64]{1,2,0:T(8,128)S(1)}, f32[12,128,64]{1,2,0:T(8,128)}, u32[]{:S(2)}) copy-start(f32[12,128,64]{1,2,0:T(8,128)} %param.13) | copy-start | bytes 1179652
  19.0 72.3 %collective-permute-start.1 = (bf16[2,128,1536]{2,1,0:T(8,128)(2,1)}, bf16[2,128,1536]{2,1,0:T(8,128)(2,1)S(1)}, u32[]{:S(2)}, u32[]{:S(2)}) collective-permute-start(bf16[2,128,1536]{2,1,0:T(8,128)(2,1)} %pad_maximum_fusion.1), channel_id=1, source_target_pairs={{4,0},{8,4},{12,8},{5,1},{9,5},{13,9},{6,2},{10,6},{14,10},{7,3},{... | collective-permute-start | bytes 2359304 | tf_op jit(solution)/shard_map/ppermute | solution.py:198
  21.5 2.3 %copy-start = (bf16[1,16,16,1536]{3,2,1,0:T(8,128)(2,1)S(1)}, bf16[1,16,16,1536]{3,2,1,0:T(8,128)(2,1)}, u32[]{:S(2)}) copy-start(bf16[1,16,16,1536]{3,2,1,0:T(8,128)(2,1)} %param.9) | copy-start | bytes 2359300
  31.2 32.5 %all-to-all-start.1 = ((f32[32,4,128]{2,1,0:T(4,128)}), f32[32,4,128]{2,1,0:T(4,128)S(1)}, u32[]{:S(2)}, u32[]{:S(2)}) async-start(f32[32,4,128]{2,1,0:T(4,128)} %bitcast.49), calls=%async_computation.1 | async-start | bytes 131072 | tf_op jit(solution)/shard_map/all_to_all | solution.py:245
  48.2 1.0 copy-start.4
  50.2 48.1 %collective-permute-start.2 = (bf16[2,128,1536]{2,1,0:T(8,128)(2,1)}, bf16[2,128,1536]{2,1,0:T(8,128)(2,1)}, u32[]{:S(2)}, u32[]{:S(2)}) collective-permute-start(bf16[2,128,1536]{2,1,0:T(8,128)(2,1)} %pad_maximum_fusion.2), channel_id=1, source_target_pairs={{0,1},{1,2},{2,3},{4,5},{5,6},{6,7},{8,9},{9,10},{10,11},{12,13},{... | collective-permute-start | bytes 2359304 | tf_op jit(solution)/shard_map/ppermute | solution.py:198
  64.3 18.7 %all-to-all-start.2 = ((bf16[32,4,128]{2,1,0:T(4,128)(2,1)}), bf16[32,4,128]{2,1,0:T(4,128)(2,1)S(1)}, u32[]{:S(2)}, u32[]{:S(2)}) async-start(bf16[32,4,128]{2,1,0:T(4,128)(2,1)} %broadcast_in_dim.17), calls=%async_computation.2 | async-start | bytes 65536 | tf_op jit(solution)/shard_map/all_to_all | solution.py:225
  69.3 28.9 %collective-permute-start.3 = (bf16[2,128,1536]{2,1,0:T(8,128)(2,1)}, bf16[2,128,1536]{2,1,0:T(8,128)(2,1)}, u32[]{:S(2)}, u32[]{:S(2)}) collective-permute-start(bf16[2,128,1536]{2,1,0:T(8,128)(2,1)} %pad_maximum_fusion.3), channel_id=1, source_target_pairs={{1,0},{2,1},{3,2},{5,4},{6,5},{7,6},{9,8},{10,9},{11,10},{13,12},{... | collective-permute-start | bytes 2359304 | tf_op jit(solution)/shard_map/ppermute | solution.py:198
  84.1 48.6 %all-to-all-start.3 = ((bf16[16,128,128]{1,2,0:T(8,128)(2,1)}), bf16[16,128,128]{1,2,0:T(8,128)(2,1)S(1)}, u32[]{:S(2)}, u32[]{:S(2)}) async-start(bf16[16,128,128]{1,2,0:T(8,128)(2,1)} %broadcast_in_dim.19), calls=%async_computation.3 | async-start | bytes 1048576 | tf_op jit(solution)/shard_map/all_to_all | solution.py:225
  90.4 0.9 copy-start.2
  91.3 0.9 copy-start.3
  92.3 26.5 %collective-permute-start.4 = (bf16[2,128,1536]{2,1,0:T(8,128)(2,1)S(1)}, bf16[2,128,1536]{2,1,0:T(8,128)(2,1)S(1)}, u32[]{:S(2)}, u32[]{:S(2)}) collective-permute-start(bf16[2,128,1536]{2,1,0:T(8,128)(2,1)S(1)} %pad_maximum_fusion.4), channel_id=1, source_target_pairs={{0,1},{1,2},{2,3},{4,5},{5,6},{6,7},{8,9},{9,10},{10,11},{12,13},{... | collective-permute-start | bytes 2359304 | tf_op jit(solution)/shard_map/ppermute | solution.py:198
  95.7 25.1 %collective-permute-start.5 = (bf16[2,128,1536]{2,1,0:T(8,128)(2,1)S(1)}, bf16[2,128,1536]{2,1,0:T(8,128)(2,1)S(1)}, u32[]{:S(2)}, u32[]{:S(2)}) collective-permute-start(bf16[2,128,1536]{2,1,0:T(8,128)(2,1)S(1)} %pad_maximum_fusion.5), channel_id=1, source_target_pairs={{1,0},{2,1},{3,2},{5,4},{6,5},{7,6},{9,8},{10,9},{11,10},{13,12},{... | collective-permute-start | bytes 2359304 | tf_op jit(solution)/shard_map/ppermute | solution.py:198
  118.8 2.1 %copy-start.5 = (bf16[2,128,1536]{2,1,0:T(8,128)(2,1)}, bf16[2,128,1536]{2,1,0:T(8,128)(2,1)S(1)}, u32[]{:S(2)}) copy-start(bf16[2,128,1536]{2,1,0:T(8,128)(2,1)S(1)} %collective-permute-done.4.rest_4_) | copy-start | bytes 2359300
  120.9 0.9 copy-start.6

commit v2 on v1

--- a/solution.py
+++ b/solution.py
@@ -7,6 +7,7 @@
 from jax import lax
 from jax.experimental import pallas as pl
 from jax.experimental.pallas import tpu as pltpu
+from jax.sharding import Mesh
 from jax.sharding import PartitionSpec as P
 
 HEADS = 12
@@ -25,6 +26,9 @@
 LIVE_CAP = 3.4e38
 DEAD_CAP = -1e30
 TILES = ("py", "px")
+NEAR = ("x", "core")
+IMG = ("x", "far", "core")
+IMG_SIZES = (4, 4, 2)
 
 
 def key_block_ids():
@@ -77,8 +81,8 @@
     )
     ab, abt, atb = (((1,), (0,)), ((), ())), (((1,), (1,)), ((), ())), (((0,), (0,)), ((), ()))
     pooled_q, pooled_k, aux = pq_ref[...], pk_ref[...], ax_ref[...]
-    route_q = dot(pooled_q, wq_ref[0], ab)
-    route_k = dot(pooled_k, wk_ref[0], ab)
+    route_q = dot(pooled_q, wq_ref[0], abt)
+    route_k = dot(pooled_k, wk_ref[0], abt)
     logits = dot(route_q, route_k, abt) / math.sqrt(RW)
 
     def place(i):
@@ -102,16 +106,15 @@
     soft = weights / jnp.sum(weights, axis=1, keepdims=True)
     count = jnp.sum(picks, axis=1, keepdims=True)
     slope = jnp.where(live > 0.5, count * soft - picks, 0.0) * (1.0 / (normal * math.sqrt(RW)))
-    grad_q = dot(pooled_q, dot(slope, route_k, ab), atb)
-    grad_k = dot(pooled_k, dot(slope, route_q, atb), atb)
-    out_ref[...] = jnp.concatenate([grad_q, grad_k], axis=1)
+    out_ref[0:RW, :] = dot(dot(slope, route_k, ab), pooled_q, atb)
+    out_ref[RW:, :] = dot(dot(slope, route_q, atb), pooled_k, atb)
 
 
 def router_grads(head, recv, weights_q, weights_k, normal):
-    spec = pl.BlockSpec((1, DH, RW), lambda i, h: (h[0], 0, 0))
+    spec = pl.BlockSpec((1, RW, DH), lambda i, h: (h[0], 0, 0))
     return pl.pallas_call(
         functools.partial(router_kernel, normal),
-        out_shape=jax.ShapeDtypeStruct((DH, 2 * RW), jnp.float32),
+        out_shape=jax.ShapeDtypeStruct((2 * RW, DH), jnp.float32),
         grid_spec=pltpu.PrefetchScalarGridSpec(
             num_scalar_prefetch=1,
             grid=(1,),
@@ -120,7 +123,7 @@
                 spec,
                 spec,
             ],
-            out_specs=pl.BlockSpec((DH, 2 * RW), lambda i, h: (0, 0)),
+            out_specs=pl.BlockSpec((2 * RW, DH), lambda i, h: (0, 0)),
             scratch_shapes=[pltpu.VMEM((4 * SLOTS, DH), jnp.float32)] * 3,
         ),
         name="router",
@@ -128,7 +131,8 @@
 
 
 def attend_kernel(pat_ref, ids_ref, q_ref, k_ref, v_ref, *rest):
-    sides, out_ref, cap_ref = rest[:6], rest[6], rest[7]
+    sides, (corner_l, corner_r, corner_a, corner_b, out_ref, cap_ref) = rest[:4], rest[4:]
+    cell = BS * BS
 
     @pl.when(pl.program_id(0) == 0)
     def _():
@@ -148,8 +152,23 @@
     for h in range(HSTEP):
         lanes = slice(h * DH, (h + 1) * DH)
         query = q_ref[:, lanes]
-        keys = jnp.concatenate([k_ref[:, lanes]] + [s[0, :, lanes] for s in sides], axis=0)
-        values = jnp.concatenate([v_ref[:, lanes]] + [s[1, :, lanes] for s in sides], axis=0)
+        keys = jnp.concatenate(
+            [k_ref[:, lanes]]
+            + [s[0, :, lanes] for s in sides]
+            + [corner_l[:, lanes], corner_r[:, lanes]],
+            axis=0,
+        )
+        values = jnp.concatenate(
+            [v_ref[:, lanes]]
+            + [s[1, :, lanes] for s in sides]
+            + [
+                corner_a[:cell, lanes],
+                corner_b[:cell, lanes],
+                corner_a[cell:, lanes],
+                corner_b[cell:, lanes],
+            ],
+            axis=0,
+        )
         scores = lax.dot_general(
             query, keys, (((1,), (1,)), ((), ())), preferred_element_type=jnp.float32
         )
@@ -162,10 +181,11 @@
         out_ref[:, lanes] = out.astype(jnp.bfloat16)
 
 
-def attend(pattern, query, key, value, sides):
+def attend(pattern, query, key, value, sides, corners):
     wide = HSTEP * DH
     own = pl.BlockSpec((TOK, wide), lambda h: (0, h))
     side = pl.BlockSpec((2, EDGE, wide), lambda h: (0, 0, h))
+    corner = pl.BlockSpec((EDGE, wide), lambda h: (0, h))
     return pl.pallas_call(
         attend_kernel,
         out_shape=jax.ShapeDtypeStruct((TOK, FEAT), jnp.bfloat16),
@@ -177,7 +197,8 @@
             own,
             own,
         ]
-        + [side] * 6,
+        + [side] * 4
+        + [corner] * 4,
         out_specs=own,
         scratch_shapes=[pltpu.VMEM((TOK, NKEY), jnp.float32)],
         cost_estimate=pl.CostEstimate(
@@ -186,7 +207,7 @@
             transcendentals=HEADS * TOK * NKEY,
         ),
         name="attend",
-    )(pattern, jnp.asarray(key_block_ids()), query, key, value, *sides)
+    )(pattern, jnp.asarray(key_block_ids()), query, key, value, *sides, *corners)
 
 
 def shift(x, axis, step):
@@ -198,35 +219,52 @@
     return lax.ppermute(x, axis, pairs)
 
 
-def halos(key, value):
-    both = (key, value)
-
+def edges(key, value):
     def flat(cut):
-        return jnp.stack([cut(x).reshape(EDGE, FEAT) for x in both])
-
-    above = shift(flat(lambda x: x[TILE - BS :]), "py", 1)
-    below = shift(flat(lambda x: x[:BS]), "py", -1)
-    left = shift(flat(lambda x: x[:, TILE - BS :]), "px", 1)
-    right = shift(flat(lambda x: x[:, :BS]), "px", -1)
-
-    def corners(lo):
+        return jnp.stack([cut(x).reshape(EDGE, FEAT) for x in (key, value)])
+
+    return (
+        flat(lambda x: x[TILE - BS :]),
+        flat(lambda x: x[:BS]),
+        flat(lambda x: x[:, TILE - BS :]),
+        flat(lambda x: x[:, :BS]),
+    )
+
+
+def sides_of(low, high, right, left):
+    return (
+        shift(low, "py", 1), shift(high, "py", -1), shift(right, "px", 1), shift(left, "px", -1)
+    )
+
+
+def corners_of(above, below, left, right):
+    def columns(lo):
         cuts = [
-            x.reshape(2, BS, TILE, FEAT)[:, :, lo : lo + BS].reshape(2, BS * BS, FEAT)
+            x[0].reshape(BS, TILE, FEAT)[:, lo : lo + BS].reshape(BS * BS, FEAT)
             for x in (above, below)
         ]
-        return jnp.concatenate(cuts, axis=1)
-
-    corner_l = shift(corners(TILE - BS), "px", 1)
-    corner_r = shift(corners(0), "px", -1)
-    return above, below, left, right, corner_l, corner_r
+        return jnp.concatenate(cuts, axis=0)
+
+    def rows(lo):
+        return jnp.concatenate([x[1, lo * BS : lo * BS + BS * BS] for x in (left, right)], axis=0)
+
+    return (
+        shift(columns(TILE - BS), "px", 1),
+        shift(columns(0), "px", -1),
+        shift(rows(TILE - BS), "py", 1),
+        shift(rows(0), "py", -1),
+    )
+
+
+def exchange(x, axis):
+    return lax.all_to_all(x, axis, 0, 0)
 
 
 def everyone(x, axis, count):
-    return lax.all_to_all(jnp.broadcast_to(x[None], (count,) + x.shape), axis, 0, 0)
+    return exchange(jnp.broadcast_to(x[None], (count,) + x.shape), axis)
 
 
 def per_device(queries, keys, values, pattern, targets, router_q, router_k):
-    images = lax.axis_size("img")
     tiles_y, tiles_x = lax.axis_size("py"), lax.axis_size("px")
     tiles = tiles_y * tiles_x
     normal = float(TOPK * HEADS * 4 * tiles)
@@ -237,32 +275,44 @@
     aux = jnp.pad(aux.astype(jnp.float32), ((0, 0), (0, 4), (0, DH - NOFF - TOPK)))
 
     sent = pool(query, key, aux)
-    recv = lax.all_to_all(sent, TILES, 0, 0)
-    sides = halos(keys[0], values[0])
+    recv = exchange(sent, TILES)
+    rims = edges(keys[0], values[0])
+    sides = sides_of(*rims)
     me = lax.axis_index("py") * tiles_x + lax.axis_index("px")
     head = jnp.minimum(me, HEADS - 1).astype(jnp.int32).reshape(1)
-    grads = router_grads(head, recv, router_q, router_k, normal)
-    parts = lax.all_to_all(grads.reshape(images, DH // images, 2 * RW), "img", 0, 0)
-    part = jnp.sum(parts, axis=0).astype(jnp.bfloat16)
-    mine = everyone(part, "img", images).reshape(DH, 2 * RW)
-    every = everyone(mine, TILES, tiles)[:HEADS].astype(jnp.float32)
-    attended = attend(pat, query, key, value, sides)
-    return (attended.reshape(1, TILE, TILE, FEAT), every[:, :, :RW], every[:, :, RW:])
+    grads = router_grads(
+        head, recv, router_q.swapaxes(1, 2), router_k.swapaxes(1, 2), normal
+    )
+    near = lax.axis_size("x") * lax.axis_size("core")
+    rows = 2 * RW // near
+    parts = exchange(grads.reshape(near, rows, DH), NEAR)
+    part = jnp.sum(parts, axis=0)
+    far = everyone(part, "far", lax.axis_size("far"))
+    part = jnp.sum(far, axis=0).astype(jnp.bfloat16)
+    heads = everyone(part, TILES, tiles)
+    every = everyone(heads, NEAR, near)[:, :HEADS].astype(jnp.float32)
+    every = every.transpose(1, 0, 2, 3).reshape(HEADS, 2 * RW, DH)
+    grad_q, grad_k = (x.swapaxes(1, 2) for x in (every[:, :RW], every[:, RW:]))
+    corners = corners_of(*sides)
+    attended = attend(pat, query, key, value, sides, corners)
+    return (attended.reshape(1, TILE, TILE, FEAT), grad_q, grad_k)
 
 
 def solution(mesh):
+    sizes = IMG_SIZES if mesh.shape["img"] == math.prod(IMG_SIZES) else (1, 1, mesh.shape["img"])
+    split = Mesh(mesh.devices.reshape(sizes + mesh.devices.shape[1:]), IMG + TILES)
     return jax.shard_map(
         per_device,
-        mesh=mesh,
+        mesh=split,
         in_specs=(
-            P("img", "py", "px", None),
-            P("img", "py", "px", None),
-            P("img", "py", "px", None),
-            P("img", "py", "px", None),
-            P("img", "py", "px", None, None),
+            P(IMG, "py", "px", None),
+            P(IMG, "py", "px", None),
+            P(IMG, "py", "px", None),
+            P(IMG, "py", "px", None),
+            P(IMG, "py", "px", None, None),
             P(),
             P(),
         ),
-        out_specs=(P("img", "py", "px", None), P(), P()),
+        out_specs=(P(IMG, "py", "px", None), P(), P()),
         check_vma=False,
     )

time: 134 us -> 118 us (0.88)
  the two profiles are of different devices: /device:TPU:32 before, /device:TPU:2 now
where the time goes in v2:
time: 118 us; the launch traced here: 117 us
  starting transfers between devices  59.4 us (50%)
  waiting for transfers between devices  23.1 us (20%)
  Pallas kernels  16.1 us (14%)
  local copies, waits for them, and re-layouts  11.9 us (10%)
  other arithmetic  5.68 us (5%)
    all_to_all x5, starting transfers between devices, exchange(): return lax.all_to_all(x, axis, 0, 0)  38.6 us
    ppermute x8, starting transfers between devices, shift(): return lax.ppermute(x, axis, pairs)  20.8 us
    all_to_all x5, waiting for transfers between devices, exchange(): return lax.all_to_all(x, axis, 0, 0)  20.5 us
    pallas_call x1, Pallas kernels, attend(): pl.pallas_call(attend_kernel, out_shape=jax.ShapeDtypeStruct((TOK, FEAT),...  11 us
    another operation x4, other arithmetic, flat(): return jnp.stack([cut(x).reshape(EDGE, FEAT) for x in (key, value)])  3.81 us
    broadcast_in_dim x3, local copies, waits for them, and re-layouts, everyone(): return exchange(jnp.broadcast_to(x[None], (count,) + x.shape), axis)  2.96 us
    pallas_call x1, Pallas kernels, router_grads(): pl.pallas_call(functools.partial(router_kernel, normal), out_shape=jax.Sh...  2.69 us
    ppermute x8, waiting for transfers between devices, shift(): return lax.ppermute(x, axis, pairs)  2.69 us
  transfers between devices with their start and end apart: 13, of which 3 were waited for; matrix products, arithmetic and copies ran while one was open for 10% of the time, Pallas kernels for 14%

profile of v2, /device:TPU:2, one launch (start us, length us, event | category | flops | bytes accessed | tf_op | source)
XLA Modules:
  0.0 117.2 jit_solution(9152157256936197264)
XLA Ops:
  0.6 0.0 copy-start.1
  0.6 1.2 %fusion = (bf16[1,8,16,1536]{3,2,1,0:T(8,128)(2,1)S(1)}, bf16[1,8,16,1536]{3,2,1,0:T(8,128)(2,1)S(1)}) fusion(bf16[1,16,16,1536]{3,2,1,0:T(8,128)(2,1)} %param.9), kind=kLoop, calls=%fused_computation.24 | loop fusion | bytes 1572864 | tf_op jit(solution)/shard_map/slice | solution.py:228
  1.9 0.1 copy-done.1
  2.0 0.1 fusion.1
  2.1 0.9 pad_maximum_fusion
  3.0 3.5 %collective-permute-start = (bf16[2,128,1536]{2,1,0:T(8,128)(2,1)}, bf16[2,128,1536]{2,1,0:T(8,128)(2,1)S(1)}, u32[]{:S(2)}, u32[]{:S(2)}) collective-permute-start(bf16[2,128,1536]{2,1,0:T(8,128)(2,1)} %pad_maximum_fusion), channel_id=1, source_target_pairs={{0,4},{4,8},{8,12},{1,5},{5,9},{9,13},{2,6},{6,10},{10,14},{3,7},{... | collective-permute-start | bytes 2359304 | tf_op jit(solution)/shard_map/ppermute | solution.py:219
  6.5 0.0 copy-start.12
  6.5 0.0 copy-start.11
  6.6 1.0 pad_maximum_fusion.1
  7.5 1.3 %collective-permute-start.1 = (bf16[2,128,1536]{2,1,0:T(8,128)(2,1)}, bf16[2,128,1536]{2,1,0:T(8,128)(2,1)S(1)}, u32[]{:S(2)}, u32[]{:S(2)}) collective-permute-start(bf16[2,128,1536]{2,1,0:T(8,128)(2,1)} %pad_maximum_fusion.1), channel_id=1, source_target_pairs={{4,0},{8,4},{12,8},{5,1},{9,5},{13,9},{6,2},{10,6},{14,10},{7,3},{... | collective-permute-start | bytes 2359304 | tf_op jit(solution)/shard_map/ppermute | solution.py:219
  8.8 0.0 copy-done.12
  8.8 0.1 copy.15
  8.9 0.0 copy-done.11
  9.0 0.1 add_convert_fusion
  9.0 0.6 pad.4.aux_ref
  9.7 2.4 %pool.1 = f32[16,16,128]{2,1,0:T(8,128)} custom-call(bf16[256,1536]{1,0:T(8,128)(2,1)} %bitcast.56, bf16[256,1536]{1,0:T(8,128)(2,1)} %bitcast.51, f32[12,8,128]{2,1,0:T(8,128)} %pad.4.aux_ref), custom_call_target="tpu_custom_call" | custom-call | tf_op jit(solution)/shard_map/pool/pallas_call | solution.py:66
  12.1 9.7 %all-to-all-start = ((f32[16,16,128]{2,1,0:T(8,128)}), f32[16,16,128]{2,1,0:T(8,128)}, u32[]{:S(2)}, u32[]{:S(2)}) async-start(f32[16,16,128]{2,1,0:T(8,128)} %pool.1), calls=%async_computation | async-start | bytes 262144 | tf_op jit(solution)/shard_map/all_to_all | solution.py:260
  21.8 0.0 copy-done
  21.8 0.8 slice_bitcast_fusion.3
  22.6 0.8 slice_bitcast_fusion.2
  23.4 6.8 %all-to-all-done.recv_ref = f32[16,16,128]{2,1,0:T(8,128)} async-done(((f32[16,16,128]{2,1,0:T(8,128)}), f32[16,16,128]{2,1,0:T(8,128)}, u32[]{:S(2)}, u32[]{:S(2)}) %all-to-all-start) | async-done | bytes 131104 | tf_op jit(solution)/shard_map/all_to_all | solution.py:260
  30.2 2.7 %router.1 = f32[128,128]{1,0:T(8,128)} custom-call(s32[1]{0:T(128)} %bitcast.25.head_ref, f32[16,16,128]{2,1,0:T(8,128)} %all-to-all-done.recv_ref, f32[12,64,128]{2,1,0:T(8,128)} %bitcast.66, f32[12,64,128]{2,1,0:T(8,128)} %bitcast.67), custom_call_target="tpu_custom_call" | custom-call | tf_op jit(solution)/shard_map/router/pallas_call | solution.py:115
  32.9 4.8 %all-to-all-start.1 = ((f32[8,16,128]{2,1,0:T(8,128)}), f32[8,16,128]{2,1,0:T(8,128)}, u32[]{:S(2)}, u32[]{:S(2)}) async-start(f32[8,16,128]{2,1,0:T(8,128)} %bitcast.68), calls=%async_computation.1 | async-start | bytes 131072 | tf_op jit(solution)/shard_map/all_to_all | solution.py:260
  37.8 0.0 copy-done.5
  37.8 1.0 pad_maximum_fusion.2
  38.7 3.7 %collective-permute-start.2 = (bf16[2,128,1536]{2,1,0:T(8,128)(2,1)}, bf16[2,128,1536]{2,1,0:T(8,128)(2,1)S(1)}, u32[]{:S(2)}, u32[]{:S(2)}) collective-permute-start(bf16[2,128,1536]{2,1,0:T(8,128)(2,1)} %pad_maximum_fusion.2), channel_id=1, source_target_pairs={{0,1},{1,2},{2,3},{4,5},{5,6},{6,7},{8,9},{9,10},{10,11},{12,13},{... | collective-permute-start | bytes 2359304 | tf_op jit(solution)/shard_map/ppermute | solution.py:219
  42.5 0.0 all-to-all-done.1
  42.5 0.9 reduce_sum.18
  43.3 0.6 broadcast_in_dim.9
  44.0 14.5 %all-to-all-start.2 = ((f32[4,16,128]{2,1,0:T(8,128)}), f32[4,16,128]{2,1,0:T(8,128)S(1)}, u32[]{:S(2)}, u32[]{:S(2)}) async-start(f32[4,16,128]{2,1,0:T(8,128)} %broadcast_in_dim.9), calls=%async_computation.2 | async-start | bytes 65536 | tf_op jit(solution)/shard_map/all_to_all | solution.py:260
  58.5 0.0 copy-done.6
  58.5 0.9 pad_maximum_fusion.3
  59.4 1.3 %collective-permute-start.3 = (bf16[2,128,1536]{2,1,0:T(8,128)(2,1)}, bf16[2,128,1536]{2,1,0:T(8,128)(2,1)}, u32[]{:S(2)}, u32[]{:S(2)}) collective-permute-start(bf16[2,128,1536]{2,1,0:T(8,128)(2,1)} %pad_maximum_fusion.3), channel_id=1, source_target_pairs={{1,0},{2,1},{3,2},{5,4},{6,5},{7,6},{9,8},{10,9},{11,10},{13,12},{... | collective-permute-start | bytes 2359304 | tf_op jit(solution)/shard_map/ppermute | solution.py:219
  60.7 13.6 %all-to-all-done.2 = f32[4,16,128]{2,1,0:T(8,128)S(1)} async-done(((f32[4,16,128]{2,1,0:T(8,128)}), f32[4,16,128]{2,1,0:T(8,128)S(1)}, u32[]{:S(2)}, u32[]{:S(2)}) %all-to-all-start.2) | async-done | bytes 32800 | tf_op jit(solution)/shard_map/all_to_all | solution.py:260
  74.3 0.6 broadcast_in_dim.10
  75.0 4.8 %all-to-all-start.3 = ((bf16[16,16,128]{2,1,0:T(8,128)(2,1)}), bf16[16,16,128]{2,1,0:T(8,128)(2,1)}, u32[]{:S(2)}, u32[]{:S(2)}) async-start(bf16[16,16,128]{2,1,0:T(8,128)(2,1)} %broadcast_in_dim.10), calls=%async_computation.3 | async-start | bytes 131072 | tf_op jit(solution)/shard_map/all_to_all | solution.py:260
  79.8 0.0 collective-permute-done.rest_0_
  79.8 0.0 copy-start.2
  79.8 0.9 copy-done.2
  80.7 0.0 collective-permute-done.1.rest_1_
  80.7 1.2 %slice-done = bf16[1,128,1536]{2,1,0:T(8,128)(2,1)S(1)} async-done(((bf16[2,128,1536]{2,1,0:T(8,128)(2,1)}), bf16[1,128,1536]{2,1,0:T(8,128)(2,1)S(1)}, s32[]{:S(2)}) %slice-start) | async-done | bytes 393240 | tf_op jit(solution)/shard_map/slice | solution.py:243
  81.9 0.1 slice_bitcast_fusion.10
  82.0 1.3 %collective-permute-start.5 = (bf16[128,1536]{1,0:T(8,128)(2,1)S(1)}, bf16[128,1536]{1,0:T(8,128)(2,1)S(1)}, u32[]{:S(2)}, u32[]{:S(2)}) collective-permute-start(bf16[128,1536]{1,0:T(8,128)(2,1)S(1)} %pad_maximum_fusion.5), channel_id=1, source_target_pairs={{1,0},{2,1},{3,2},{5,4},{6,5},{7,6},{9,8},{10,9},{11,10},{13,12},{... | collective-permute-start | bytes 1179656 | tf_op jit(solution)/shard_map/ppermute | solution.py:219
  83.4 4.6 %collective-permute-start.4 = (bf16[128,1536]{1,0:T(8,128)(2,1)S(1)}, bf16[128,1536]{1,0:T(8,128)(2,1)S(1)}, u32[]{:S(2)}, u32[]{:S(2)}) collective-permute-start(bf16[128,1536]{1,0:T(8,128)(2,1)S(1)} %pad_maximum_fusion.4), channel_id=1, source_target_pairs={{0,1},{1,2},{2,3},{4,5},{5,6},{6,7},{8,9},{9,10},{10,11},{12,13},{... | collective-permute-start | bytes 1179656 | tf_op jit(solution)/shard_map/ppermute | solution.py:219
  88.0 0.0 collective-permute-done.2.rest_2_
  88.0 0.0 collective-permute-done.3.rest_3_
  88.0 1.3 %slice_bitcast_fusion.6 = (bf16[64,1536]{1,0:T(8,128)(2,1)S(1)}, bf16[64,1536]{1,0:T(8,128)(2,1)S(1)}) fusion(bf16[2,128,1536]{2,1,0:T(8,128)(2,1)} %collective-permute-done.3.rest_3_), kind=kLoop, calls=%fused_computation.15 | loop fusion | bytes 786432 | tf_op jit(solution)/shard_map/squeeze | solution.py:249
  89.4 3.8 %collective-permute-start.6 = (bf16[128,1536]{1,0:T(8,128)(2,1)S(1)}, bf16[128,1536]{1,0:T(8,128)(2,1)S(1)}, u32[]{:S(2)}, u32[]{:S(2)}) collective-permute-start(bf16[128,1536]{1,0:T(8,128)(2,1)S(1)} %pad_maximum_fusion.6), channel_id=1, source_target_pairs={{0,4},{4,8},{8,12},{1,5},{5,9},{9,13},{2,6},{6,10},{10,14},{3,7},{... | collective-permute-start | bytes 1179656 | tf_op jit(solution)/shard_map/ppermute | solution.py:219
  93.2 0.8 pad_maximum_fusion.7
  93.9 1.3 %collective-permute-start.7 = (bf16[128,1536]{1,0:T(8,128)(2,1)}, bf16[128,1536]{1,0:T(8,128)(2,1)S(1)}, u32[]{:S(2)}, u32[]{:S(2)}) collective-permute-start(bf16[128,1536]{1,0:T(8,128)(2,1)} %pad_maximum_fusion.7), channel_id=1, source_target_pairs={{4,0},{8,4},{12,8},{5,1},{9,5},{13,9},{6,2},{10,6},{14,10},{7,3},{... | collective-permute-start | bytes 1179656 | tf_op jit(solution)/shard_map/ppermute | solution.py:219
  95.2 0.0 all-to-all-done.3
  95.2 1.7 %broadcast_in_dim.11 = bf16[8,16,16,128]{3,2,1,0:T(8,128)(2,1)} broadcast(bf16[16,16,128]{2,1,0:T(8,128)(2,1)} %all-to-all-done.3), dimensions={1,2,3} | broadcast | bytes 589824 | tf_op jit(solution)/shard_map/broadcast_in_dim | solution.py:264
  96.9 4.8 %all-to-all-start.4 = ((bf16[8,16,16,128]{3,2,1,0:T(8,128)(2,1)}), bf16[8,16,16,128]{3,2,1,0:T(8,128)(2,1)S(1)}, u32[]{:S(2)}, u32[]{:S(2)}) async-start(bf16[8,16,16,128]{3,2,1,0:T(8,128)(2,1)} %broadcast_in_dim.11), calls=%async_computation.4 | async-start | bytes 1048576 | tf_op jit(solution)/shard_map/all_to_all | solution.py:260
  101.7 0.0 collective-permute-done.5.rest_5_
  101.8 0.0 collective-permute-done.4.rest_4_
  101.8 0.0 copy-start.8
  101.8 0.0 collective-permute-done.6.rest_6_
  101.8 2.7 %collective-permute-done.7.rest_7_ = bf16[128,1536]{1,0:T(8,128)(2,1)S(1)} collective-permute-done((bf16[128,1536]{1,0:T(8,128)(2,1)}, bf16[128,1536]{1,0:T(8,128)(2,1)S(1)}, u32[]{:S(2)}, u32[]{:S(2)}) %collective-permute-start.7) | collective-permute-done | bytes 393248 | tf_op jit(solution)/shard_map/ppermute | solution.py:219
  104.5 0.0 copy-done.8
  104.5 0.7 copy-done.10
  105.2 11.0 %attend.1 = bf16[256,1536]{1,0:T(8,128)(2,1)} custom-call(s32[4,9]{1,0:T(4,128)} %bitcast.70, s32[8,1024]{1,0:T(8,128)} %constant.17.clone.ids_ref, bf16[256,1536]{1,0:T(8,128)(2,1)} %bitcast.57, bf16[256,1536]{1,0:T(8,128)(2,1)} %bitcast.52, bf16[256,1536]{1,0:T(8,128)(2,1)} %bitcast.54, bf16[2,128,1536]{2,1,0:T(8,128)(2,1)} %copy-done.2, ...), custom_call_target="tpu_custom_call" | custom-call | flops 1610612736 | bytes 7864320 | tf_op jit(solution)/shard_map/attend/pallas_call | solution.py:189
  116.2 0.0 all-to-all-done.4
  116.2 0.1 copy_convert_fusion
  116.3 0.9 slice_bitcast_fusion
  (20 shorter events, 0.2 us)
Async XLA Ops:
  0.6 1.4 %copy-start.1 = (bf16[1,16,16,1536]{3,2,1,0:T(8,128)(2,1)S(1)}, bf16[1,16,16,1536]{3,2,1,0:T(8,128)(2,1)}, u32[]{:S(2)}) copy-start(bf16[1,16,16,1536]{3,2,1,0:T(8,128)(2,1)} %param.10) | copy-start | bytes 2359300
  3.0 76.8 %collective-permute-start = (bf16[2,128,1536]{2,1,0:T(8,128)(2,1)}, bf16[2,128,1536]{2,1,0:T(8,128)(2,1)S(1)}, u32[]{:S(2)}, u32[]{:S(2)}) collective-permute-start(bf16[2,128,1536]{2,1,0:T(8,128)(2,1)} %pad_maximum_fusion), channel_id=1, source_target_pairs={{0,4},{4,8},{8,12},{1,5},{5,9},{9,13},{2,6},{6,10},{10,14},{3,7},{... | collective-permute-start | bytes 2359304 | tf_op jit(solution)/shard_map/ppermute | solution.py:219
  6.5 2.3 %copy-start.12 = (s32[1,2,2,12,3]{3,2,4,1,0:T(2,128)S(1)}, s32[1,2,2,12,3]{3,2,4,1,0:T(2,128)}, u32[]{:S(2)}) copy-start(s32[1,2,2,12,3]{3,2,4,1,0:T(2,128)} %param.12) | copy-start | bytes 1732
  6.5 2.4 %copy-start.11 = (s32[1,2,2,9]{3,2,1,0:T(2,128)S(1)}, s32[1,2,2,9]{3,2,1,0:T(2,128)}, u32[]{:S(2)}) copy-start(s32[1,2,2,9]{3,2,1,0:T(2,128)} %param.11) | copy-start | bytes 436
  7.5 73.2 %collective-permute-start.1 = (bf16[2,128,1536]{2,1,0:T(8,128)(2,1)}, bf16[2,128,1536]{2,1,0:T(8,128)(2,1)S(1)}, u32[]{:S(2)}, u32[]{:S(2)}) collective-permute-start(bf16[2,128,1536]{2,1,0:T(8,128)(2,1)} %pad_maximum_fusion.1), channel_id=1, source_target_pairs={{4,0},{8,4},{12,8},{5,1},{9,5},{13,9},{6,2},{10,6},{14,10},{7,3},{... | collective-permute-start | bytes 2359304 | tf_op jit(solution)/shard_map/ppermute | solution.py:219
  9.7 12.1 %copy-start = (bf16[1,16,16,1536]{3,2,1,0:T(8,128)(2,1)S(1)}, bf16[1,16,16,1536]{3,2,1,0:T(8,128)(2,1)}, u32[]{:S(2)}) copy-start(bf16[1,16,16,1536]{3,2,1,0:T(8,128)(2,1)} %param.9) | copy-start | bytes 2359300
  12.1 18.2 %all-to-all-start = ((f32[16,16,128]{2,1,0:T(8,128)}), f32[16,16,128]{2,1,0:T(8,128)}, u32[]{:S(2)}, u32[]{:S(2)}) async-start(f32[16,16,128]{2,1,0:T(8,128)} %pool.1), calls=%async_computation | async-start | bytes 262144 | tf_op jit(solution)/shard_map/all_to_all | solution.py:260
  30.2 7.5 %copy-start.5 = (bf16[1,128,1536]{2,1,0:T(8,128)(2,1)S(1)}, bf16[1,128,1536]{2,1,0:T(8,128)(2,1)}, u32[]{:S(2)}) copy-start(bf16[1,128,1536]{2,1,0:T(8,128)(2,1)} %get-tuple-element.10) | copy-start | bytes 1179652
  32.9 9.5 %all-to-all-start.1 = ((f32[8,16,128]{2,1,0:T(8,128)}), f32[8,16,128]{2,1,0:T(8,128)}, u32[]{:S(2)}, u32[]{:S(2)}) async-start(f32[8,16,128]{2,1,0:T(8,128)} %bitcast.68), calls=%async_computation.1 | async-start | bytes 131072 | tf_op jit(solution)/shard_map/all_to_all | solution.py:260
  37.8 20.7 %copy-start.6 = (bf16[1,128,1536]{2,1,0:T(8,128)(2,1)S(1)}, bf16[1,128,1536]{2,1,0:T(8,128)(2,1)}, u32[]{:S(2)}) copy-start(bf16[1,128,1536]{2,1,0:T(8,128)(2,1)} %get-tuple-element.11) | copy-start | bytes 1179652
  38.7 49.2 %collective-permute-start.2 = (bf16[2,128,1536]{2,1,0:T(8,128)(2,1)}, bf16[2,128,1536]{2,1,0:T(8,128)(2,1)S(1)}, u32[]{:S(2)}, u32[]{:S(2)}) collective-permute-start(bf16[2,128,1536]{2,1,0:T(8,128)(2,1)} %pad_maximum_fusion.2), channel_id=1, source_target_pairs={{0,1},{1,2},{2,3},{4,5},{5,6},{6,7},{8,9},{9,10},{10,11},{12,13},{... | collective-permute-start | bytes 2359304 | tf_op jit(solution)/shard_map/ppermute | solution.py:219
  44.0 30.4 %all-to-all-start.2 = ((f32[4,16,128]{2,1,0:T(8,128)}), f32[4,16,128]{2,1,0:T(8,128)S(1)}, u32[]{:S(2)}, u32[]{:S(2)}) async-start(f32[4,16,128]{2,1,0:T(8,128)} %broadcast_in_dim.9), calls=%async_computation.2 | async-start | bytes 65536 | tf_op jit(solution)/shard_map/all_to_all | solution.py:260
  59.4 28.6 %collective-permute-start.3 = (bf16[2,128,1536]{2,1,0:T(8,128)(2,1)}, bf16[2,128,1536]{2,1,0:T(8,128)(2,1)}, u32[]{:S(2)}, u32[]{:S(2)}) collective-permute-start(bf16[2,128,1536]{2,1,0:T(8,128)(2,1)} %pad_maximum_fusion.3), channel_id=1, source_target_pairs={{1,0},{2,1},{3,2},{5,4},{6,5},{7,6},{9,8},{10,9},{11,10},{13,12},{... | collective-permute-start | bytes 2359304 | tf_op jit(solution)/shard_map/ppermute | solution.py:219
  75.0 20.3 %all-to-all-start.3 = ((bf16[16,16,128]{2,1,0:T(8,128)(2,1)}), bf16[16,16,128]{2,1,0:T(8,128)(2,1)}, u32[]{:S(2)}, u32[]{:S(2)}) async-start(bf16[16,16,128]{2,1,0:T(8,128)(2,1)} %broadcast_in_dim.10), calls=%async_computation.3 | async-start | bytes 131072 | tf_op jit(solution)/shard_map/all_to_all | solution.py:260
  79.8 0.9 copy-start.2
  80.7 1.3 %copy-start.3 = (bf16[2,128,1536]{2,1,0:T(8,128)(2,1)}, bf16[2,128,1536]{2,1,0:T(8,128)(2,1)S(1)}, u32[]{:S(2)}) copy-start(bf16[2,128,1536]{2,1,0:T(8,128)(2,1)S(1)} %collective-permute-done.1.rest_1_) | copy-start | bytes 2359300
  80.7 1.3 %slice-start = ((bf16[2,128,1536]{2,1,0:T(8,128)(2,1)}), bf16[1,128,1536]{2,1,0:T(8,128)(2,1)S(1)}, s32[]{:S(2)}) async-start(bf16[2,128,1536]{2,1,0:T(8,128)(2,1)} %copy-done.2), calls=%async_computation.5 | async-start | bytes 786432 | tf_op jit(solution)/shard_map/slice | solution.py:243
  82.0 19.7 %collective-permute-start.5 = (bf16[128,1536]{1,0:T(8,128)(2,1)S(1)}, bf16[128,1536]{1,0:T(8,128)(2,1)S(1)}, u32[]{:S(2)}, u32[]{:S(2)}) collective-permute-start(bf16[128,1536]{1,0:T(8,128)(2,1)S(1)} %pad_maximum_fusion.5), channel_id=1, source_target_pairs={{1,0},{2,1},{3,2},{5,4},{6,5},{7,6},{9,8},{10,9},{11,10},{13,12},{... | collective-permute-start | bytes 1179656 | tf_op jit(solution)/shard_map/ppermute | solution.py:219
  83.4 18.4 %collective-permute-start.4 = (bf16[128,1536]{1,0:T(8,128)(2,1)S(1)}, bf16[128,1536]{1,0:T(8,128)(2,1)S(1)}, u32[]{:S(2)}, u32[]{:S(2)}) collective-permute-start(bf16[128,1536]{1,0:T(8,128)(2,1)S(1)} %pad_maximum_fusion.4), channel_id=1, source_target_pairs={{0,1},{1,2},{2,3},{4,5},{5,6},{6,7},{8,9},{9,10},{10,11},{12,13},{... | collective-permute-start | bytes 1179656 | tf_op jit(solution)/shard_map/ppermute | solution.py:219
  88.0 1.4 %copy-start.4 = (bf16[2,128,1536]{2,1,0:T(8,128)(2,1)}, bf16[2,128,1536]{2,1,0:T(8,128)(2,1)S(1)}, u32[]{:S(2)}) copy-start(bf16[2,128,1536]{2,1,0:T(8,128)(2,1)S(1)} %collective-permute-done.2.rest_2_) | copy-start | bytes 2359300
  89.4 12.4 %collective-permute-start.6 = (bf16[128,1536]{1,0:T(8,128)(2,1)S(1)}, bf16[128,1536]{1,0:T(8,128)(2,1)S(1)}, u32[]{:S(2)}, u32[]{:S(2)}) collective-permute-start(bf16[128,1536]{1,0:T(8,128)(2,1)S(1)} %pad_maximum_fusion.6), channel_id=1, source_target_pairs={{0,4},{4,8},{8,12},{1,5},{5,9},{9,13},{2,6},{6,10},{10,14},{3,7},{... | collective-permute-start | bytes 1179656 | tf_op jit(solution)/shard_map/ppermute | solution.py:219
  93.9 10.5 %collective-permute-start.7 = (bf16[128,1536]{1,0:T(8,128)(2,1)}, bf16[128,1536]{1,0:T(8,128)(2,1)S(1)}, u32[]{:S(2)}, u32[]{:S(2)}) collective-permute-start(bf16[128,1536]{1,0:T(8,128)(2,1)} %pad_maximum_fusion.7), channel_id=1, source_target_pairs={{4,0},{8,4},{12,8},{5,1},{9,5},{13,9},{6,2},{10,6},{14,10},{7,3},{... | collective-permute-start | bytes 1179656 | tf_op jit(solution)/shard_map/ppermute | solution.py:219
  96.9 19.3 %all-to-all-start.4 = ((bf16[8,16,16,128]{3,2,1,0:T(8,128)(2,1)}), bf16[8,16,16,128]{3,2,1,0:T(8,128)(2,1)S(1)}, u32[]{:S(2)}, u32[]{:S(2)}) async-start(bf16[8,16,16,128]{3,2,1,0:T(8,128)(2,1)} %broadcast_in_dim.11), calls=%async_computation.4 | async-start | bytes 1048576 | tf_op jit(solution)/shard_map/all_to_all | solution.py:260
  101.8 2.7 %copy-start.7 = (bf16[128,1536]{1,0:T(8,128)(2,1)}, bf16[128,1536]{1,0:T(8,128)(2,1)S(1)}, u32[]{:S(2)}) copy-start(bf16[128,1536]{1,0:T(8,128)(2,1)S(1)} %collective-permute-done.5.rest_5_) | copy-start | bytes 1179652
  101.8 2.7 %copy-start.8 = (bf16[128,1536]{1,0:T(8,128)(2,1)}, bf16[128,1536]{1,0:T(8,128)(2,1)S(1)}, u32[]{:S(2)}) copy-start(bf16[128,1536]{1,0:T(8,128)(2,1)S(1)} %collective-permute-done.4.rest_4_) | copy-start | bytes 1179652
  101.8 2.7 %copy-start.9 = (bf16[128,1536]{1,0:T(8,128)(2,1)}, bf16[128,1536]{1,0:T(8,128)(2,1)S(1)}, u32[]{:S(2)}) copy-start(bf16[128,1536]{1,0:T(8,128)(2,1)S(1)} %collective-permute-done.6.rest_6_) | copy-start | bytes 1179652
  104.5 0.7 copy-start.10

commit v3 on v2

--- a/solution.py
+++ b/solution.py
@@ -22,6 +22,8 @@
 EDGE = BS * TILE
 NKEY = TOK + 6 * EDGE
 SLOTS = 16
+AIM_LANE = 16
+CUT = 512
 HSTEP = 2
 LIVE_CAP = 3.4e38
 DEAD_CAP = -1e30
@@ -46,7 +48,7 @@
     return ids
 
 
-def pool_kernel(q_ref, k_ref, aux_ref, out_ref):
+def pool_kernel(pat_ref, aim_ref, q_ref, k_ref, out_ref, aux_ref):
     row = lax.broadcasted_iota(jnp.int32, (8, TOK), 0)
     tok = lax.broadcasted_iota(jnp.int32, (8, TOK), 1)
     block = tok // TILE // BS * 2 + tok % TILE // BS
@@ -55,19 +57,80 @@
     sums = jnp.dot(pick_q, q_ref[...], preferred_element_type=jnp.float32)
     sums += jnp.dot(pick_k, k_ref[...], preferred_element_type=jnp.float32)
     means = sums / (BS * BS)
+    aux_ref[...] = jnp.zeros((8, DH), jnp.float32)
+    for y in range(2):
+        aux_ref[2 * y : 2 * y + 2, 0:NOFF] = pat_ref[y].astype(jnp.float32)
+        for k in range(TOPK):
+            at = AIM_LANE * (k + 1)
+            aux_ref[2 * y : 2 * y + 2, at : at + HEADS] = aim_ref[y, k].astype(jnp.float32)
+    aux = aux_ref[...]
     for h in range(HEADS):
         out_ref[h, 0:8, :] = means[:, h * DH : (h + 1) * DH]
-        out_ref[h, 8:16, :] = aux_ref[h]
+        out_ref[h, 8:16, :] = aux
     for h in range(HEADS, SLOTS):
         out_ref[h] = jnp.zeros((16, DH), jnp.float32)
 
 
-def pool(query, key, aux):
+def pool(pattern, aims, query, key):
     return pl.pallas_call(
         pool_kernel,
         out_shape=jax.ShapeDtypeStruct((SLOTS, 16, DH), jnp.float32),
+        scratch_shapes=[pltpu.VMEM((8, DH), jnp.float32)],
         name="pool",
-    )(query, key, aux)
+    )(pattern, aims, query, key)
+
+
+def rim_kernel(k_ref, v_ref, low_ref, high_ref, right_ref, left_ref):
+    for i, ref in enumerate((k_ref, v_ref)):
+        wide = ref[...].astype(jnp.float32)
+        lanes = wide.shape[-1]
+
+        def flat(x):
+            return x.reshape(EDGE, lanes).astype(jnp.bfloat16)
+
+        low_ref[i] = flat(wide[TILE - BS :])
+        high_ref[i] = flat(wide[:BS])
+        right_ref[i] = flat(wide[:, TILE - BS :])
+        left_ref[i] = flat(wide[:, :BS])
+
+
+def rims_of(key, value):
+    tile = pl.BlockSpec((TILE, TILE, CUT), lambda i: (0, 0, i))
+    return pl.pallas_call(
+        rim_kernel,
+        out_shape=[jax.ShapeDtypeStruct((2, EDGE, FEAT), jnp.bfloat16)] * 4,
+        grid=(FEAT // CUT,),
+        in_specs=[tile, tile],
+        out_specs=[pl.BlockSpec((2, EDGE, CUT), lambda i: (0, 0, i))] * 4,
+        name="rims",
+    )(key, value)
+
+
+def corner_kernel(a_ref, b_ref, l_ref, r_ref, right_ref, left_ref, low_ref, high_ref):
+    lanes = a_ref.shape[-1]
+    cell = BS * BS
+    for i, ref in enumerate((a_ref, b_ref)):
+        wide = ref[0].astype(jnp.float32).reshape(BS, TILE, lanes)
+        at = slice(i * cell, (i + 1) * cell)
+        right_ref[at] = wide[:, TILE - BS :].reshape(cell, lanes).astype(jnp.bfloat16)
+        left_ref[at] = wide[:, :BS].reshape(cell, lanes).astype(jnp.bfloat16)
+    for i, ref in enumerate((l_ref, r_ref)):
+        at = slice(i * cell, (i + 1) * cell)
+        low_ref[at] = ref[0, cell:]
+        high_ref[at] = ref[0, :cell]
+
+
+def corner_parts(above, below, left, right):
+    key_side = pl.BlockSpec((1, EDGE, CUT), lambda i: (0, 0, i))
+    value_side = pl.BlockSpec((1, EDGE, CUT), lambda i: (1, 0, i))
+    return pl.pallas_call(
+        corner_kernel,
+        out_shape=[jax.ShapeDtypeStruct((EDGE, FEAT), jnp.bfloat16)] * 4,
+        grid=(FEAT // CUT,),
+        in_specs=[key_side, key_side, value_side, value_side],
+        out_specs=[pl.BlockSpec((EDGE, CUT), lambda i: (0, i))] * 4,
+        name="corners",
+    )(above, below, left, right)
 
 
 def router_kernel(normal, head_ref, recv_ref, wq_ref, wk_ref, out_ref, pq_ref, pk_ref, ax_ref):
@@ -98,8 +161,10 @@
     for o in range(NOFF):
         live = jnp.where(off == float(o), aux[:, o : o + 1], live)
     picks = jnp.zeros((n, n), jnp.float32)
+    lane = lax.broadcasted_iota(jnp.int32, (n, DH), 1)
     for k in range(TOPK):
-        picks += (off == aux[:, NOFF + k : NOFF + k + 1]).astype(jnp.float32)
+        mine = jnp.where(lane == AIM_LANE * (k + 1) + head_ref[0], aux, 0.0)
+        picks += (off == jnp.sum(mine, axis=1, keepdims=True)).astype(jnp.float32)
     logits = jnp.where(live > 0.5, logits, -1e30)
     top = jnp.max(logits, axis=1, keepdims=True)
     weights = jnp.exp(logits - top)
@@ -219,18 +284,6 @@
     return lax.ppermute(x, axis, pairs)
 
 
-def edges(key, value):
-    def flat(cut):
-        return jnp.stack([cut(x).reshape(EDGE, FEAT) for x in (key, value)])
-
-    return (
-        flat(lambda x: x[TILE - BS :]),
-        flat(lambda x: x[:BS]),
-        flat(lambda x: x[:, TILE - BS :]),
-        flat(lambda x: x[:, :BS]),
-    )
-
-
 def sides_of(low, high, right, left):
     return (
         shift(low, "py", 1), shift(high, "py", -1), shift(right, "px", 1), shift(left, "px", -1)
@@ -238,21 +291,12 @@
 
 
 def corners_of(above, below, left, right):
-    def columns(lo):
-        cuts = [
-            x[0].reshape(BS, TILE, FEAT)[:, lo : lo + BS].reshape(BS * BS, FEAT)
-            for x in (above, below)
-        ]
-        return jnp.concatenate(cuts, axis=0)
-
-    def rows(lo):
-        return jnp.concatenate([x[1, lo * BS : lo * BS + BS * BS] for x in (left, right)], axis=0)
-
+    to_right, to_left, to_low, to_high = corner_parts(above, below, left, right)
     return (
-        shift(columns(TILE - BS), "px", 1),
-        shift(columns(0), "px", -1),
-        shift(rows(TILE - BS), "py", 1),
-        shift(rows(0), "py", -1),
+        shift(to_right, "px", 1),
+        shift(to_left, "px", -1),
+        shift(to_low, "py", 1),
+        shift(to_high, "py", -1),
     )
 
 
@@ -269,15 +313,10 @@
     tiles = tiles_y * tiles_x
     normal = float(TOPK * HEADS * 4 * tiles)
     query, key, value = (x[0].reshape(TOK, FEAT) for x in (queries, keys, values))
-    pat = pattern.reshape(4, NOFF)
-    aim = targets.reshape(4, HEADS, TOPK).transpose(1, 0, 2)
-    aux = jnp.concatenate([jnp.broadcast_to(pat, (HEADS, 4, NOFF)), aim], axis=2)
-    aux = jnp.pad(aux.astype(jnp.float32), ((0, 0), (0, 4), (0, DH - NOFF - TOPK)))
-
-    sent = pool(query, key, aux)
+    aims = targets[0].transpose(0, 3, 1, 2)
+    sent = pool(pattern[0], aims, query, key)
     recv = exchange(sent, TILES)
-    rims = edges(keys[0], values[0])
-    sides = sides_of(*rims)
+    sides = sides_of(*rims_of(keys[0], values[0]))
     me = lax.axis_index("py") * tiles_x + lax.axis_index("px")
     head = jnp.minimum(me, HEADS - 1).astype(jnp.int32).reshape(1)
     grads = router_grads(
@@ -294,7 +333,7 @@
     every = every.transpose(1, 0, 2, 3).reshape(HEADS, 2 * RW, DH)
     grad_q, grad_k = (x.swapaxes(1, 2) for x in (every[:, :RW], every[:, RW:]))
     corners = corners_of(*sides)
-    attended = attend(pat, query, key, value, sides, corners)
+    attended = attend(pattern.reshape(4, NOFF), query, key, value, sides, corners)
     return (attended.reshape(1, TILE, TILE, FEAT), grad_q, grad_k)
 
 

time: 118 us -> 112 us (0.949)
  the two profiles are of different devices: /device:TPU:2 before, /device:TPU:32 now
where the time goes in v3:
time: 112 us; the launch traced here: 111 us
  starting transfers between devices  42 us (38%)
  blocking collectives  34.6 us (31%)
  Pallas kernels  23.1 us (21%)
  local copies, waits for them, and re-layouts  6.12 us (5%)
  waiting for transfers between devices  4.33 us (4%)
    all_to_all x2, blocking collectives, exchange(): return lax.all_to_all(x, axis, 0, 0)  34.6 us
    ppermute x8, starting transfers between devices, shift(): return lax.ppermute(x, axis, pairs)  21.1 us
    all_to_all x3, starting transfers between devices, exchange(): return lax.all_to_all(x, axis, 0, 0)  20.9 us
    pallas_call x1, Pallas kernels, attend(): pl.pallas_call(attend_kernel, out_shape=jax.ShapeDtypeStruct((TOK, FEAT),...  11 us
    ppermute x8, waiting for transfers between devices, shift(): return lax.ppermute(x, axis, pairs)  4.32 us
    unnamed x18, local copies, waits for them, and re-layouts  3.68 us
    pallas_call x1, Pallas kernels, rims_of(): pl.pallas_call(rim_kernel, out_shape=[jax.ShapeDtypeStruct((2, EDGE, FEAT...  3.62 us
    pallas_call x1, Pallas kernels, corner_parts(): pl.pallas_call(corner_kernel, out_shape=[jax.ShapeDtypeStruct((EDGE, FEAT...  3.41 us
  transfers between devices with their start and end apart: 11, of which 2 were waited for; matrix products, arithmetic and copies ran while one was open for 1% of the time, Pallas kernels for 19%

profile of v3, /device:TPU:32, one launch (start us, length us, event | category | flops | bytes accessed | tf_op | source)
XLA Modules:
  0.0 111.1 jit_solution(787486948423016077)
XLA Ops:
  0.6 2.4 %pool.1 = f32[16,16,128]{2,1,0:T(8,128)} custom-call(s32[2,2,9]{2,1,0:T(2,128)} %bitcast.34, s32[2,3,2,12]{3,2,1,0:T(2,128)} %bitcast.36, bf16[256,1536]{1,0:T(8,128)(2,1)} %bitcast.27, bf16[256,1536]{1,0:T(8,128)(2,1)} %bitcast.22), custom_call_target="tpu_custom_call" | custom-call | tf_op jit(solution)/shard_map/pool/pallas_call | solution.py:75
  3.0 8.8 %all-to-all-start = ((f32[16,16,128]{2,1,0:T(8,128)}), f32[16,16,128]{2,1,0:T(8,128)S(1)}, u32[]{:S(2)}, u32[]{:S(2)}) async-start(f32[16,16,128]{2,1,0:T(8,128)} %pool.1), calls=%async_computation | async-start | bytes 262144 | tf_op jit(solution)/shard_map/all_to_all | solution.py:304
  11.8 3.6 %rims.1 = (bf16[2,128,1536]{2,1,0:T(8,128)(2,1)}, bf16[2,128,1536]{2,1,0:T(8,128)(2,1)}, bf16[2,128,1536]{2,1,0:T(8,128)(2,1)}, bf16[2,128,1536]{2,1,0:T(8,128)(2,1)}) custom-call(bf16[16,16,1536]{2,1,0:T(8,128)(2,1)} %bitcast.23, bf16[16,16,1536]{2,1,0:T(8,128)(2,1)} %bitcast.25), custom_call_target="tpu_custom_call" | custom-call | tf_op jit(solution)/shard_map/rims/pallas_call | solution.py:99
  15.4 3.4 %collective-permute-start = (bf16[2,128,1536]{2,1,0:T(8,128)(2,1)}, bf16[2,128,1536]{2,1,0:T(8,128)(2,1)S(1)}, u32[]{:S(2)}, u32[]{:S(2)}) collective-permute-start(bf16[2,128,1536]{2,1,0:T(8,128)(2,1)} %get-tuple-element.11), channel_id=1, source_target_pairs={{0,4},{4,8},{8,12},{1,5},{5,9},{9,13},{2,6},{6,10},{10,14},{3,7},{... | collective-permute-start | bytes 2359304 | tf_op jit(solution)/shard_map/ppermute | solution.py:284
  18.8 1.3 %collective-permute-start.1 = (bf16[2,128,1536]{2,1,0:T(8,128)(2,1)}, bf16[2,128,1536]{2,1,0:T(8,128)(2,1)S(1)}, u32[]{:S(2)}, u32[]{:S(2)}) collective-permute-start(bf16[2,128,1536]{2,1,0:T(8,128)(2,1)} %get-tuple-element.12), channel_id=1, source_target_pairs={{4,0},{8,4},{12,8},{5,1},{9,5},{13,9},{6,2},{10,6},{14,10},{7,3},{... | collective-permute-start | bytes 2359304 | tf_op jit(solution)/shard_map/ppermute | solution.py:284
  20.1 3.4 %collective-permute-start.2 = (bf16[2,128,1536]{2,1,0:T(8,128)(2,1)}, bf16[2,128,1536]{2,1,0:T(8,128)(2,1)S(1)}, u32[]{:S(2)}, u32[]{:S(2)}) collective-permute-start(bf16[2,128,1536]{2,1,0:T(8,128)(2,1)} %get-tuple-element.13), channel_id=1, source_target_pairs={{0,1},{1,2},{2,3},{4,5},{5,6},{6,7},{8,9},{9,10},{10,11},{12,13},{... | collective-permute-start | bytes 2359304 | tf_op jit(solution)/shard_map/ppermute | solution.py:284
  23.5 2.5 %collective-permute-start.3 = (bf16[2,128,1536]{2,1,0:T(8,128)(2,1)}, bf16[2,128,1536]{2,1,0:T(8,128)(2,1)S(1)}, u32[]{:S(2)}, u32[]{:S(2)}) collective-permute-start(bf16[2,128,1536]{2,1,0:T(8,128)(2,1)} %get-tuple-element.14), channel_id=1, source_target_pairs={{1,0},{2,1},{3,2},{5,4},{6,5},{7,6},{9,8},{10,9},{11,10},{13,12},{... | collective-permute-start | bytes 2359304 | tf_op jit(solution)/shard_map/ppermute | solution.py:284
  26.0 0.0 all-to-all-done.recv_ref
  26.0 0.0 copy-start.4
  26.1 0.6 copy-done.4
  26.7 2.7 %router.1 = f32[128,128]{1,0:T(8,128)} custom-call(s32[1]{0:T(128)} %bitcast.7.head_ref, f32[16,16,128]{2,1,0:T(8,128)} %copy-done.4, f32[12,64,128]{2,1,0:T(8,128)} %bitcast.31, f32[12,64,128]{2,1,0:T(8,128)} %bitcast.32), custom_call_target="tpu_custom_call" | custom-call | tf_op jit(solution)/shard_map/router/pallas_call | solution.py:180
  29.4 9.8 %all_to_all.25 = f32[8,16,128]{2,1,0:T(8,128)S(1)} all-to-all(f32[8,16,128]{2,1,0:T(8,128)} %bitcast.33), channel_id=1, replica_groups=mesh['x'=4,'far'=4,'core'=2,'py'=4,'px'=4] {'x','core'}, dimensions={0} | all-to-all | bytes 131072 | tf_op jit(solution)/shard_map/all_to_all | solution.py:304
  39.2 24.9 %all_to_all.26 = f32[4,16,128]{2,1,0:T(8,128)S(1)} all-to-all(f32[4,16,128]{2,1,0:T(8,128)S(1)} %broadcast_in_dim.6), channel_id=1, replica_groups=mesh['x'=4,'far'=4,'core'=2,'py'=4,'px'=4] {'far'}, dimensions={0} | all-to-all | bytes 65536 | tf_op jit(solution)/shard_map/all_to_all | solution.py:304
  64.0 0.6 broadcast_in_dim.7
  64.7 8.7 %all-to-all-start.3 = ((bf16[16,16,128]{2,1,0:T(8,128)(2,1)}), bf16[16,16,128]{2,1,0:T(8,128)(2,1)S(1)}, u32[]{:S(2)}, u32[]{:S(2)}) async-start(bf16[16,16,128]{2,1,0:T(8,128)(2,1)} %broadcast_in_dim.7), calls=%async_computation.3 | async-start | bytes 131072 | tf_op jit(solution)/shard_map/all_to_all | solution.py:304
  73.3 0.0 collective-permute-done.a_ref.rest_0_
  73.3 0.0 copy-start
  73.4 0.0 collective-permute-done.1.b_ref.rest_1_
  73.4 0.0 copy-start.1
  73.4 0.0 collective-permute-done.2.l_ref.rest_2_
  73.4 0.0 copy-start.2
  73.4 0.0 collective-permute-done.3.r_ref.rest_3_
  73.4 0.8 copy-done
  74.2 0.3 copy-done.1
  74.5 0.2 copy-done.2
  74.8 0.0 copy-start.3
  74.8 0.9 copy-done.3
  75.7 3.4 %corners.1 = (bf16[128,1536]{1,0:T(8,128)(2,1)}, bf16[128,1536]{1,0:T(8,128)(2,1)}, bf16[128,1536]{1,0:T(8,128)(2,1)}, bf16[128,1536]{1,0:T(8,128)(2,1)}) custom-call(bf16[2,128,1536]{2,1,0:T(8,128)(2,1)} %copy-done, bf16[2,128,1536]{2,1,0:T(8,128)(2,1)} %copy-done.1, bf16[2,128,1536]{2,1,0:T(8,128)(2,1)} %copy-done.2, bf16[2,128,1536]{2,1,0:T(8,128)(2,1)} %copy-done.3), custom_call_target="tpu_custom_call" | custom-call | tf_op jit(solution)/shard_map/corners/pallas_call | solution.py:126
  79.1 3.4 %collective-permute-start.4 = (bf16[128,1536]{1,0:T(8,128)(2,1)}, bf16[128,1536]{1,0:T(8,128)(2,1)S(1)}, u32[]{:S(2)}, u32[]{:S(2)}) collective-permute-start(bf16[128,1536]{1,0:T(8,128)(2,1)} %get-tuple-element.15), channel_id=1, source_target_pairs={{0,1},{1,2},{2,3},{4,5},{5,6},{6,7},{8,9},{9,10},{10,11},{12,13},{... | collective-permute-start | bytes 1179656 | tf_op jit(solution)/shard_map/ppermute | solution.py:284
  82.4 2.5 %collective-permute-start.5 = (bf16[128,1536]{1,0:T(8,128)(2,1)}, bf16[128,1536]{1,0:T(8,128)(2,1)S(1)}, u32[]{:S(2)}, u32[]{:S(2)}) collective-permute-start(bf16[128,1536]{1,0:T(8,128)(2,1)} %get-tuple-element.16), channel_id=1, source_target_pairs={{1,0},{2,1},{3,2},{5,4},{6,5},{7,6},{9,8},{10,9},{11,10},{13,12},{... | collective-permute-start | bytes 1179656 | tf_op jit(solution)/shard_map/ppermute | solution.py:284
  84.9 3.4 %collective-permute-start.6 = (bf16[128,1536]{1,0:T(8,128)(2,1)}, bf16[128,1536]{1,0:T(8,128)(2,1)S(1)}, u32[]{:S(2)}, u32[]{:S(2)}) collective-permute-start(bf16[128,1536]{1,0:T(8,128)(2,1)} %get-tuple-element.17), channel_id=1, source_target_pairs={{0,4},{4,8},{8,12},{1,5},{5,9},{9,13},{2,6},{6,10},{10,14},{3,7},{... | collective-permute-start | bytes 1179656 | tf_op jit(solution)/shard_map/ppermute | solution.py:284
  88.3 1.3 %collective-permute-start.7 = (bf16[128,1536]{1,0:T(8,128)(2,1)}, bf16[128,1536]{1,0:T(8,128)(2,1)S(1)}, u32[]{:S(2)}, u32[]{:S(2)}) collective-permute-start(bf16[128,1536]{1,0:T(8,128)(2,1)} %get-tuple-element.18), channel_id=1, source_target_pairs={{4,0},{8,4},{12,8},{5,1},{9,5},{13,9},{6,2},{10,6},{14,10},{7,3},{... | collective-permute-start | bytes 1179656 | tf_op jit(solution)/shard_map/ppermute | solution.py:284
  89.6 0.0 all-to-all-done.3
  89.6 0.9 broadcast_in_dim.8
  90.5 3.5 %all-to-all-start.4 = ((bf16[8,16,16,128]{3,2,1,0:T(8,128)(2,1)}), bf16[8,16,16,128]{3,2,1,0:T(8,128)(2,1)S(1)}, u32[]{:S(2)}, u32[]{:S(2)}) async-start(bf16[8,16,16,128]{3,2,1,0:T(8,128)(2,1)} %broadcast_in_dim.8), calls=%async_computation.4 | async-start | bytes 1048576 | tf_op jit(solution)/shard_map/all_to_all | solution.py:304
  94.0 0.0 collective-permute-done.4.rest_4_
  94.0 0.0 copy-start.5
  94.0 0.0 collective-permute-done.5.rest_5_
  94.0 0.0 copy-start.6
  94.0 0.3 collective-permute-done.6.rest_6_
  94.3 0.0 copy-start.7
  94.3 4.0 %collective-permute-done.7.rest_7_ = bf16[128,1536]{1,0:T(8,128)(2,1)S(1)} collective-permute-done((bf16[128,1536]{1,0:T(8,128)(2,1)}, bf16[128,1536]{1,0:T(8,128)(2,1)S(1)}, u32[]{:S(2)}, u32[]{:S(2)}) %collective-permute-start.7) | collective-permute-done | bytes 393248 | tf_op jit(solution)/shard_map/ppermute | solution.py:284
  98.4 0.0 copy-start.8
  98.4 0.0 copy-done.5
  98.4 0.0 copy-done.6
  98.4 0.0 copy-done.7
  98.4 0.8 copy-done.8
  99.1 11.0 %attend.1 = bf16[256,1536]{1,0:T(8,128)(2,1)} custom-call(s32[4,9]{1,0:T(4,128)} %bitcast.35, s32[8,1024]{1,0:T(8,128)} %constant.15.clone.ids_ref, bf16[256,1536]{1,0:T(8,128)(2,1)} %bitcast.28, bf16[256,1536]{1,0:T(8,128)(2,1)} %bitcast.24, bf16[256,1536]{1,0:T(8,128)(2,1)} %bitcast.26, bf16[2,128,1536]{2,1,0:T(8,128)(2,1)} %copy-done, ...), custom_call_target="tpu_custom_call" | custom-call | flops 1610612736 | bytes 7864320 | tf_op jit(solution)/shard_map/attend/pallas_call | solution.py:254
  110.1 0.0 all-to-all-done.4
  110.1 0.1 copy_convert_fusion
  110.2 0.9 slice_bitcast_fusion
  (3 shorter events, 0.0 us)
Async XLA Ops:
  3.0 23.0 %all-to-all-start = ((f32[16,16,128]{2,1,0:T(8,128)}), f32[16,16,128]{2,1,0:T(8,128)S(1)}, u32[]{:S(2)}, u32[]{:S(2)}) async-start(f32[16,16,128]{2,1,0:T(8,128)} %pool.1), calls=%async_computation | async-start | bytes 262144 | tf_op jit(solution)/shard_map/all_to_all | solution.py:304
  15.4 58.0 %collective-permute-start = (bf16[2,128,1536]{2,1,0:T(8,128)(2,1)}, bf16[2,128,1536]{2,1,0:T(8,128)(2,1)S(1)}, u32[]{:S(2)}, u32[]{:S(2)}) collective-permute-start(bf16[2,128,1536]{2,1,0:T(8,128)(2,1)} %get-tuple-element.11), channel_id=1, source_target_pairs={{0,4},{4,8},{8,12},{1,5},{5,9},{9,13},{2,6},{6,10},{10,14},{3,7},{... | collective-permute-start | bytes 2359304 | tf_op jit(solution)/shard_map/ppermute | solution.py:284
  18.8 54.5 %collective-permute-start.1 = (bf16[2,128,1536]{2,1,0:T(8,128)(2,1)}, bf16[2,128,1536]{2,1,0:T(8,128)(2,1)S(1)}, u32[]{:S(2)}, u32[]{:S(2)}) collective-permute-start(bf16[2,128,1536]{2,1,0:T(8,128)(2,1)} %get-tuple-element.12), channel_id=1, source_target_pairs={{4,0},{8,4},{12,8},{5,1},{9,5},{13,9},{6,2},{10,6},{14,10},{7,3},{... | collective-permute-start | bytes 2359304 | tf_op jit(solution)/shard_map/ppermute | solution.py:284
  20.1 53.3 %collective-permute-start.2 = (bf16[2,128,1536]{2,1,0:T(8,128)(2,1)}, bf16[2,128,1536]{2,1,0:T(8,128)(2,1)S(1)}, u32[]{:S(2)}, u32[]{:S(2)}) collective-permute-start(bf16[2,128,1536]{2,1,0:T(8,128)(2,1)} %get-tuple-element.13), channel_id=1, source_target_pairs={{0,1},{1,2},{2,3},{4,5},{5,6},{6,7},{8,9},{9,10},{10,11},{12,13},{... | collective-permute-start | bytes 2359304 | tf_op jit(solution)/shard_map/ppermute | solution.py:284
  23.5 49.9 %collective-permute-start.3 = (bf16[2,128,1536]{2,1,0:T(8,128)(2,1)}, bf16[2,128,1536]{2,1,0:T(8,128)(2,1)S(1)}, u32[]{:S(2)}, u32[]{:S(2)}) collective-permute-start(bf16[2,128,1536]{2,1,0:T(8,128)(2,1)} %get-tuple-element.14), channel_id=1, source_target_pairs={{1,0},{2,1},{3,2},{5,4},{6,5},{7,6},{9,8},{10,9},{11,10},{13,12},{... | collective-permute-start | bytes 2359304 | tf_op jit(solution)/shard_map/ppermute | solution.py:284
  26.0 0.7 copy-start.4
  64.7 24.9 %all-to-all-start.3 = ((bf16[16,16,128]{2,1,0:T(8,128)(2,1)}), bf16[16,16,128]{2,1,0:T(8,128)(2,1)S(1)}, u32[]{:S(2)}, u32[]{:S(2)}) async-start(bf16[16,16,128]{2,1,0:T(8,128)(2,1)} %broadcast_in_dim.7), calls=%async_computation.3 | async-start | bytes 131072 | tf_op jit(solution)/shard_map/all_to_all | solution.py:304
  73.3 0.9 copy-start
  73.4 1.2 %copy-start.1 = (bf16[2,128,1536]{2,1,0:T(8,128)(2,1)}, bf16[2,128,1536]{2,1,0:T(8,128)(2,1)S(1)}, u32[]{:S(2)}) copy-start(bf16[2,128,1536]{2,1,0:T(8,128)(2,1)S(1)} %collective-permute-done.1.b_ref.rest_1_) | copy-start | bytes 2359300
  73.4 1.4 %copy-start.2 = (bf16[2,128,1536]{2,1,0:T(8,128)(2,1)}, bf16[2,128,1536]{2,1,0:T(8,128)(2,1)S(1)}, u32[]{:S(2)}) copy-start(bf16[2,128,1536]{2,1,0:T(8,128)(2,1)S(1)} %collective-permute-done.2.l_ref.rest_2_) | copy-start | bytes 2359300
  74.8 0.9 copy-start.3
  79.1 14.9 %collective-permute-start.4 = (bf16[128,1536]{1,0:T(8,128)(2,1)}, bf16[128,1536]{1,0:T(8,128)(2,1)S(1)}, u32[]{:S(2)}, u32[]{:S(2)}) collective-permute-start(bf16[128,1536]{1,0:T(8,128)(2,1)} %get-tuple-element.15), channel_id=1, source_target_pairs={{0,1},{1,2},{2,3},{4,5},{5,6},{6,7},{8,9},{9,10},{10,11},{12,13},{... | collective-permute-start | bytes 1179656 | tf_op jit(solution)/shard_map/ppermute | solution.py:284
  82.4 11.6 %collective-permute-start.5 = (bf16[128,1536]{1,0:T(8,128)(2,1)}, bf16[128,1536]{1,0:T(8,128)(2,1)S(1)}, u32[]{:S(2)}, u32[]{:S(2)}) collective-permute-start(bf16[128,1536]{1,0:T(8,128)(2,1)} %get-tuple-element.16), channel_id=1, source_target_pairs={{1,0},{2,1},{3,2},{5,4},{6,5},{7,6},{9,8},{10,9},{11,10},{13,12},{... | collective-permute-start | bytes 1179656 | tf_op jit(solution)/shard_map/ppermute | solution.py:284
  84.9 9.4 %collective-permute-start.6 = (bf16[128,1536]{1,0:T(8,128)(2,1)}, bf16[128,1536]{1,0:T(8,128)(2,1)S(1)}, u32[]{:S(2)}, u32[]{:S(2)}) collective-permute-start(bf16[128,1536]{1,0:T(8,128)(2,1)} %get-tuple-element.17), channel_id=1, source_target_pairs={{0,4},{4,8},{8,12},{1,5},{5,9},{9,13},{2,6},{6,10},{10,14},{3,7},{... | collective-permute-start | bytes 1179656 | tf_op jit(solution)/shard_map/ppermute | solution.py:284
  88.3 10.0 %collective-permute-start.7 = (bf16[128,1536]{1,0:T(8,128)(2,1)}, bf16[128,1536]{1,0:T(8,128)(2,1)S(1)}, u32[]{:S(2)}, u32[]{:S(2)}) collective-permute-start(bf16[128,1536]{1,0:T(8,128)(2,1)} %get-tuple-element.18), channel_id=1, source_target_pairs={{4,0},{8,4},{12,8},{5,1},{9,5},{13,9},{6,2},{10,6},{14,10},{7,3},{... | collective-permute-start | bytes 1179656 | tf_op jit(solution)/shard_map/ppermute | solution.py:284
  90.5 19.6 %all-to-all-start.4 = ((bf16[8,16,16,128]{3,2,1,0:T(8,128)(2,1)}), bf16[8,16,16,128]{3,2,1,0:T(8,128)(2,1)S(1)}, u32[]{:S(2)}, u32[]{:S(2)}) async-start(bf16[8,16,16,128]{3,2,1,0:T(8,128)(2,1)} %broadcast_in_dim.8), calls=%async_computation.4 | async-start | bytes 1048576 | tf_op jit(solution)/shard_map/all_to_all | solution.py:304
  94.0 4.3 %copy-start.5 = (bf16[128,1536]{1,0:T(8,128)(2,1)}, bf16[128,1536]{1,0:T(8,128)(2,1)S(1)}, u32[]{:S(2)}) copy-start(bf16[128,1536]{1,0:T(8,128)(2,1)S(1)} %collective-permute-done.4.rest_4_) | copy-start | bytes 1179652
  94.0 4.3 %copy-start.6 = (bf16[128,1536]{1,0:T(8,128)(2,1)}, bf16[128,1536]{1,0:T(8,128)(2,1)S(1)}, u32[]{:S(2)}) copy-start(bf16[128,1536]{1,0:T(8,128)(2,1)S(1)} %collective-permute-done.5.rest_5_) | copy-start | bytes 1179652
  94.3 4.0 %copy-start.7 = (bf16[128,1536]{1,0:T(8,128)(2,1)}, bf16[128,1536]{1,0:T(8,128)(2,1)S(1)}, u32[]{:S(2)}) copy-start(bf16[128,1536]{1,0:T(8,128)(2,1)S(1)} %collective-permute-done.6.rest_6_) | copy-start | bytes 1179652
  98.4 0.8 copy-start.8

commit v4 on v3

--- a/solution.py
+++ b/solution.py
@@ -23,7 +23,8 @@
 NKEY = TOK + 6 * EDGE
 SLOTS = 16
 AIM_LANE = 16
-CUT = 512
+PSTEP = 4
+CUT = 768
 HSTEP = 2
 LIVE_CAP = 3.4e38
 DEAD_CAP = -1e30
@@ -42,39 +43,57 @@
     row.append(12 + 1 + edge % TILE // BS)
     row.append((1 + edge // BS // BS) * 4)
     row.append((1 + edge // BS // BS) * 4 + 3)
-    row.append(edge // (BS * BS) * 12)
-    row.append(edge // (BS * BS) * 12 + 3)
+    row.append(edge // (BS * BS) * 3)
+    row.append(edge // (BS * BS) * 3 + 12)
     ids[:] = np.concatenate(row)[None]
     return ids
 
 
 def pool_kernel(pat_ref, aim_ref, q_ref, k_ref, out_ref, aux_ref):
-    row = lax.broadcasted_iota(jnp.int32, (8, TOK), 0)
-    tok = lax.broadcasted_iota(jnp.int32, (8, TOK), 1)
-    block = tok // TILE // BS * 2 + tok % TILE // BS
-    pick_q = (row == block).astype(jnp.float32).astype(jnp.bfloat16)
-    pick_k = (row == block + 4).astype(jnp.float32).astype(jnp.bfloat16)
-    sums = jnp.dot(pick_q, q_ref[...], preferred_element_type=jnp.float32)
-    sums += jnp.dot(pick_k, k_ref[...], preferred_element_type=jnp.float32)
-    means = sums / (BS * BS)
-    aux_ref[...] = jnp.zeros((8, DH), jnp.float32)
-    for y in range(2):
-        aux_ref[2 * y : 2 * y + 2, 0:NOFF] = pat_ref[y].astype(jnp.float32)
-        for k in range(TOPK):
-            at = AIM_LANE * (k + 1)
-            aux_ref[2 * y : 2 * y + 2, at : at + HEADS] = aim_ref[y, k].astype(jnp.float32)
-    aux = aux_ref[...]
-    for h in range(HEADS):
-        out_ref[h, 0:8, :] = means[:, h * DH : (h + 1) * DH]
-        out_ref[h, 8:16, :] = aux
-    for h in range(HEADS, SLOTS):
-        out_ref[h] = jnp.zeros((16, DH), jnp.float32)
+    step = pl.program_id(0)
+
+    @pl.when(step == 0)
+    def _():
+        aux_ref[...] = jnp.zeros((8, DH), jnp.float32)
+        for y in range(2):
+            aux_ref[2 * y : 2 * y + 2, 0:NOFF] = pat_ref[y].astype(jnp.float32)
+            for k in range(TOPK):
+                at = AIM_LANE * (k + 1)
+                aux_ref[2 * y : 2 * y + 2, at : at + HEADS] = aim_ref[y, k].astype(jnp.float32)
+
+    @pl.when(step < HEADS // PSTEP)
+    def _():
+        row = lax.broadcasted_iota(jnp.int32, (8, TOK), 0)
+        tok = lax.broadcasted_iota(jnp.int32, (8, TOK), 1)
+        block = tok // TILE // BS * 2 + tok % TILE // BS
+        pick_q = (row == block).astype(jnp.float32).astype(jnp.bfloat16)
+        pick_k = (row == block + 4).astype(jnp.float32).astype(jnp.bfloat16)
+        sums = jnp.dot(pick_q, q_ref[...], preferred_element_type=jnp.float32)
+        sums += jnp.dot(pick_k, k_ref[...], preferred_element_type=jnp.float32)
+        means = sums / (BS * BS)
+        for h in range(PSTEP):
+            out_ref[h, 0:8, :] = means[:, h * DH : (h + 1) * DH]
+            out_ref[h, 8:16, :] = aux_ref[...]
+
+    @pl.when(step >= HEADS // PSTEP)
+    def _():
+        out_ref[...] = jnp.zeros((PSTEP, 16, DH), jnp.float32)
 
 
 def pool(pattern, aims, query, key):
+    last = HEADS // PSTEP - 1
+    tile = pl.BlockSpec((TOK, PSTEP * DH), lambda i: (0, jnp.minimum(i, last)))
     return pl.pallas_call(
         pool_kernel,
         out_shape=jax.ShapeDtypeStruct((SLOTS, 16, DH), jnp.float32),
+        grid=(SLOTS // PSTEP,),
+        in_specs=[
+            pl.BlockSpec(pattern.shape, lambda i: (0, 0, 0)),
+            pl.BlockSpec(aims.shape, lambda i: (0, 0, 0, 0)),
+            tile,
+            tile,
+        ],
+        out_specs=pl.BlockSpec((PSTEP, 16, DH), lambda i: (i, 0, 0)),
         scratch_shapes=[pltpu.VMEM((8, DH), jnp.float32)],
         name="pool",
     )(pattern, aims, query, key)
@@ -106,31 +125,24 @@
     )(key, value)
 
 
-def corner_kernel(a_ref, b_ref, l_ref, r_ref, right_ref, left_ref, low_ref, high_ref):
-    lanes = a_ref.shape[-1]
+def corner_kernel(l_ref, r_ref, low_ref, high_ref):
     cell = BS * BS
-    for i, ref in enumerate((a_ref, b_ref)):
-        wide = ref[0].astype(jnp.float32).reshape(BS, TILE, lanes)
-        at = slice(i * cell, (i + 1) * cell)
-        right_ref[at] = wide[:, TILE - BS :].reshape(cell, lanes).astype(jnp.bfloat16)
-        left_ref[at] = wide[:, :BS].reshape(cell, lanes).astype(jnp.bfloat16)
     for i, ref in enumerate((l_ref, r_ref)):
         at = slice(i * cell, (i + 1) * cell)
-        low_ref[at] = ref[0, cell:]
-        high_ref[at] = ref[0, :cell]
-
-
-def corner_parts(above, below, left, right):
-    key_side = pl.BlockSpec((1, EDGE, CUT), lambda i: (0, 0, i))
-    value_side = pl.BlockSpec((1, EDGE, CUT), lambda i: (1, 0, i))
+        low_ref[:, at] = ref[:, cell:]
+        high_ref[:, at] = ref[:, :cell]
+
+
+def corner_parts(left, right):
+    side = pl.BlockSpec((2, EDGE, CUT), lambda i: (0, 0, i))
     return pl.pallas_call(
         corner_kernel,
-        out_shape=[jax.ShapeDtypeStruct((EDGE, FEAT), jnp.bfloat16)] * 4,
+        out_shape=[jax.ShapeDtypeStruct((2, EDGE, FEAT), jnp.bfloat16)] * 2,
         grid=(FEAT // CUT,),
-        in_specs=[key_side, key_side, value_side, value_side],
-        out_specs=[pl.BlockSpec((EDGE, CUT), lambda i: (0, i))] * 4,
+        in_specs=[side] * 2,
+        out_specs=[side] * 2,
         name="corners",
-    )(above, below, left, right)
+    )(left, right)
 
 
 def router_kernel(normal, head_ref, recv_ref, wq_ref, wk_ref, out_ref, pq_ref, pk_ref, ax_ref):
@@ -196,8 +208,7 @@
 
 
 def attend_kernel(pat_ref, ids_ref, q_ref, k_ref, v_ref, *rest):
-    sides, (corner_l, corner_r, corner_a, corner_b, out_ref, cap_ref) = rest[:4], rest[4:]
-    cell = BS * BS
+    sides, (out_ref, cap_ref) = rest[:6], rest[6:]
 
     @pl.when(pl.program_id(0) == 0)
     def _():
@@ -217,23 +228,8 @@
     for h in range(HSTEP):
         lanes = slice(h * DH, (h + 1) * DH)
         query = q_ref[:, lanes]
-        keys = jnp.concatenate(
-            [k_ref[:, lanes]]
-            + [s[0, :, lanes] for s in sides]
-            + [corner_l[:, lanes], corner_r[:, lanes]],
-            axis=0,
-        )
-        values = jnp.concatenate(
-            [v_ref[:, lanes]]
-            + [s[1, :, lanes] for s in sides]
-            + [
-                corner_a[:cell, lanes],
-                corner_b[:cell, lanes],
-                corner_a[cell:, lanes],
-                corner_b[cell:, lanes],
-            ],
-            axis=0,
-        )
+        keys = jnp.concatenate([k_ref[:, lanes]] + [s[0, :, lanes] for s in sides], axis=0)
+        values = jnp.concatenate([v_ref[:, lanes]] + [s[1, :, lanes] for s in sides], axis=0)
         scores = lax.dot_general(
             query, keys, (((1,), (1,)), ((), ())), preferred_element_type=jnp.float32
         )
@@ -246,11 +242,10 @@
         out_ref[:, lanes] = out.astype(jnp.bfloat16)
 
 
-def attend(pattern, query, key, value, sides, corners):
+def attend(pattern, query, key, value, sides):
     wide = HSTEP * DH
     own = pl.BlockSpec((TOK, wide), lambda h: (0, h))
     side = pl.BlockSpec((2, EDGE, wide), lambda h: (0, 0, h))
-    corner = pl.BlockSpec((EDGE, wide), lambda h: (0, h))
     return pl.pallas_call(
         attend_kernel,
         out_shape=jax.ShapeDtypeStruct((TOK, FEAT), jnp.bfloat16),
@@ -262,8 +257,7 @@
             own,
             own,
         ]
-        + [side] * 4
-        + [corner] * 4,
+        + [side] * 6,
         out_specs=own,
         scratch_shapes=[pltpu.VMEM((TOK, NKEY), jnp.float32)],
         cost_estimate=pl.CostEstimate(
@@ -272,7 +266,7 @@
             transcendentals=HEADS * TOK * NKEY,
         ),
         name="attend",
-    )(pattern, jnp.asarray(key_block_ids()), query, key, value, *sides, *corners)
+    )(pattern, jnp.asarray(key_block_ids()), query, key, value, *sides)
 
 
 def shift(x, axis, step):
@@ -290,14 +284,9 @@
     )
 
 
-def corners_of(above, below, left, right):
-    to_right, to_left, to_low, to_high = corner_parts(above, below, left, right)
-    return (
-        shift(to_right, "px", 1),
-        shift(to_left, "px", -1),
-        shift(to_low, "py", 1),
-        shift(to_high, "py", -1),
-    )
+def corners_of(left, right):
+    low, high = corner_parts(left, right)
+    return shift(low, "py", 1), shift(high, "py", -1)
 
 
 def exchange(x, axis):
@@ -332,8 +321,8 @@
     every = everyone(heads, NEAR, near)[:, :HEADS].astype(jnp.float32)
     every = every.transpose(1, 0, 2, 3).reshape(HEADS, 2 * RW, DH)
     grad_q, grad_k = (x.swapaxes(1, 2) for x in (every[:, :RW], every[:, RW:]))
-    corners = corners_of(*sides)
-    attended = attend(pattern.reshape(4, NOFF), query, key, value, sides, corners)
+    corners = corners_of(*sides[2:])
+    attended = attend(pattern.reshape(4, NOFF), query, key, value, sides + corners)
     return (attended.reshape(1, TILE, TILE, FEAT), grad_q, grad_k)
 
 

time: 112 us -> 133 us (1.19)
  the two profiles are of different devices: /device:TPU:32 before, /device:TPU:1 now
where the time goes in v4:
time: 133 us; the launch traced here: 132 us
  blocking collectives  48.8 us (37%)
  starting transfers between devices  29.6 us (22%)
  waiting for transfers between devices  25.9 us (19%)
  Pallas kernels  22 us (17%)
  local copies, waits for them, and re-layouts  5.09 us (4%)
    all_to_all x3, blocking collectives, exchange(): return lax.all_to_all(x, axis, 0, 0)  48.8 us
    ppermute x6, waiting for transfers between devices, shift(): return lax.ppermute(x, axis, pairs)  25.9 us
    all_to_all x2, starting transfers between devices, exchange(): return lax.all_to_all(x, axis, 0, 0)  16.2 us
    ppermute x6, starting transfers between devices, shift(): return lax.ppermute(x, axis, pairs)  13.4 us
    pallas_call x1, Pallas kernels, attend(): pl.pallas_call(attend_kernel, out_shape=jax.ShapeDtypeStruct((TOK, FEAT),...  10.9 us
    unnamed x12, local copies, waits for them, and re-layouts  3.26 us
    pallas_call x1, Pallas kernels, pool(): pl.pallas_call(pool_kernel, out_shape=jax.ShapeDtypeStruct((SLOTS, 16, DH...  3.17 us
    pallas_call x1, Pallas kernels, rims_of(): pl.pallas_call(rim_kernel, out_shape=[jax.ShapeDtypeStruct((2, EDGE, FEAT...  2.92 us
  transfers between devices with their start and end apart: 8, of which 4 were waited for; matrix products, arithmetic and copies ran while one was open for 1% of the time, Pallas kernels for 6%

profile of v4, /device:TPU:1, one launch (start us, length us, event | category | flops | bytes accessed | tf_op | source)
XLA Modules:
  0.0 132.3 jit_solution(11900949018086461730)
XLA Ops:
  0.6 3.2 %pool.1 = f32[16,16,128]{2,1,0:T(8,128)} custom-call(s32[2,2,9]{2,1,0:T(2,128)} %bitcast.34, s32[2,3,2,12]{3,2,1,0:T(2,128)} %bitcast.36, bf16[256,1536]{1,0:T(8,128)(2,1)} %bitcast.27, bf16[256,1536]{1,0:T(8,128)(2,1)} %bitcast.22), custom_call_target="tpu_custom_call" | custom-call | tf_op jit(solution)/shard_map/pool/pallas_call | solution.py:86
  3.8 9.2 %all-to-all-start = ((f32[16,16,128]{2,1,0:T(8,128)}), f32[16,16,128]{2,1,0:T(8,128)S(1)}, u32[]{:S(2)}, u32[]{:S(2)}) async-start(f32[16,16,128]{2,1,0:T(8,128)} %pool.1), calls=%async_computation | async-start | bytes 262144 | tf_op jit(solution)/shard_map/all_to_all | solution.py:293
  13.0 2.9 %rims.1 = (bf16[2,128,1536]{2,1,0:T(8,128)(2,1)}, bf16[2,128,1536]{2,1,0:T(8,128)(2,1)}, bf16[2,128,1536]{2,1,0:T(8,128)(2,1)}, bf16[2,128,1536]{2,1,0:T(8,128)(2,1)}) custom-call(bf16[16,16,1536]{2,1,0:T(8,128)(2,1)} %bitcast.23, bf16[16,16,1536]{2,1,0:T(8,128)(2,1)} %bitcast.25), custom_call_target="tpu_custom_call" | custom-call | tf_op jit(solution)/shard_map/rims/pallas_call | solution.py:118
  15.9 3.3 %collective-permute-start.2 = (bf16[2,128,1536]{2,1,0:T(8,128)(2,1)}, bf16[2,128,1536]{2,1,0:T(8,128)(2,1)S(1)}, u32[]{:S(2)}, u32[]{:S(2)}) collective-permute-start(bf16[2,128,1536]{2,1,0:T(8,128)(2,1)} %get-tuple-element.11), channel_id=1, source_target_pairs={{0,1},{1,2},{2,3},{4,5},{5,6},{6,7},{8,9},{9,10},{10,11},{12,13},{... | collective-permute-start | bytes 2359304 | tf_op jit(solution)/shard_map/ppermute | solution.py:278
  19.2 1.3 collective-permute-start.3
  20.5 0.0 all-to-all-done.recv_ref
  20.5 0.0 copy-start.5
  20.5 0.6 copy-done.5
  21.2 2.7 %router.1 = f32[128,128]{1,0:T(8,128)} custom-call(s32[1]{0:T(128)} %bitcast.7.head_ref, f32[16,16,128]{2,1,0:T(8,128)} %copy-done.5, f32[12,64,128]{2,1,0:T(8,128)} %bitcast.31, f32[12,64,128]{2,1,0:T(8,128)} %bitcast.32), custom_call_target="tpu_custom_call" | custom-call | tf_op jit(solution)/shard_map/router/pallas_call | solution.py:192
  23.8 11.0 %all_to_all.25 = f32[8,16,128]{2,1,0:T(8,128)S(1)} all-to-all(f32[8,16,128]{2,1,0:T(8,128)} %bitcast.33), channel_id=1, replica_groups=mesh['x'=4,'far'=4,'core'=2,'py'=4,'px'=4] {'x','core'}, dimensions={0} | all-to-all | bytes 131072 | tf_op jit(solution)/shard_map/all_to_all | solution.py:293
  34.8 23.4 %all_to_all.26 = f32[4,16,128]{2,1,0:T(8,128)S(1)} all-to-all(f32[4,16,128]{2,1,0:T(8,128)S(1)} %broadcast_in_dim.6), channel_id=1, replica_groups=mesh['x'=4,'far'=4,'core'=2,'py'=4,'px'=4] {'far'}, dimensions={0} | all-to-all | bytes 65536 | tf_op jit(solution)/shard_map/all_to_all | solution.py:293
  58.3 14.4 %all_to_all.27 = bf16[16,16,128]{2,1,0:T(8,128)(2,1)S(1)} all-to-all(bf16[16,16,128]{2,1,0:T(8,128)(2,1)S(1)} %broadcast_in_dim.7), channel_id=1, replica_groups=mesh['x'=4,'far'=4,'core'=2,'py'=4,'px'=4] {'py','px'}, dimensions={0} | all-to-all | bytes 131072 | tf_op jit(solution)/shard_map/all_to_all | solution.py:293
  72.7 0.9 broadcast_in_dim.8
  73.6 7.0 %all-to-all-start.4 = ((bf16[8,16,16,128]{3,2,1,0:T(8,128)(2,1)}), bf16[8,16,16,128]{3,2,1,0:T(8,128)(2,1)S(1)}, u32[]{:S(2)}, u32[]{:S(2)}) async-start(bf16[8,16,16,128]{3,2,1,0:T(8,128)(2,1)} %broadcast_in_dim.8), calls=%async_computation.4 | async-start | bytes 1048576 | tf_op jit(solution)/shard_map/all_to_all | solution.py:293
  80.6 2.2 %collective-permute-start = (bf16[2,128,1536]{2,1,0:T(8,128)(2,1)}, bf16[2,128,1536]{2,1,0:T(8,128)(2,1)S(1)}, u32[]{:S(2)}, u32[]{:S(2)}) collective-permute-start(bf16[2,128,1536]{2,1,0:T(8,128)(2,1)} %get-tuple-element.9), channel_id=1, source_target_pairs={{0,4},{4,8},{8,12},{1,5},{5,9},{9,13},{2,6},{6,10},{10,14},{3,7},{... | collective-permute-start | bytes 2359304 | tf_op jit(solution)/shard_map/ppermute | solution.py:278
  82.8 1.3 collective-permute-start.1
  84.1 0.0 collective-permute-done.2.l_ref.rest_2_
  84.2 0.0 copy-start
  84.2 0.0 collective-permute-done.3.r_ref.rest_3_
  84.2 0.9 copy-done
  85.0 0.0 copy-start.1
  85.0 0.9 copy-done.1
  85.9 2.3 %corners.1 = (bf16[2,128,1536]{2,1,0:T(8,128)(2,1)}, bf16[2,128,1536]{2,1,0:T(8,128)(2,1)}) custom-call(bf16[2,128,1536]{2,1,0:T(8,128)(2,1)} %copy-done, bf16[2,128,1536]{2,1,0:T(8,128)(2,1)} %copy-done.1), custom_call_target="tpu_custom_call" | custom-call | tf_op jit(solution)/shard_map/corners/pallas_call | solution.py:138
  88.3 4.0 %collective-permute-start.4 = (bf16[2,128,1536]{2,1,0:T(8,128)(2,1)}, bf16[2,128,1536]{2,1,0:T(8,128)(2,1)S(1)}, u32[]{:S(2)}, u32[]{:S(2)}) collective-permute-start(bf16[2,128,1536]{2,1,0:T(8,128)(2,1)} %get-tuple-element.13), channel_id=1, source_target_pairs={{0,4},{4,8},{8,12},{1,5},{5,9},{9,13},{2,6},{6,10},{10,14},{3,7},{... | collective-permute-start | bytes 2359304 | tf_op jit(solution)/shard_map/ppermute | solution.py:278
  92.3 1.3 collective-permute-start.5
  93.6 0.0 all-to-all-done.4
  93.6 0.1 copy_convert_fusion
  93.7 0.9 slice_bitcast_fusion
  94.6 5.3 %collective-permute-done.rest_0_ = bf16[2,128,1536]{2,1,0:T(8,128)(2,1)S(1)} collective-permute-done((bf16[2,128,1536]{2,1,0:T(8,128)(2,1)}, bf16[2,128,1536]{2,1,0:T(8,128)(2,1)S(1)}, u32[]{:S(2)}, u32[]{:S(2)}) %collective-permute-start) | collective-permute-done | bytes 786464 | tf_op jit(solution)/shard_map/ppermute | solution.py:278
  99.9 0.0 copy-start.2
  99.9 3.9 %collective-permute-done.1.rest_1_ = bf16[2,128,1536]{2,1,0:T(8,128)(2,1)} collective-permute-done((bf16[2,128,1536]{2,1,0:T(8,128)(2,1)}, bf16[2,128,1536]{2,1,0:T(8,128)(2,1)}, u32[]{:S(2)}, u32[]{:S(2)}) %collective-permute-start.1) | collective-permute-done | bytes 786464 | tf_op jit(solution)/shard_map/ppermute | solution.py:278
  103.8 13.0 %collective-permute-done.4.rest_4_ = bf16[2,128,1536]{2,1,0:T(8,128)(2,1)S(1)} collective-permute-done((bf16[2,128,1536]{2,1,0:T(8,128)(2,1)}, bf16[2,128,1536]{2,1,0:T(8,128)(2,1)S(1)}, u32[]{:S(2)}, u32[]{:S(2)}) %collective-permute-start.4) | collective-permute-done | bytes 786464 | tf_op jit(solution)/shard_map/ppermute | solution.py:278
  116.7 0.0 copy-start.3
  116.7 3.8 %collective-permute-done.5.rest_5_ = bf16[2,128,1536]{2,1,0:T(8,128)(2,1)S(1)} collective-permute-done((bf16[2,128,1536]{2,1,0:T(8,128)(2,1)}, bf16[2,128,1536]{2,1,0:T(8,128)(2,1)S(1)}, u32[]{:S(2)}, u32[]{:S(2)}) %collective-permute-start.5) | collective-permute-done | bytes 786464 | tf_op jit(solution)/shard_map/ppermute | solution.py:278
  120.5 0.0 copy-start.4
  120.5 0.0 copy-done.2
  120.5 0.0 copy-done.3
  120.5 0.9 copy-done.4
  121.4 10.9 %attend.1 = bf16[256,1536]{1,0:T(8,128)(2,1)} custom-call(s32[4,9]{1,0:T(4,128)} %bitcast.35, s32[8,1024]{1,0:T(8,128)} %constant.15.clone.ids_ref, bf16[256,1536]{1,0:T(8,128)(2,1)} %bitcast.28, bf16[256,1536]{1,0:T(8,128)(2,1)} %bitcast.24, bf16[256,1536]{1,0:T(8,128)(2,1)} %bitcast.26, bf16[2,128,1536]{2,1,0:T(8,128)(2,1)} %copy-done.2, ...), custom_call_target="tpu_custom_call" | custom-call | flops 1610612736 | bytes 7864320 | tf_op jit(solution)/shard_map/attend/pallas_call | solution.py:249
  (4 shorter events, 0.0 us)
Async XLA Ops:
  3.8 16.7 %all-to-all-start = ((f32[16,16,128]{2,1,0:T(8,128)}), f32[16,16,128]{2,1,0:T(8,128)S(1)}, u32[]{:S(2)}, u32[]{:S(2)}) async-start(f32[16,16,128]{2,1,0:T(8,128)} %pool.1), calls=%async_computation | async-start | bytes 262144 | tf_op jit(solution)/shard_map/all_to_all | solution.py:293
  15.9 68.3 %collective-permute-start.2 = (bf16[2,128,1536]{2,1,0:T(8,128)(2,1)}, bf16[2,128,1536]{2,1,0:T(8,128)(2,1)S(1)}, u32[]{:S(2)}, u32[]{:S(2)}) collective-permute-start(bf16[2,128,1536]{2,1,0:T(8,128)(2,1)} %get-tuple-element.11), channel_id=1, source_target_pairs={{0,1},{1,2},{2,3},{4,5},{5,6},{6,7},{8,9},{9,10},{10,11},{12,13},{... | collective-permute-start | bytes 2359304 | tf_op jit(solution)/shard_map/ppermute | solution.py:278
  19.2 65.0 %collective-permute-start.3 = (bf16[2,128,1536]{2,1,0:T(8,128)(2,1)}, bf16[2,128,1536]{2,1,0:T(8,128)(2,1)S(1)}, u32[]{:S(2)}, u32[]{:S(2)}) collective-permute-start(bf16[2,128,1536]{2,1,0:T(8,128)(2,1)} %get-tuple-element.12), channel_id=1, source_target_pairs={{1,0},{2,1},{3,2},{5,4},{6,5},{7,6},{9,8},{10,9},{11,10},{13,12},{... | collective-permute-start | bytes 2359304 | tf_op jit(solution)/shard_map/ppermute | solution.py:278
  20.5 0.7 copy-start.5
  73.6 20.0 %all-to-all-start.4 = ((bf16[8,16,16,128]{3,2,1,0:T(8,128)(2,1)}), bf16[8,16,16,128]{3,2,1,0:T(8,128)(2,1)S(1)}, u32[]{:S(2)}, u32[]{:S(2)}) async-start(bf16[8,16,16,128]{3,2,1,0:T(8,128)(2,1)} %broadcast_in_dim.8), calls=%async_computation.4 | async-start | bytes 1048576 | tf_op jit(solution)/shard_map/all_to_all | solution.py:293
  80.6 19.3 %collective-permute-start = (bf16[2,128,1536]{2,1,0:T(8,128)(2,1)}, bf16[2,128,1536]{2,1,0:T(8,128)(2,1)S(1)}, u32[]{:S(2)}, u32[]{:S(2)}) collective-permute-start(bf16[2,128,1536]{2,1,0:T(8,128)(2,1)} %get-tuple-element.9), channel_id=1, source_target_pairs={{0,4},{4,8},{8,12},{1,5},{5,9},{9,13},{2,6},{6,10},{10,14},{3,7},{... | collective-permute-start | bytes 2359304 | tf_op jit(solution)/shard_map/ppermute | solution.py:278
  82.8 20.9 %collective-permute-start.1 = (bf16[2,128,1536]{2,1,0:T(8,128)(2,1)}, bf16[2,128,1536]{2,1,0:T(8,128)(2,1)}, u32[]{:S(2)}, u32[]{:S(2)}) collective-permute-start(bf16[2,128,1536]{2,1,0:T(8,128)(2,1)} %get-tuple-element.10), channel_id=1, source_target_pairs={{4,0},{8,4},{12,8},{5,1},{9,5},{13,9},{6,2},{10,6},{14,10},{7,3},{... | collective-permute-start | bytes 2359304 | tf_op jit(solution)/shard_map/ppermute | solution.py:278
  84.2 0.9 copy-start
  85.0 0.9 copy-start.1
  88.3 28.5 %collective-permute-start.4 = (bf16[2,128,1536]{2,1,0:T(8,128)(2,1)}, bf16[2,128,1536]{2,1,0:T(8,128)(2,1)S(1)}, u32[]{:S(2)}, u32[]{:S(2)}) collective-permute-start(bf16[2,128,1536]{2,1,0:T(8,128)(2,1)} %get-tuple-element.13), channel_id=1, source_target_pairs={{0,4},{4,8},{8,12},{1,5},{5,9},{9,13},{2,6},{6,10},{10,14},{3,7},{... | collective-permute-start | bytes 2359304 | tf_op jit(solution)/shard_map/ppermute | solution.py:278
  92.3 28.2 %collective-permute-start.5 = (bf16[2,128,1536]{2,1,0:T(8,128)(2,1)}, bf16[2,128,1536]{2,1,0:T(8,128)(2,1)S(1)}, u32[]{:S(2)}, u32[]{:S(2)}) collective-permute-start(bf16[2,128,1536]{2,1,0:T(8,128)(2,1)} %get-tuple-element.14), channel_id=1, source_target_pairs={{4,0},{8,4},{12,8},{5,1},{9,5},{13,9},{6,2},{10,6},{14,10},{7,3},{... | collective-permute-start | bytes 2359304 | tf_op jit(solution)/shard_map/ppermute | solution.py:278
  99.9 20.6 %copy-start.2 = (bf16[2,128,1536]{2,1,0:T(8,128)(2,1)}, bf16[2,128,1536]{2,1,0:T(8,128)(2,1)S(1)}, u32[]{:S(2)}) copy-start(bf16[2,128,1536]{2,1,0:T(8,128)(2,1)S(1)} %collective-permute-done.rest_0_) | copy-start | bytes 2359300
  116.7 3.8 %copy-start.3 = (bf16[2,128,1536]{2,1,0:T(8,128)(2,1)}, bf16[2,128,1536]{2,1,0:T(8,128)(2,1)S(1)}, u32[]{:S(2)}) copy-start(bf16[2,128,1536]{2,1,0:T(8,128)(2,1)S(1)} %collective-permute-done.4.rest_4_) | copy-start | bytes 2359300
  120.5 0.9 copy-start.4

commit v5 on v4

--- a/solution.py
+++ b/solution.py
@@ -23,7 +23,6 @@
 NKEY = TOK + 6 * EDGE
 SLOTS = 16
 AIM_LANE = 16
-PSTEP = 4
 CUT = 768
 HSTEP = 2
 LIVE_CAP = 3.4e38
@@ -50,50 +49,32 @@
 
 
 def pool_kernel(pat_ref, aim_ref, q_ref, k_ref, out_ref, aux_ref):
-    step = pl.program_id(0)
-
-    @pl.when(step == 0)
-    def _():
-        aux_ref[...] = jnp.zeros((8, DH), jnp.float32)
-        for y in range(2):
-            aux_ref[2 * y : 2 * y + 2, 0:NOFF] = pat_ref[y].astype(jnp.float32)
-            for k in range(TOPK):
-                at = AIM_LANE * (k + 1)
-                aux_ref[2 * y : 2 * y + 2, at : at + HEADS] = aim_ref[y, k].astype(jnp.float32)
-
-    @pl.when(step < HEADS // PSTEP)
-    def _():
-        row = lax.broadcasted_iota(jnp.int32, (8, TOK), 0)
-        tok = lax.broadcasted_iota(jnp.int32, (8, TOK), 1)
-        block = tok // TILE // BS * 2 + tok % TILE // BS
-        pick_q = (row == block).astype(jnp.float32).astype(jnp.bfloat16)
-        pick_k = (row == block + 4).astype(jnp.float32).astype(jnp.bfloat16)
-        sums = jnp.dot(pick_q, q_ref[...], preferred_element_type=jnp.float32)
-        sums += jnp.dot(pick_k, k_ref[...], preferred_element_type=jnp.float32)
-        means = sums / (BS * BS)
-        for h in range(PSTEP):
-            out_ref[h, 0:8, :] = means[:, h * DH : (h + 1) * DH]
-            out_ref[h, 8:16, :] = aux_ref[...]
-
-    @pl.when(step >= HEADS // PSTEP)
-    def _():
-        out_ref[...] = jnp.zeros((PSTEP, 16, DH), jnp.float32)
+    row = lax.broadcasted_iota(jnp.int32, (8, TOK), 0)
+    tok = lax.broadcasted_iota(jnp.int32, (8, TOK), 1)
+    block = tok // TILE // BS * 2 + tok % TILE // BS
+    pick_q = (row == block).astype(jnp.float32).astype(jnp.bfloat16)
+    pick_k = (row == block + 4).astype(jnp.float32).astype(jnp.bfloat16)
+    sums = jnp.dot(pick_q, q_ref[...], preferred_element_type=jnp.float32)
+    sums += jnp.dot(pick_k, k_ref[...], preferred_element_type=jnp.float32)
+    means = sums / (BS * BS)
+    aux_ref[...] = jnp.zeros((8, DH), jnp.float32)
+    for y in range(2):
+        aux_ref[2 * y : 2 * y + 2, 0:NOFF] = pat_ref[y].astype(jnp.float32)
+        for k in range(TOPK):
+            at = AIM_LANE * (k + 1)
+            aux_ref[2 * y : 2 * y + 2, at : at + HEADS] = aim_ref[y, k].astype(jnp.float32)
+    aux = aux_ref[...]
+    for h in range(HEADS):
+        out_ref[h, 0:8, :] = means[:, h * DH : (h + 1) * DH]
+        out_ref[h, 8:16, :] = aux
+    for h in range(HEADS, SLOTS):
+        out_ref[h] = jnp.zeros((16, DH), jnp.float32)
 
 
 def pool(pattern, aims, query, key):
-    last = HEADS // PSTEP - 1
-    tile = pl.BlockSpec((TOK, PSTEP * DH), lambda i: (0, jnp.minimum(i, last)))
     return pl.pallas_call(
         pool_kernel,
         out_shape=jax.ShapeDtypeStruct((SLOTS, 16, DH), jnp.float32),
-        grid=(SLOTS // PSTEP,),
-        in_specs=[
-            pl.BlockSpec(pattern.shape, lambda i: (0, 0, 0)),
-            pl.BlockSpec(aims.shape, lambda i: (0, 0, 0, 0)),
-            tile,
-            tile,
-        ],
-        out_specs=pl.BlockSpec((PSTEP, 16, DH), lambda i: (i, 0, 0)),
         scratch_shapes=[pltpu.VMEM((8, DH), jnp.float32)],
         name="pool",
     )(pattern, aims, query, key)

time: 133 us -> 132 us (level)
  no operation moved by 1% of the time
where the time goes in v5:
time: 132 us
  blocking collectives  48.8 us (37%)
  starting transfers between devices  29.6 us (22%)
  waiting for transfers between devices  25.9 us (20%)
  Pallas kernels  21.2 us (16%)
  local copies, waits for them, and re-layouts  5.09 us (4%)
    all_to_all x3, blocking collectives, exchange(): return lax.all_to_all(x, axis, 0, 0)  48.8 us
    ppermute x6, waiting for transfers between devices, shift(): return lax.ppermute(x, axis, pairs)  25.9 us
    all_to_all x2, starting transfers between devices, exchange(): return lax.all_to_all(x, axis, 0, 0)  16.2 us
    ppermute x6, starting transfers between devices, shift(): return lax.ppermute(x, axis, pairs)  13.4 us
    pallas_call x1, Pallas kernels, attend(): pl.pallas_call(attend_kernel, out_shape=jax.ShapeDtypeStruct((TOK, FEAT),...  10.9 us
    unnamed x12, local copies, waits for them, and re-layouts  3.26 us
    pallas_call x1, Pallas kernels, rims_of(): pl.pallas_call(rim_kernel, out_shape=[jax.ShapeDtypeStruct((2, EDGE, FEAT...  2.92 us
    pallas_call x1, Pallas kernels, router_grads(): pl.pallas_call(functools.partial(router_kernel, normal), out_shape=jax.Sh...  2.65 us
  transfers between devices with their start and end apart: 8, of which 4 were waited for; matrix products, arithmetic and copies ran while one was open for 1% of the time, Pallas kernels for 6%

profile of v5, /device:TPU:1, one launch (start us, length us, event | category | flops | bytes accessed | tf_op | source)
XLA Modules:
  0.0 131.5 jit_solution(13670961900280472808)
XLA Ops:
  0.6 2.4 %pool.1 = f32[16,16,128]{2,1,0:T(8,128)} custom-call(s32[2,2,9]{2,1,0:T(2,128)} %bitcast.34, s32[2,3,2,12]{3,2,1,0:T(2,128)} %bitcast.36, bf16[256,1536]{1,0:T(8,128)(2,1)} %bitcast.27, bf16[256,1536]{1,0:T(8,128)(2,1)} %bitcast.22), custom_call_target="tpu_custom_call" | custom-call | tf_op jit(solution)/shard_map/pool/pallas_call | solution.py:75
  3.0 9.2 %all-to-all-start = ((f32[16,16,128]{2,1,0:T(8,128)}), f32[16,16,128]{2,1,0:T(8,128)S(1)}, u32[]{:S(2)}, u32[]{:S(2)}) async-start(f32[16,16,128]{2,1,0:T(8,128)} %pool.1), calls=%async_computation | async-start | bytes 262144 | tf_op jit(solution)/shard_map/all_to_all | solution.py:274
  12.2 2.9 %rims.1 = (bf16[2,128,1536]{2,1,0:T(8,128)(2,1)}, bf16[2,128,1536]{2,1,0:T(8,128)(2,1)}, bf16[2,128,1536]{2,1,0:T(8,128)(2,1)}, bf16[2,128,1536]{2,1,0:T(8,128)(2,1)}) custom-call(bf16[16,16,1536]{2,1,0:T(8,128)(2,1)} %bitcast.23, bf16[16,16,1536]{2,1,0:T(8,128)(2,1)} %bitcast.25), custom_call_target="tpu_custom_call" | custom-call | tf_op jit(solution)/shard_map/rims/pallas_call | solution.py:99
  15.1 3.3 %collective-permute-start.2 = (bf16[2,128,1536]{2,1,0:T(8,128)(2,1)}, bf16[2,128,1536]{2,1,0:T(8,128)(2,1)S(1)}, u32[]{:S(2)}, u32[]{:S(2)}) collective-permute-start(bf16[2,128,1536]{2,1,0:T(8,128)(2,1)} %get-tuple-element.11), channel_id=1, source_target_pairs={{0,1},{1,2},{2,3},{4,5},{5,6},{6,7},{8,9},{9,10},{10,11},{12,13},{... | collective-permute-start | bytes 2359304 | tf_op jit(solution)/shard_map/ppermute | solution.py:259
  18.4 1.3 collective-permute-start.3
  19.7 0.0 all-to-all-done.recv_ref
  19.7 0.0 copy-start.5
  19.7 0.6 copy-done.5
  20.4 2.7 %router.1 = f32[128,128]{1,0:T(8,128)} custom-call(s32[1]{0:T(128)} %bitcast.7.head_ref, f32[16,16,128]{2,1,0:T(8,128)} %copy-done.5, f32[12,64,128]{2,1,0:T(8,128)} %bitcast.31, f32[12,64,128]{2,1,0:T(8,128)} %bitcast.32), custom_call_target="tpu_custom_call" | custom-call | tf_op jit(solution)/shard_map/router/pallas_call | solution.py:173
  23.0 11.0 %all_to_all.25 = f32[8,16,128]{2,1,0:T(8,128)S(1)} all-to-all(f32[8,16,128]{2,1,0:T(8,128)} %bitcast.33), channel_id=1, replica_groups=mesh['x'=4,'far'=4,'core'=2,'py'=4,'px'=4] {'x','core'}, dimensions={0} | all-to-all | bytes 131072 | tf_op jit(solution)/shard_map/all_to_all | solution.py:274
  34.0 23.4 %all_to_all.26 = f32[4,16,128]{2,1,0:T(8,128)S(1)} all-to-all(f32[4,16,128]{2,1,0:T(8,128)S(1)} %broadcast_in_dim.6), channel_id=1, replica_groups=mesh['x'=4,'far'=4,'core'=2,'py'=4,'px'=4] {'far'}, dimensions={0} | all-to-all | bytes 65536 | tf_op jit(solution)/shard_map/all_to_all | solution.py:274
  57.5 14.4 %all_to_all.27 = bf16[16,16,128]{2,1,0:T(8,128)(2,1)S(1)} all-to-all(bf16[16,16,128]{2,1,0:T(8,128)(2,1)S(1)} %broadcast_in_dim.7), channel_id=1, replica_groups=mesh['x'=4,'far'=4,'core'=2,'py'=4,'px'=4] {'py','px'}, dimensions={0} | all-to-all | bytes 131072 | tf_op jit(solution)/shard_map/all_to_all | solution.py:274
  71.9 0.9 broadcast_in_dim.8
  72.8 7.0 %all-to-all-start.4 = ((bf16[8,16,16,128]{3,2,1,0:T(8,128)(2,1)}), bf16[8,16,16,128]{3,2,1,0:T(8,128)(2,1)S(1)}, u32[]{:S(2)}, u32[]{:S(2)}) async-start(bf16[8,16,16,128]{3,2,1,0:T(8,128)(2,1)} %broadcast_in_dim.8), calls=%async_computation.4 | async-start | bytes 1048576 | tf_op jit(solution)/shard_map/all_to_all | solution.py:274
  79.8 2.2 %collective-permute-start = (bf16[2,128,1536]{2,1,0:T(8,128)(2,1)}, bf16[2,128,1536]{2,1,0:T(8,128)(2,1)S(1)}, u32[]{:S(2)}, u32[]{:S(2)}) collective-permute-start(bf16[2,128,1536]{2,1,0:T(8,128)(2,1)} %get-tuple-element.9), channel_id=1, source_target_pairs={{0,4},{4,8},{8,12},{1,5},{5,9},{9,13},{2,6},{6,10},{10,14},{3,7},{... | collective-permute-start | bytes 2359304 | tf_op jit(solution)/shard_map/ppermute | solution.py:259
  82.1 1.3 collective-permute-start.1
  83.4 0.0 collective-permute-done.2.l_ref.rest_2_
  83.4 0.0 copy-start
  83.4 0.0 collective-permute-done.3.r_ref.rest_3_
  83.4 0.9 copy-done
  84.2 0.0 copy-start.1
  84.2 0.9 copy-done.1
  85.1 2.3 %corners.1 = (bf16[2,128,1536]{2,1,0:T(8,128)(2,1)}, bf16[2,128,1536]{2,1,0:T(8,128)(2,1)}) custom-call(bf16[2,128,1536]{2,1,0:T(8,128)(2,1)} %copy-done, bf16[2,128,1536]{2,1,0:T(8,128)(2,1)} %copy-done.1), custom_call_target="tpu_custom_call" | custom-call | tf_op jit(solution)/shard_map/corners/pallas_call | solution.py:119
  87.5 4.0 %collective-permute-start.4 = (bf16[2,128,1536]{2,1,0:T(8,128)(2,1)}, bf16[2,128,1536]{2,1,0:T(8,128)(2,1)S(1)}, u32[]{:S(2)}, u32[]{:S(2)}) collective-permute-start(bf16[2,128,1536]{2,1,0:T(8,128)(2,1)} %get-tuple-element.13), channel_id=1, source_target_pairs={{0,4},{4,8},{8,12},{1,5},{5,9},{9,13},{2,6},{6,10},{10,14},{3,7},{... | collective-permute-start | bytes 2359304 | tf_op jit(solution)/shard_map/ppermute | solution.py:259
  91.5 1.3 collective-permute-start.5
  92.8 0.0 all-to-all-done.4
  92.8 0.1 copy_convert_fusion
  92.9 0.9 slice_bitcast_fusion
  93.8 5.3 %collective-permute-done.rest_0_ = bf16[2,128,1536]{2,1,0:T(8,128)(2,1)S(1)} collective-permute-done((bf16[2,128,1536]{2,1,0:T(8,128)(2,1)}, bf16[2,128,1536]{2,1,0:T(8,128)(2,1)S(1)}, u32[]{:S(2)}, u32[]{:S(2)}) %collective-permute-start) | collective-permute-done | bytes 786464 | tf_op jit(solution)/shard_map/ppermute | solution.py:259
  99.1 0.0 copy-start.2
  99.1 3.9 %collective-permute-done.1.rest_1_ = bf16[2,128,1536]{2,1,0:T(8,128)(2,1)} collective-permute-done((bf16[2,128,1536]{2,1,0:T(8,128)(2,1)}, bf16[2,128,1536]{2,1,0:T(8,128)(2,1)}, u32[]{:S(2)}, u32[]{:S(2)}) %collective-permute-start.1) | collective-permute-done | bytes 786464 | tf_op jit(solution)/shard_map/ppermute | solution.py:259
  103.0 13.0 %collective-permute-done.4.rest_4_ = bf16[2,128,1536]{2,1,0:T(8,128)(2,1)S(1)} collective-permute-done((bf16[2,128,1536]{2,1,0:T(8,128)(2,1)}, bf16[2,128,1536]{2,1,0:T(8,128)(2,1)S(1)}, u32[]{:S(2)}, u32[]{:S(2)}) %collective-permute-start.4) | collective-permute-done | bytes 786464 | tf_op jit(solution)/shard_map/ppermute | solution.py:259
  115.9 0.0 copy-start.3
  115.9 3.8 %collective-permute-done.5.rest_5_ = bf16[2,128,1536]{2,1,0:T(8,128)(2,1)S(1)} collective-permute-done((bf16[2,128,1536]{2,1,0:T(8,128)(2,1)}, bf16[2,128,1536]{2,1,0:T(8,128)(2,1)S(1)}, u32[]{:S(2)}, u32[]{:S(2)}) %collective-permute-start.5) | collective-permute-done | bytes 786464 | tf_op jit(solution)/shard_map/ppermute | solution.py:259
  119.7 0.0 copy-start.4
  119.7 0.0 copy-done.2
  119.7 0.0 copy-done.3
  119.7 0.9 copy-done.4
  120.6 10.9 %attend.1 = bf16[256,1536]{1,0:T(8,128)(2,1)} custom-call(s32[4,9]{1,0:T(4,128)} %bitcast.35, s32[8,1024]{1,0:T(8,128)} %constant.15.clone.ids_ref, bf16[256,1536]{1,0:T(8,128)(2,1)} %bitcast.28, bf16[256,1536]{1,0:T(8,128)(2,1)} %bitcast.24, bf16[256,1536]{1,0:T(8,128)(2,1)} %bitcast.26, bf16[2,128,1536]{2,1,0:T(8,128)(2,1)} %copy-done.2, ...), custom_call_target="tpu_custom_call" | custom-call | flops 1610612736 | bytes 7864320 | tf_op jit(solution)/shard_map/attend/pallas_call | solution.py:230
  (4 shorter events, 0.0 us)
Async XLA Ops:
  3.0 16.7 %all-to-all-start = ((f32[16,16,128]{2,1,0:T(8,128)}), f32[16,16,128]{2,1,0:T(8,128)S(1)}, u32[]{:S(2)}, u32[]{:S(2)}) async-start(f32[16,16,128]{2,1,0:T(8,128)} %pool.1), calls=%async_computation | async-start | bytes 262144 | tf_op jit(solution)/shard_map/all_to_all | solution.py:274
  15.1 68.3 %collective-permute-start.2 = (bf16[2,128,1536]{2,1,0:T(8,128)(2,1)}, bf16[2,128,1536]{2,1,0:T(8,128)(2,1)S(1)}, u32[]{:S(2)}, u32[]{:S(2)}) collective-permute-start(bf16[2,128,1536]{2,1,0:T(8,128)(2,1)} %get-tuple-element.11), channel_id=1, source_target_pairs={{0,1},{1,2},{2,3},{4,5},{5,6},{6,7},{8,9},{9,10},{10,11},{12,13},{... | collective-permute-start | bytes 2359304 | tf_op jit(solution)/shard_map/ppermute | solution.py:259
  18.4 65.0 %collective-permute-start.3 = (bf16[2,128,1536]{2,1,0:T(8,128)(2,1)}, bf16[2,128,1536]{2,1,0:T(8,128)(2,1)S(1)}, u32[]{:S(2)}, u32[]{:S(2)}) collective-permute-start(bf16[2,128,1536]{2,1,0:T(8,128)(2,1)} %get-tuple-element.12), channel_id=1, source_target_pairs={{1,0},{2,1},{3,2},{5,4},{6,5},{7,6},{9,8},{10,9},{11,10},{13,12},{... | collective-permute-start | bytes 2359304 | tf_op jit(solution)/shard_map/ppermute | solution.py:259
  19.7 0.7 copy-start.5
  72.8 20.0 %all-to-all-start.4 = ((bf16[8,16,16,128]{3,2,1,0:T(8,128)(2,1)}), bf16[8,16,16,128]{3,2,1,0:T(8,128)(2,1)S(1)}, u32[]{:S(2)}, u32[]{:S(2)}) async-start(bf16[8,16,16,128]{3,2,1,0:T(8,128)(2,1)} %broadcast_in_dim.8), calls=%async_computation.4 | async-start | bytes 1048576 | tf_op jit(solution)/shard_map/all_to_all | solution.py:274
  79.8 19.3 %collective-permute-start = (bf16[2,128,1536]{2,1,0:T(8,128)(2,1)}, bf16[2,128,1536]{2,1,0:T(8,128)(2,1)S(1)}, u32[]{:S(2)}, u32[]{:S(2)}) collective-permute-start(bf16[2,128,1536]{2,1,0:T(8,128)(2,1)} %get-tuple-element.9), channel_id=1, source_target_pairs={{0,4},{4,8},{8,12},{1,5},{5,9},{9,13},{2,6},{6,10},{10,14},{3,7},{... | collective-permute-start | bytes 2359304 | tf_op jit(solution)/shard_map/ppermute | solution.py:259
  82.1 20.9 %collective-permute-start.1 = (bf16[2,128,1536]{2,1,0:T(8,128)(2,1)}, bf16[2,128,1536]{2,1,0:T(8,128)(2,1)}, u32[]{:S(2)}, u32[]{:S(2)}) collective-permute-start(bf16[2,128,1536]{2,1,0:T(8,128)(2,1)} %get-tuple-element.10), channel_id=1, source_target_pairs={{4,0},{8,4},{12,8},{5,1},{9,5},{13,9},{6,2},{10,6},{14,10},{7,3},{... | collective-permute-start | bytes 2359304 | tf_op jit(solution)/shard_map/ppermute | solution.py:259
  83.4 0.9 copy-start
  84.2 0.9 copy-start.1
  87.5 28.5 %collective-permute-start.4 = (bf16[2,128,1536]{2,1,0:T(8,128)(2,1)}, bf16[2,128,1536]{2,1,0:T(8,128)(2,1)S(1)}, u32[]{:S(2)}, u32[]{:S(2)}) collective-permute-start(bf16[2,128,1536]{2,1,0:T(8,128)(2,1)} %get-tuple-element.13), channel_id=1, source_target_pairs={{0,4},{4,8},{8,12},{1,5},{5,9},{9,13},{2,6},{6,10},{10,14},{3,7},{... | collective-permute-start | bytes 2359304 | tf_op jit(solution)/shard_map/ppermute | solution.py:259
  91.5 28.2 %collective-permute-start.5 = (bf16[2,128,1536]{2,1,0:T(8,128)(2,1)}, bf16[2,128,1536]{2,1,0:T(8,128)(2,1)S(1)}, u32[]{:S(2)}, u32[]{:S(2)}) collective-permute-start(bf16[2,128,1536]{2,1,0:T(8,128)(2,1)} %get-tuple-element.14), channel_id=1, source_target_pairs={{4,0},{8,4},{12,8},{5,1},{9,5},{13,9},{6,2},{10,6},{14,10},{7,3},{... | collective-permute-start | bytes 2359304 | tf_op jit(solution)/shard_map/ppermute | solution.py:259
  99.1 20.6 %copy-start.2 = (bf16[2,128,1536]{2,1,0:T(8,128)(2,1)}, bf16[2,128,1536]{2,1,0:T(8,128)(2,1)S(1)}, u32[]{:S(2)}) copy-start(bf16[2,128,1536]{2,1,0:T(8,128)(2,1)S(1)} %collective-permute-done.rest_0_) | copy-start | bytes 2359300
  115.9 3.8 %copy-start.3 = (bf16[2,128,1536]{2,1,0:T(8,128)(2,1)}, bf16[2,128,1536]{2,1,0:T(8,128)(2,1)S(1)}, u32[]{:S(2)}) copy-start(bf16[2,128,1536]{2,1,0:T(8,128)(2,1)S(1)} %collective-permute-done.4.rest_4_) | copy-start | bytes 2359300
  119.7 0.9 copy-start.4

commit v6 on v5

--- a/solution.py
+++ b/solution.py
@@ -23,6 +23,7 @@
 NKEY = TOK + 6 * EDGE
 SLOTS = 16
 AIM_LANE = 16
+TOTAL_LANE = 64
 CUT = 768
 HSTEP = 2
 LIVE_CAP = 3.4e38
@@ -188,66 +189,134 @@
     )(head, recv, weights_q, weights_k)
 
 
-def attend_kernel(pat_ref, ids_ref, q_ref, k_ref, v_ref, *rest):
-    sides, (out_ref, cap_ref) = rest[:6], rest[6:]
-
-    @pl.when(pl.program_id(0) == 0)
+def build_cap(pat_ref, ids):
+    width = ids.shape[1]
+    tok = lax.broadcasted_iota(jnp.int32, (TOK, width), 0)
+    block = tok // TILE // BS * 2 + tok % TILE // BS
+    cap = jnp.full((TOK, width), DEAD_CAP, jnp.float32)
+    for b in range(4):
+        line = jnp.full((8, width), DEAD_CAP, jnp.float32)
+        for o in range(NOFF):
+            at = (b // 2 + o // 3) * 4 + b % 2 + o % 3
+            value = jnp.where(pat_ref[b, o] > 0, LIVE_CAP, DEAD_CAP)
+            line = jnp.where(ids == at, value, line)
+        cap = jnp.where(block == b, line[0:1, :], cap)
+    return cap
+
+
+def capped_scores(query, keys, cap):
+    scores = lax.dot_general(
+        query, keys, (((1,), (1,)), ((), ())), preferred_element_type=jnp.float32
+    )
+    return jnp.minimum(scores, cap)
+
+
+def power(x):
+    return jnp.exp2(x * (math.log2(math.e) / math.sqrt(DH)))
+
+
+def attend_main_kernel(pat_ref, ids_ref, q_ref, k_ref, v_ref, *rest):
+    sides, (acc_ref, stat_ref, cap_ref) = rest[:4], rest[4:]
+    step = pl.program_id(0)
+
+    @pl.when(step == 0)
     def _():
-        ids = ids_ref[...]
-        tok = lax.broadcasted_iota(jnp.int32, (TOK, NKEY), 0)
-        block = tok // TILE // BS * 2 + tok % TILE // BS
-        cap = jnp.full((TOK, NKEY), DEAD_CAP, jnp.float32)
-        for b in range(4):
-            line = jnp.full((8, NKEY), DEAD_CAP, jnp.float32)
-            for o in range(NOFF):
-                at = (b // 2 + o // 3) * 4 + b % 2 + o % 3
-                value = jnp.where(pat_ref[b, o] > 0, LIVE_CAP, DEAD_CAP)
-                line = jnp.where(ids == at, value, line)
-            cap = jnp.where(block == b, line[0:1, :], cap)
-        cap_ref[...] = cap
-
+        cap_ref[...] = build_cap(pat_ref, ids_ref[...])
+        stat_ref[...] = jnp.zeros((TOK, DH), jnp.float32)
+
+    lane = lax.broadcasted_iota(jnp.int32, (TOK, DH), 1)
     for h in range(HSTEP):
+        head = step * HSTEP + h
         lanes = slice(h * DH, (h + 1) * DH)
-        query = q_ref[:, lanes]
         keys = jnp.concatenate([k_ref[:, lanes]] + [s[0, :, lanes] for s in sides], axis=0)
         values = jnp.concatenate([v_ref[:, lanes]] + [s[1, :, lanes] for s in sides], axis=0)
-        scores = lax.dot_general(
-            query, keys, (((1,), (1,)), ((), ())), preferred_element_type=jnp.float32
+        scores = capped_scores(q_ref[:, lanes], keys, cap_ref[...])
+        top = jnp.max(scores, axis=1, keepdims=True)
+        weights = power(scores - top)
+        total = jnp.sum(weights, axis=1, keepdims=True)
+        acc_ref[:, lanes] = jnp.dot(
+            weights.astype(jnp.bfloat16), values, preferred_element_type=jnp.float32
         )
-        scores = jnp.minimum(scores, cap_ref[...])
-        top = jnp.max(scores, axis=1, keepdims=True)
-        weights = jnp.exp2((scores - top) * (math.log2(math.e) / math.sqrt(DH)))
-        total = jnp.sum(weights, axis=1, keepdims=True)
-        probs = (weights * (1.0 / total)).astype(jnp.bfloat16)
-        out = jnp.dot(probs, values, preferred_element_type=jnp.float32)
-        out_ref[:, lanes] = out.astype(jnp.bfloat16)
-
-
-def attend(pattern, query, key, value, sides):
+        stat = jnp.where(lane == head, top, stat_ref[...])
+        stat_ref[...] = jnp.where(lane == head + TOTAL_LANE, total, stat)
+
+
+def attend_rest_kernel(pat_ref, ids_ref, q_ref, acc_ref, stat_ref, a_ref, b_ref, out_ref, cap_ref):
+    step = pl.program_id(0)
+
+    @pl.when(step == 0)
+    def _():
+        cap_ref[...] = build_cap(pat_ref, ids_ref[...])
+
+    lane = lax.broadcasted_iota(jnp.int32, (TOK, DH), 1)
+    for h in range(HSTEP):
+        head = step * HSTEP + h
+        lanes = slice(h * DH, (h + 1) * DH)
+        keys = jnp.concatenate([s[0, :, lanes] for s in (a_ref, b_ref)], axis=0)
+        values = jnp.concatenate([s[1, :, lanes] for s in (a_ref, b_ref)], axis=0)
+        stat = stat_ref[...]
+        main_top = jnp.sum(jnp.where(lane == head, stat, 0.0), axis=1, keepdims=True)
+        main_total = jnp.sum(jnp.where(lane == head + TOTAL_LANE, stat, 0.0), axis=1, keepdims=True)
+        scores = capped_scores(q_ref[:, lanes], keys, cap_ref[...])
+        top = jnp.maximum(main_top, jnp.max(scores, axis=1, keepdims=True))
+        weights = power(scores - top)
+        keep = power(main_top - top)
+        total = main_total * keep + jnp.sum(weights, axis=1, keepdims=True)
+        out = acc_ref[:, lanes] * keep + jnp.dot(
+            weights.astype(jnp.bfloat16), values, preferred_element_type=jnp.float32
+        )
+        out_ref[:, lanes] = (out / total).astype(jnp.bfloat16)
+
+
+def attend_specs():
     wide = HSTEP * DH
-    own = pl.BlockSpec((TOK, wide), lambda h: (0, h))
-    side = pl.BlockSpec((2, EDGE, wide), lambda h: (0, 0, h))
-    return pl.pallas_call(
-        attend_kernel,
+    return (
+        pl.BlockSpec(memory_space=pltpu.SMEM),
+        pl.BlockSpec((TOK, wide), lambda h: (0, h)),
+        pl.BlockSpec((2, EDGE, wide), lambda h: (0, 0, h)),
+        pl.BlockSpec((TOK, DH), lambda h: (0, 0)),
+    )
+
+
+def attend_main(pattern, query, key, value, sides):
+    smem, own, side, stat = attend_specs()
+    width = TOK + 4 * EDGE
+    return pl.pallas_call(
+        attend_main_kernel,
+        out_shape=(
+            jax.ShapeDtypeStruct((TOK, FEAT), jnp.float32),
+            jax.ShapeDtypeStruct((TOK, DH), jnp.float32),
+        ),
+        grid=(HEADS // HSTEP,),
+        in_specs=[smem, pl.BlockSpec((8, width), lambda h: (0, 0)), own, own, own] + [side] * 4,
+        out_specs=(own, stat),
+        scratch_shapes=[pltpu.VMEM((TOK, width), jnp.float32)],
+        cost_estimate=pl.CostEstimate(
+            flops=4 * HEADS * TOK * width * DH,
+            bytes_accessed=2 * FEAT * (3 * TOK + 2 * width),
+            transcendentals=HEADS * TOK * width,
+        ),
+        name="attend_main",
+    )(pattern, jnp.asarray(key_block_ids()[:, :width]), query, key, value, *sides)
+
+
+def attend_rest(pattern, query, acc, stat_in, corners):
+    smem, own, side, stat = attend_specs()
+    width = 2 * EDGE
+    return pl.pallas_call(
+        attend_rest_kernel,
         out_shape=jax.ShapeDtypeStruct((TOK, FEAT), jnp.bfloat16),
         grid=(HEADS // HSTEP,),
-        in_specs=[
-            pl.BlockSpec(memory_space=pltpu.SMEM),
-            pl.BlockSpec((8, NKEY), lambda h: (0, 0)),
-            own,
-            own,
-            own,
-        ]
-        + [side] * 6,
+        in_specs=[smem, pl.BlockSpec((8, width), lambda h: (0, 0)), own, own, stat] + [side] * 2,
         out_specs=own,
-        scratch_shapes=[pltpu.VMEM((TOK, NKEY), jnp.float32)],
+        scratch_shapes=[pltpu.VMEM((TOK, width), jnp.float32)],
         cost_estimate=pl.CostEstimate(
-            flops=4 * HEADS * TOK * NKEY * DH,
-            bytes_accessed=2 * FEAT * (2 * TOK + 2 * NKEY),
-            transcendentals=HEADS * TOK * NKEY,
-        ),
-        name="attend",
-    )(pattern, jnp.asarray(key_block_ids()), query, key, value, *sides)
+            flops=4 * HEADS * TOK * width * DH,
+            bytes_accessed=2 * FEAT * (4 * TOK + 2 * width),
+            transcendentals=HEADS * TOK * width,
+        ),
+        name="attend_rest",
+    )(pattern, jnp.asarray(key_block_ids()[:, -width:]), query, acc, stat_in, *corners)
 
 
 def shift(x, axis, step):
@@ -303,7 +372,9 @@
     every = every.transpose(1, 0, 2, 3).reshape(HEADS, 2 * RW, DH)
     grad_q, grad_k = (x.swapaxes(1, 2) for x in (every[:, :RW], every[:, RW:]))
     corners = corners_of(*sides[2:])
-    attended = attend(pattern.reshape(4, NOFF), query, key, value, sides + corners)
+    pat = pattern.reshape(4, NOFF)
+    acc, stat = attend_main(pat, query, key, value, sides)
+    attended = attend_rest(pat, query, acc, stat, corners)
     return (attended.reshape(1, TILE, TILE, FEAT), grad_q, grad_k)
 
 

time: 132 us -> 123 us (0.932)
  waiting for transfers between devices: 25.9 us -> 8.58 us
  Pallas kernels: 21.2 us -> 26.6 us
  blocking collectives: 48.8 us -> 50.8 us
    ppermute x6, waiting for transfers between devices: 25.9 us -> 8.57 us  [shift(): return lax.ppermute(x, axis, pairs)]
    pallas_call x1 -> x2, Pallas kernels: 10.9 us -> 16.3 us  [the longest x1 9.02 us: attend_main(): pl.pallas_call(attend_main_kernel, out_shape=(jax.ShapeDtypeStruct((TOK,...]
    all_to_all x3, blocking collectives: 48.8 us -> 50.8 us  [exchange(): return lax.all_to_all(x, axis, 0, 0)]
  transfers between devices with their start and end apart: 8 -> 8, of which waited for: 4 -> 2; matrix products, arithmetic and copies ran while one was open for 1% -> 2% of each run, Pallas kernels for 6% -> 14%
where the time goes in v6:
time: 123 us; the launch traced here: 122 us
  blocking collectives  50.8 us (41%)
  starting transfers between devices  28.7 us (23%)
  Pallas kernels  26.6 us (22%)
  waiting for transfers between devices  8.58 us (7%)
  local copies, waits for them, and re-layouts  6.02 us (5%)
    all_to_all x3, blocking collectives, exchange(): return lax.all_to_all(x, axis, 0, 0)  50.8 us
    all_to_all x2, starting transfers between devices, exchange(): return lax.all_to_all(x, axis, 0, 0)  16.2 us
    ppermute x6, starting transfers between devices, shift(): return lax.ppermute(x, axis, pairs)  12.5 us
    pallas_call x1, Pallas kernels, attend_main(): pl.pallas_call(attend_main_kernel, out_shape=(jax.ShapeDtypeStruct((TOK,...  9.02 us
    ppermute x6, waiting for transfers between devices, shift(): return lax.ppermute(x, axis, pairs)  8.57 us
    pallas_call x1, Pallas kernels, attend_rest(): pl.pallas_call(attend_rest_kernel, out_shape=jax.ShapeDtypeStruct((TOK, F...  7.29 us
    unnamed x12, local copies, waits for them, and re-layouts  4.19 us
    pallas_call x1, Pallas kernels, rims_of(): pl.pallas_call(rim_kernel, out_shape=[jax.ShapeDtypeStruct((2, EDGE, FEAT...  2.91 us
  transfers between devices with their start and end apart: 8, of which 2 were waited for; matrix products, arithmetic and copies ran while one was open for 2% of the time, Pallas kernels for 14%

profile of v6, /device:TPU:1, one launch (start us, length us, event | category | flops | bytes accessed | tf_op | source)
XLA Modules:
  0.0 121.6 jit_solution(13704562620405345884)
XLA Ops:
  0.6 2.4 %pool.1 = f32[16,16,128]{2,1,0:T(8,128)} custom-call(s32[2,2,9]{2,1,0:T(2,128)} %bitcast.35, s32[2,3,2,12]{3,2,1,0:T(2,128)} %bitcast.38, bf16[256,1536]{1,0:T(8,128)(2,1)} %bitcast.25, bf16[256,1536]{1,0:T(8,128)(2,1)} %bitcast.22), custom_call_target="tpu_custom_call" | custom-call | tf_op jit(solution)/shard_map/pool/pallas_call | solution.py:76
  3.0 9.2 %all-to-all-start = ((f32[16,16,128]{2,1,0:T(8,128)}), f32[16,16,128]{2,1,0:T(8,128)S(1)}, u32[]{:S(2)}, u32[]{:S(2)}) async-start(f32[16,16,128]{2,1,0:T(8,128)} %pool.1), calls=%async_computation | async-start | bytes 262144 | tf_op jit(solution)/shard_map/all_to_all | solution.py:343
  12.2 2.9 %rims.1 = (bf16[2,128,1536]{2,1,0:T(8,128)(2,1)}, bf16[2,128,1536]{2,1,0:T(8,128)(2,1)}, bf16[2,128,1536]{2,1,0:T(8,128)(2,1)}, bf16[2,128,1536]{2,1,0:T(8,128)(2,1)}) custom-call(bf16[16,16,1536]{2,1,0:T(8,128)(2,1)} %bitcast.23, bf16[16,16,1536]{2,1,0:T(8,128)(2,1)} %bitcast.28), custom_call_target="tpu_custom_call" | custom-call | tf_op jit(solution)/shard_map/rims/pallas_call | solution.py:100
  15.1 3.3 %collective-permute-start.2 = (bf16[2,128,1536]{2,1,0:T(8,128)(2,1)}, bf16[2,128,1536]{2,1,0:T(8,128)(2,1)S(1)}, u32[]{:S(2)}, u32[]{:S(2)}) collective-permute-start(bf16[2,128,1536]{2,1,0:T(8,128)(2,1)} %get-tuple-element.13), channel_id=1, source_target_pairs={{0,1},{1,2},{2,3},{4,5},{5,6},{6,7},{8,9},{9,10},{10,11},{12,13},{... | collective-permute-start | bytes 2359304 | tf_op jit(solution)/shard_map/ppermute | solution.py:328
  18.4 1.3 %collective-permute-start.3 = (bf16[2,128,1536]{2,1,0:T(8,128)(2,1)}, bf16[2,128,1536]{2,1,0:T(8,128)(2,1)S(1)}, u32[]{:S(2)}, u32[]{:S(2)}) collective-permute-start(bf16[2,128,1536]{2,1,0:T(8,128)(2,1)} %get-tuple-element.14), channel_id=1, source_target_pairs={{1,0},{2,1},{3,2},{5,4},{6,5},{7,6},{9,8},{10,9},{11,10},{13,12},{... | collective-permute-start | bytes 2359304 | tf_op jit(solution)/shard_map/ppermute | solution.py:328
  19.7 3.1 %collective-permute-start = (bf16[2,128,1536]{2,1,0:T(8,128)(2,1)}, bf16[2,128,1536]{2,1,0:T(8,128)(2,1)S(1)}, u32[]{:S(2)}, u32[]{:S(2)}) collective-permute-start(bf16[2,128,1536]{2,1,0:T(8,128)(2,1)} %get-tuple-element.11), channel_id=1, source_target_pairs={{0,4},{4,8},{8,12},{1,5},{5,9},{9,13},{2,6},{6,10},{10,14},{3,7},{... | collective-permute-start | bytes 2359304 | tf_op jit(solution)/shard_map/ppermute | solution.py:328
  22.8 1.3 %collective-permute-start.1 = (bf16[2,128,1536]{2,1,0:T(8,128)(2,1)}, bf16[2,128,1536]{2,1,0:T(8,128)(2,1)}, u32[]{:S(2)}, u32[]{:S(2)}) collective-permute-start(bf16[2,128,1536]{2,1,0:T(8,128)(2,1)} %get-tuple-element.12), channel_id=1, source_target_pairs={{4,0},{8,4},{12,8},{5,1},{9,5},{13,9},{6,2},{10,6},{14,10},{7,3},{... | collective-permute-start | bytes 2359304 | tf_op jit(solution)/shard_map/ppermute | solution.py:328
  24.2 0.0 all-to-all-done.recv_ref
  24.2 0.0 copy-start.5
  24.2 0.6 copy-done.5
  24.8 2.7 %router.1 = f32[128,128]{1,0:T(8,128)} custom-call(s32[1]{0:T(128)} %bitcast.7.head_ref, f32[16,16,128]{2,1,0:T(8,128)} %copy-done.5, f32[12,64,128]{2,1,0:T(8,128)} %bitcast.32, f32[12,64,128]{2,1,0:T(8,128)} %bitcast.33), custom_call_target="tpu_custom_call" | custom-call | tf_op jit(solution)/shard_map/router/pallas_call | solution.py:174
  27.5 10.9 %all_to_all.25 = f32[8,16,128]{2,1,0:T(8,128)S(1)} all-to-all(f32[8,16,128]{2,1,0:T(8,128)} %bitcast.34), channel_id=1, replica_groups=mesh['x'=4,'far'=4,'core'=2,'py'=4,'px'=4] {'x','core'}, dimensions={0} | all-to-all | bytes 131072 | tf_op jit(solution)/shard_map/all_to_all | solution.py:343
  38.4 23.4 %all_to_all.26 = f32[4,16,128]{2,1,0:T(8,128)S(1)} all-to-all(f32[4,16,128]{2,1,0:T(8,128)S(1)} %broadcast_in_dim.6), channel_id=1, replica_groups=mesh['x'=4,'far'=4,'core'=2,'py'=4,'px'=4] {'far'}, dimensions={0} | all-to-all | bytes 65536 | tf_op jit(solution)/shard_map/all_to_all | solution.py:343
  61.9 16.4 %all_to_all.27 = bf16[16,16,128]{2,1,0:T(8,128)(2,1)S(1)} all-to-all(bf16[16,16,128]{2,1,0:T(8,128)(2,1)S(1)} %broadcast_in_dim.7), channel_id=1, replica_groups=mesh['x'=4,'far'=4,'core'=2,'py'=4,'px'=4] {'py','px'}, dimensions={0} | all-to-all | bytes 131072 | tf_op jit(solution)/shard_map/all_to_all | solution.py:343
  78.3 0.9 broadcast_in_dim.8
  79.2 7.0 %all-to-all-start.4 = ((bf16[8,16,16,128]{3,2,1,0:T(8,128)(2,1)}), bf16[8,16,16,128]{3,2,1,0:T(8,128)(2,1)S(1)}, u32[]{:S(2)}, u32[]{:S(2)}) async-start(bf16[8,16,16,128]{3,2,1,0:T(8,128)(2,1)} %broadcast_in_dim.8), calls=%async_computation.4 | async-start | bytes 1048576 | tf_op jit(solution)/shard_map/all_to_all | solution.py:343
  86.2 0.0 collective-permute-done.2.rest_2_.l_ref
  86.2 0.0 copy-start
  86.2 0.0 collective-permute-done.3.rest_3_.r_ref
  86.2 0.9 copy-done
  87.1 0.0 copy-start.1
  87.1 0.9 copy-done.1
  88.0 2.4 %corners.1 = (bf16[2,128,1536]{2,1,0:T(8,128)(2,1)}, bf16[2,128,1536]{2,1,0:T(8,128)(2,1)}) custom-call(bf16[2,128,1536]{2,1,0:T(8,128)(2,1)} %copy-done, bf16[2,128,1536]{2,1,0:T(8,128)(2,1)} %copy-done.1), custom_call_target="tpu_custom_call" | custom-call | tf_op jit(solution)/shard_map/corners/pallas_call | solution.py:120
  90.4 2.2 %collective-permute-start.4 = (bf16[2,128,1536]{2,1,0:T(8,128)(2,1)}, bf16[2,128,1536]{2,1,0:T(8,128)(2,1)S(1)}, u32[]{:S(2)}, u32[]{:S(2)}) collective-permute-start(bf16[2,128,1536]{2,1,0:T(8,128)(2,1)} %get-tuple-element.17), channel_id=1, source_target_pairs={{0,4},{4,8},{8,12},{1,5},{5,9},{9,13},{2,6},{6,10},{10,14},{3,7},{... | collective-permute-start | bytes 2359304 | tf_op jit(solution)/shard_map/ppermute | solution.py:328
  92.6 1.3 %collective-permute-start.5 = (bf16[2,128,1536]{2,1,0:T(8,128)(2,1)}, bf16[2,128,1536]{2,1,0:T(8,128)(2,1)S(1)}, u32[]{:S(2)}, u32[]{:S(2)}) collective-permute-start(bf16[2,128,1536]{2,1,0:T(8,128)(2,1)} %get-tuple-element.18), channel_id=1, source_target_pairs={{4,0},{8,4},{12,8},{5,1},{9,5},{13,9},{6,2},{10,6},{14,10},{7,3},{... | collective-permute-start | bytes 2359304 | tf_op jit(solution)/shard_map/ppermute | solution.py:328
  93.9 0.0 collective-permute-done.rest_0_
  94.0 0.0 copy-start.2
  94.0 0.0 collective-permute-done.1.rest_1_
  94.0 0.9 copy-done.2
  94.8 9.0 %attend_main.1 = (f32[256,1536]{1,0:T(8,128)}, f32[256,128]{1,0:T(8,128)}) custom-call(s32[4,9]{1,0:T(4,128)} %bitcast.36, s32[8,768]{1,0:T(8,128)} %constant.17.clone.ids_ref, bf16[256,1536]{1,0:T(8,128)(2,1)} %bitcast.26, bf16[256,1536]{1,0:T(8,128)(2,1)} %bitcast.24, bf16[256,1536]{1,0:T(8,128)(2,1)} %bitcast.29, bf16[2,128,1536]{2,1,0:T(8,128)(2,1)} %copy-done.2, ...), custom_call_target="tpu_custom_call" | custom-call | flops 1207959552 | bytes 7077888 | tf_op jit(solution)/shard_map/attend_main/pallas_call | solution.py:284
  103.9 0.0 all-to-all-done.4
  103.9 0.1 copy_convert_fusion
  103.9 1.0 slice_bitcast_fusion
  104.9 4.8 %collective-permute-done.4.a_ref = bf16[2,128,1536]{2,1,0:T(8,128)(2,1)S(1)} collective-permute-done((bf16[2,128,1536]{2,1,0:T(8,128)(2,1)}, bf16[2,128,1536]{2,1,0:T(8,128)(2,1)S(1)}, u32[]{:S(2)}, u32[]{:S(2)}) %collective-permute-start.4) | collective-permute-done | bytes 786464 | tf_op jit(solution)/shard_map/ppermute | solution.py:328
  109.7 0.0 copy-start.3
  109.7 3.8 %collective-permute-done.5.b_ref = bf16[2,128,1536]{2,1,0:T(8,128)(2,1)S(1)} collective-permute-done((bf16[2,128,1536]{2,1,0:T(8,128)(2,1)}, bf16[2,128,1536]{2,1,0:T(8,128)(2,1)S(1)}, u32[]{:S(2)}, u32[]{:S(2)}) %collective-permute-start.5) | collective-permute-done | bytes 786464 | tf_op jit(solution)/shard_map/ppermute | solution.py:328
  113.5 0.0 copy-start.4
  113.5 0.0 copy-done.3
  113.5 0.9 copy-done.4
  114.3 7.3 %attend_rest.1 = bf16[256,1536]{1,0:T(8,128)(2,1)} custom-call(s32[4,9]{1,0:T(4,128)} %bitcast.37, s32[8,256]{1,0:T(8,128)} %constant.18.clone.ids_ref, bf16[256,1536]{1,0:T(8,128)(2,1)} %bitcast.27, f32[256,1536]{1,0:T(8,128)} %get-tuple-element.15.acc_ref, f32[256,128]{1,0:T(8,128)} %get-tuple-element.16.stat_ref, bf16[2,128,1536]{2,1,0:T(8,128)(2,1)} %copy-done.3, ...), custom_call_target="tpu_custom_call" | custom-call | flops 402653184 | bytes 4718592 | tf_op jit(solution)/shard_map/attend_rest/pallas_call | solution.py:306
  (4 shorter events, 0.0 us)
Async XLA Ops:
  3.0 21.2 %all-to-all-start = ((f32[16,16,128]{2,1,0:T(8,128)}), f32[16,16,128]{2,1,0:T(8,128)S(1)}, u32[]{:S(2)}, u32[]{:S(2)}) async-start(f32[16,16,128]{2,1,0:T(8,128)} %pool.1), calls=%async_computation | async-start | bytes 262144 | tf_op jit(solution)/shard_map/all_to_all | solution.py:343
  15.1 71.1 %collective-permute-start.2 = (bf16[2,128,1536]{2,1,0:T(8,128)(2,1)}, bf16[2,128,1536]{2,1,0:T(8,128)(2,1)S(1)}, u32[]{:S(2)}, u32[]{:S(2)}) collective-permute-start(bf16[2,128,1536]{2,1,0:T(8,128)(2,1)} %get-tuple-element.13), channel_id=1, source_target_pairs={{0,1},{1,2},{2,3},{4,5},{5,6},{6,7},{8,9},{9,10},{10,11},{12,13},{... | collective-permute-start | bytes 2359304 | tf_op jit(solution)/shard_map/ppermute | solution.py:328
  18.4 67.8 %collective-permute-start.3 = (bf16[2,128,1536]{2,1,0:T(8,128)(2,1)}, bf16[2,128,1536]{2,1,0:T(8,128)(2,1)S(1)}, u32[]{:S(2)}, u32[]{:S(2)}) collective-permute-start(bf16[2,128,1536]{2,1,0:T(8,128)(2,1)} %get-tuple-element.14), channel_id=1, source_target_pairs={{1,0},{2,1},{3,2},{5,4},{6,5},{7,6},{9,8},{10,9},{11,10},{13,12},{... | collective-permute-start | bytes 2359304 | tf_op jit(solution)/shard_map/ppermute | solution.py:328
  19.7 74.2 %collective-permute-start = (bf16[2,128,1536]{2,1,0:T(8,128)(2,1)}, bf16[2,128,1536]{2,1,0:T(8,128)(2,1)S(1)}, u32[]{:S(2)}, u32[]{:S(2)}) collective-permute-start(bf16[2,128,1536]{2,1,0:T(8,128)(2,1)} %get-tuple-element.11), channel_id=1, source_target_pairs={{0,4},{4,8},{8,12},{1,5},{5,9},{9,13},{2,6},{6,10},{10,14},{3,7},{... | collective-permute-start | bytes 2359304 | tf_op jit(solution)/shard_map/ppermute | solution.py:328
  22.8 71.1 %collective-permute-start.1 = (bf16[2,128,1536]{2,1,0:T(8,128)(2,1)}, bf16[2,128,1536]{2,1,0:T(8,128)(2,1)}, u32[]{:S(2)}, u32[]{:S(2)}) collective-permute-start(bf16[2,128,1536]{2,1,0:T(8,128)(2,1)} %get-tuple-element.12), channel_id=1, source_target_pairs={{4,0},{8,4},{12,8},{5,1},{9,5},{13,9},{6,2},{10,6},{14,10},{7,3},{... | collective-permute-start | bytes 2359304 | tf_op jit(solution)/shard_map/ppermute | solution.py:328
  24.2 0.7 copy-start.5
  79.2 24.7 %all-to-all-start.4 = ((bf16[8,16,16,128]{3,2,1,0:T(8,128)(2,1)}), bf16[8,16,16,128]{3,2,1,0:T(8,128)(2,1)S(1)}, u32[]{:S(2)}, u32[]{:S(2)}) async-start(bf16[8,16,16,128]{3,2,1,0:T(8,128)(2,1)} %broadcast_in_dim.8), calls=%async_computation.4 | async-start | bytes 1048576 | tf_op jit(solution)/shard_map/all_to_all | solution.py:343
  86.2 0.9 copy-start
  87.1 0.9 copy-start.1
  90.4 19.3 %collective-permute-start.4 = (bf16[2,128,1536]{2,1,0:T(8,128)(2,1)}, bf16[2,128,1536]{2,1,0:T(8,128)(2,1)S(1)}, u32[]{:S(2)}, u32[]{:S(2)}) collective-permute-start(bf16[2,128,1536]{2,1,0:T(8,128)(2,1)} %get-tuple-element.17), channel_id=1, source_target_pairs={{0,4},{4,8},{8,12},{1,5},{5,9},{9,13},{2,6},{6,10},{10,14},{3,7},{... | collective-permute-start | bytes 2359304 | tf_op jit(solution)/shard_map/ppermute | solution.py:328
  92.6 20.8 %collective-permute-start.5 = (bf16[2,128,1536]{2,1,0:T(8,128)(2,1)}, bf16[2,128,1536]{2,1,0:T(8,128)(2,1)S(1)}, u32[]{:S(2)}, u32[]{:S(2)}) collective-permute-start(bf16[2,128,1536]{2,1,0:T(8,128)(2,1)} %get-tuple-element.18), channel_id=1, source_target_pairs={{4,0},{8,4},{12,8},{5,1},{9,5},{13,9},{6,2},{10,6},{14,10},{7,3},{... | collective-permute-start | bytes 2359304 | tf_op jit(solution)/shard_map/ppermute | solution.py:328
  94.0 0.9 copy-start.2
  109.7 3.8 %copy-start.3 = (bf16[2,128,1536]{2,1,0:T(8,128)(2,1)}, bf16[2,128,1536]{2,1,0:T(8,128)(2,1)S(1)}, u32[]{:S(2)}) copy-start(bf16[2,128,1536]{2,1,0:T(8,128)(2,1)S(1)} %collective-permute-done.4.a_ref) | copy-start | bytes 2359300
  113.5 0.9 copy-start.4
